TPU v7x, 512 devices: a whole 4x4x16 slice. The times are simulated.
512 devices in a mesh: src: 16 (over z_lo, x), tgt: 4 (over z_hi), feat: 8 (over y, core).
Axes of the slice: x: 4, y: 4, z: 16 (z_hi: 4, z_lo: 4; z = z_hi * 4 + z_lo), core: 2. Of those that a mesh axis runs over, the one named last changes fastest.
Arguments:
- activations: bfloat16 [16, 1792, 1280], P('src', None, 'feat'), may hold values from 0 to 12, as said below
- window_ids: int32 [16, 640], replicated, may hold values from 0 to 1279, as said below
- decoders: bfloat16 [16, 16, 640, 2048], P('src', 'tgt', 'feat'), may hold values from -3 to 3
- encoders: bfloat16 [16, 2048, 640], P('tgt', ('src', 'feat')), may hold values from -0.125 to 0.125
Outputs:
- weighted: float32 [16, 16, 640, 640], P('src', 'tgt', 'feat')
Inputs may be any that keep to these rules, and one draw needn't show every extreme that they name: `window_ids`: each layer's list names 640 distinct features. activations are zero or positive.
All inputs are finite; a program needn't handle non-finite values.
Results may differ from a plain program's by a relative error of at most 0.0029.
Values may be sent and summed in bfloat16 or wider, within the bound.
No kernel may reach another device: no remote copies, remote signals or barrier semaphores. Data moves between devices by JAX's collectives and lax.ppermute only.
A program may use at most 64 MiB of HBM per device.

v0:
```python
import jax
import jax.numpy as jnp
from jax import lax
from jax.experimental import pallas as pl
from jax.experimental.pallas import tpu as pltpu
from jax.sharding import Mesh, PartitionSpec as P

ZLO, X, TGT, Y, CORE = 4, 4, 4, 4, 2
FEAT = ("y", "core")


def total_pairs(k):
    return [(z * TGT + b, z * TGT + b + k) for z in range(ZLO) for b in range(z, TGT - k)]


def window_pairs(k):
    return [(b * TGT + b, (b - k) * TGT + b) for b in range(k, TGT)]


def split_kernel(wide_ref, out_ref):
    tokens = out_ref.shape[2]
    for f in range(out_ref.shape[0]):
        out_ref[f] = wide_ref[:, f * tokens : (f + 1) * tokens]


def select_kernel(place_ref, ids_ref, sliced_ref, columns_ref, pieces_ref):
    feats, tokens = sliced_ref.shape
    width = ids_ref.shape[1]
    step = 128
    row = ids_ref[pl.ds(place_ref[4], 1), :]
    wide = jnp.broadcast_to(row, (step, width))
    tall = wide.T
    columns = jnp.zeros((tokens, width), jnp.float32)
    rows = jnp.zeros((width, tokens), jnp.float32)
    for g in range(feats // step):
        part = sliced_ref[g * step : (g + 1) * step]
        chosen = (wide == g * step + lax.broadcasted_iota(jnp.int32, wide.shape, 0)).astype(jnp.bfloat16)
        columns += lax.dot_general(part, chosen, (((0,), (0,)), ((), ())), preferred_element_type=jnp.float32)
        chosen = (tall == g * step + lax.broadcasted_iota(jnp.int32, tall.shape, 1)).astype(jnp.bfloat16)
        rows += jnp.dot(chosen, part, preferred_element_type=jnp.float32)
    columns_ref[...] = columns.astype(columns_ref.dtype)
    rows = rows.astype(pieces_ref.dtype)
    height = width // (Y * CORE)
    for y in range(Y):
        for c in range(CORE):
            f = y * CORE + c
            for x in range(X):
                pieces_ref[x * CORE + c, y * height : (y + 1) * height] = rows[f * height : (f + 1) * height]


def virtual_kernel(place_ref, prefix_ref, own_ref, other_ref, out_ref, rows_ref):
    groups, slices, depth, width = rows_ref.shape
    core = place_ref[2]
    for r in range(Y):
        row = (place_ref[1] + Y - r) % Y
        rows_ref[:, row * CORE + core] = own_ref[r].reshape(groups, depth, width)
        rows_ref[:, row * CORE + 1 - core] = other_ref[r].reshape(groups, depth, width)
    height = prefix_ref.shape[0] * prefix_ref.shape[1]
    chunk = slices * depth
    total = jnp.zeros((height, width), jnp.float32)
    for g in range(groups):
        left = prefix_ref[:, :, g * chunk : (g + 1) * chunk].reshape(height, chunk)
        total += jnp.dot(left, rows_ref[g].reshape(chunk, width), preferred_element_type=jnp.float32)
    out_ref[...] = total.reshape(out_ref.shape)


def gram_kernel(place_ref, window_ref, own_ref, other_ref, out_ref):
    core = place_ref[2]
    for q in range(window_ref.shape[0]):
        part = jnp.dot(window_ref[q, core], own_ref[...], preferred_element_type=jnp.float32)
        part += jnp.dot(window_ref[q, 1 - core], other_ref[...], preferred_element_type=jnp.float32)
        out_ref[q] = part.astype(out_ref.dtype)


def weigh_kernel(place_ref, gram_ref, *refs):
    virtual_refs, out_ref = refs[:-1], refs[-1]
    token_count = place_ref[3].astype(jnp.float32)
    for r in range(X):
        layer = (place_ref[0] + r) % X
        gram = gram_ref[layer, 0].astype(jnp.float32)
        for row in range(1, Y):
            gram += gram_ref[layer, row].astype(jnp.float32)
        out_ref[layer] = virtual_refs[r][...] * (gram / token_count)


SMEM = pl.BlockSpec(memory_space=pltpu.SMEM)
VMEM = pl.BlockSpec(memory_space=pltpu.VMEM)


def split(wide, slices):
    feats, token_count = wide.shape
    return pl.pallas_call(
        split_kernel,
        out_shape=jax.ShapeDtypeStruct((slices, feats, token_count // slices), wide.dtype),
        in_specs=[VMEM],
        out_specs=VMEM,
    )(wide)


def select(place, window_ids, sliced):
    tokens, width = sliced.shape[1], window_ids.shape[1]
    return pl.pallas_call(
        select_kernel,
        out_shape=(
            jax.ShapeDtypeStruct((tokens, width), jnp.bfloat16),
            jax.ShapeDtypeStruct((X * CORE, width // CORE, tokens), jnp.bfloat16),
        ),
        in_specs=[SMEM, VMEM, VMEM],
        out_specs=(VMEM, VMEM),
    )(place, window_ids, sliced)


def virtual_of(place, prefix, own, other):
    sources, height, depth = prefix.shape
    width = own.shape[2]
    groups = ZLO * X
    return pl.pallas_call(
        virtual_kernel,
        out_shape=jax.ShapeDtypeStruct((sources, height, width), jnp.float32),
        in_specs=[SMEM, VMEM, VMEM, VMEM],
        out_specs=VMEM,
        scratch_shapes=[pltpu.VMEM((groups, Y * CORE, depth // (groups * Y * CORE), width), jnp.bfloat16)],
    )(place, prefix, own, other)


def gram_of(place, window, own, other):
    return pl.pallas_call(
        gram_kernel,
        out_shape=jax.ShapeDtypeStruct((X, window.shape[2], own.shape[1]), jnp.bfloat16),
        in_specs=[SMEM, VMEM, VMEM, VMEM],
        out_specs=VMEM,
    )(place, window, own, other)


def weigh(place, gram, virtual):
    return pl.pallas_call(
        weigh_kernel,
        out_shape=jax.ShapeDtypeStruct((X,) + virtual[0].shape, jnp.float32),
        in_specs=[SMEM, VMEM] + [VMEM] * len(virtual),
        out_specs=VMEM,
    )(place, gram, *virtual)


def ring(n, k):
    return [(i, (i + k) % n) for i in range(n)]


def over_feat(piece):
    others = [lax.ppermute(piece, "y", ring(Y, k)) for k in range(1, Y)]
    own = jnp.stack([piece] + others)
    return own, lax.ppermute(own, "core", ring(CORE, 1))


def per_device(activations, window_ids, decoders, encoders):
    zlo = lax.axis_index("zlo")
    block = lax.axis_index("tgt")
    x = lax.axis_index("x")
    source = zlo * X + x
    token_count, local_feats = activations.shape[1:]
    targets, height = decoders.shape[1:3]
    fw = window_ids.shape[1]
    slices = Y * CORE
    tokens = token_count // slices

    depth = block * targets + jnp.arange(targets)
    live = (depth >= source).astype(jnp.float32)
    written = decoders[0].astype(jnp.float32) * live[:, None, None]
    before = [jnp.zeros_like(written[0])]
    for k in range(targets):
        before.append(before[-1] + written[k])
    total = before.pop()
    earlier = [lax.ppermute(total, ("zlo", "tgt"), total_pairs(k)) for k in (3, 2, 1)]

    place = jnp.stack([x, lax.axis_index("y"), lax.axis_index("core"), token_count, source]).astype(jnp.int32)
    by_tokens = split(activations[0].T, slices)
    sliced = lax.all_to_all(by_tokens, FEAT, 0, 0, tiled=True).reshape(slices * local_feats, tokens)
    columns, pieces = select(place, window_ids, sliced)

    parts = [lax.ppermute(columns, ("zlo", "tgt"), window_pairs(k)) for k in (3, 2, 1)]
    target = jnp.where(zlo == block, columns, parts[0] + parts[1] + parts[2])
    swapped = lax.ppermute(target, "core", ring(CORE, 1))

    spread = jnp.broadcast_to(encoders[None], (ZLO,) + encoders.shape).reshape((ZLO * X,) + encoders.shape[1:])
    encoder_rows = lax.all_to_all(spread, ("zlo", "x"), 0, 0, tiled=True).reshape(-1, fw)
    encoder_own, encoder_other = over_feat(encoder_rows)

    window = lax.all_to_all(pieces, ("x", "core"), 0, 0, tiled=True).reshape(X, CORE, Y * height, tokens)
    partial = gram_of(place, window, target, swapped).reshape(X * Y, height, fw)
    partial = lax.all_to_all(partial, ("x", "y"), 0, 0, tiled=True).reshape(X, Y, height, fw)

    base = earlier[0] + earlier[1] + earlier[2]
    prefix = jnp.stack([(base + part).astype(jnp.bfloat16) for part in before])
    pieces = [lax.dynamic_index_in_dim(prefix, (x + k) % X, 0, keepdims=False) for k in range(X)]
    moved = [lax.ppermute(pieces[k], "x", ring(X, k)) for k in range(1, X)]
    prefix = jnp.stack([pieces[0]] + moved)

    virtual = virtual_of(place, prefix, encoder_own, encoder_other)
    virtual = [virtual[0]] + [lax.ppermute(virtual[k], "x", ring(X, X - k)) for k in range(1, X)]
    return weigh(place, partial, virtual)[None]


def solution(mesh):
    fine = Mesh(mesh.devices.reshape(ZLO, X, TGT, Y, CORE), ("zlo", "x", "tgt", "y", "core"))
    src = ("zlo", "x")
    in_specs = (
        P(src, None, FEAT),
        P(),
        P(src, "tgt", FEAT, None),
        P("tgt", src + FEAT, None),
    )
    out_specs = P(src, "tgt", FEAT, None)

    return jax.shard_map(per_device, mesh=fine, in_specs=in_specs, out_specs=out_specs, check_vma=False)
```

profile of v0, /device:TPU:296, one launch (start us, length us, event | category | flops | bytes accessed | tf_op | source)
XLA Modules:
  0.0 175.8 jit_solution(6286574587714670924)
XLA Ops:
  2.2 4.9 %all-to-all-start = ((bf16[8,160,224]{2,1,0:T(8,128)(2,1)}), bf16[8,160,224]{2,1,0:T(8,128)(2,1)S(1)}, u32[]{:S(2)}, u32[]{:S(2)}) async-start(bf16[8,160,224]{2,1,0:T(8,128)(2,1)} %shard_map.46), calls=%async_computation | async-start | bytes 1310720 | tf_op jit(solution)/shard_map/all_to_all | solution.py:176
  7.1 10.3 %all-to-all-done = bf16[8,160,224]{2,1,0:T(8,128)(2,1)S(1)} async-done(((bf16[8,160,224]{2,1,0:T(8,128)(2,1)}), bf16[8,160,224]{2,1,0:T(8,128)(2,1)S(1)}, u32[]{:S(2)}, u32[]{:S(2)}) %all-to-all-start) | async-done | bytes 573472 | tf_op jit(solution)/shard_map/all_to_all | solution.py:176
  18.2 6.7 %all-to-all-start.3 = ((bf16[16,16,640]{2,1,0:T(8,128)(2,1)}), bf16[16,16,640]{2,1,0:T(8,128)(2,1)}, u32[]{:S(2)}, u32[]{:S(2)}) async-start(bf16[16,16,640]{2,1,0:T(8,128)(2,1)} %bitcast.25), calls=%async_computation.3 | async-start | bytes 655360 | tf_op jit(solution)/shard_map/all_to_all | solution.py:184
  27.2 4.1 %shard_map.47 = (bf16[224,640]{1,0:T(8,128)(2,1)}, bf16[8,320,224]{2,1,0:T(8,128)(2,1)}) custom-call(s32[5]{0:T(128)} %stack.59.place_ref, s32[16,640]{1,0:T(8,128)} %ids_ref.1, bf16[1280,224]{1,0:T(8,128)(2,1)} %bitcast.83), custom_call_target="tpu_custom_call" | custom-call | tf_op jit(solution)/shard_map/pallas_call | solution.py:102
  35.8 4.1 %collective-permute-start.6 = (f32[80,2048]{1,0:T(8,128)}, f32[80,2048]{1,0:T(8,128)}, u32[]{:S(2)}, u32[]{:S(2)}) collective-permute-start(f32[80,2048]{1,0:T(8,128)} %fusion), channel_id=1, source_target_pairs={{0,8},{8,16},{16,24},{136,144},{144,152},{272,280},{1,9},{9,17},{1... | collective-permute-start | bytes 1966088 | tf_op jit(solution)/shard_map/ppermute | solution.py:172
  42.6 4.3 %all-to-all-start.1 = ((bf16[8,320,224]{2,1,0:T(8,128)(2,1)}), bf16[8,320,224]{2,1,0:T(8,128)(2,1)}, u32[]{:S(2)}, u32[]{:S(2)}) async-start(bf16[8,320,224]{2,1,0:T(8,128)(2,1)} %get-tuple-element.7), calls=%async_computation.1 | async-start | bytes 2621440 | tf_op jit(solution)/shard_map/all_to_all | solution.py:187
  47.0 9.1 %collective-permute-done.2 = bf16[224,640]{1,0:T(8,128)(2,1)} collective-permute-done((bf16[224,640]{1,0:T(8,128)(2,1)}, bf16[224,640]{1,0:T(8,128)(2,1)}, u32[]{:S(2)}, u32[]{:S(2)}) %collective-permute-start.2) | collective-permute-done | bytes 286752 | tf_op jit(solution)/shard_map/ppermute | solution.py:179
  61.3 5.3 %collective-permute-start.11 = (bf16[256,640]{1,0:T(8,128)(2,1)}, bf16[256,640]{1,0:T(8,128)(2,1)}, u32[]{:S(2)}, u32[]{:S(2)}) collective-permute-start(bf16[256,640]{1,0:T(8,128)(2,1)} %bitcast.27), channel_id=1, source_target_pairs={{0,4},{2,6},{4,0},{6,2},{1,5},{3,7},{5,1},{7,3},{8,12},{10,14},{12... | collective-permute-start | bytes 983048 | tf_op jit(solution)/shard_map/ppermute | solution.py:149
  66.6 2.5 %collective-permute-start.12 = (bf16[256,640]{1,0:T(8,128)(2,1)}, bf16[256,640]{1,0:T(8,128)(2,1)}, u32[]{:S(2)}, u32[]{:S(2)}) collective-permute-start(bf16[256,640]{1,0:T(8,128)(2,1)} %bitcast.27), channel_id=1, source_target_pairs={{0,6},{2,0},{4,2},{6,4},{1,7},{3,1},{5,3},{7,5},{8,14},{10,8},{12,... | collective-permute-start | bytes 983048 | tf_op jit(solution)/shard_map/ppermute | solution.py:149
  69.1 31.3 %collective-permute-done.6 = f32[80,2048]{1,0:T(8,128)} collective-permute-done((f32[80,2048]{1,0:T(8,128)}, f32[80,2048]{1,0:T(8,128)}, u32[]{:S(2)}, u32[]{:S(2)}) %collective-permute-start.6) | collective-permute-done | bytes 655392 | tf_op jit(solution)/shard_map/ppermute | solution.py:172
  100.4 2.3 %convert_bitcast_fusion = (bf16[1,80,2048]{2,1,0:T(8,128)(2,1)}, f32[80,2048]{1,0:T(8,128)S(1)}) fusion(f32[80,2048]{1,0:T(8,128)} %collective-permute-done.6, f32[80,2048]{1,0:T(8,128)} %copy-done.4, f32[80,2048]{1,0:T(8,128)} %collective-permute-done.5), kind=kLoop, calls=%fused_computation.21 | loop fusion | flops 491520 | bytes 2949120 | tf_op jit(solution)/shard_map/stack | solution.py:192
  102.7 3.8 %shard_map.48 = bf16[4,320,640]{2,1,0:T(8,128)(2,1)} custom-call(s32[5]{0:T(128)} %stack.59.place_ref, bf16[4,2,320,224]{3,2,1,0:T(8,128)(2,1)} %bitcast.7.window_ref, bf16[224,640]{1,0:T(8,128)(2,1)} %copy-done.3, bf16[224,640]{1,0:T(8,128)(2,1)} %collective-permute-done.3.other_ref), custom_call_target="tpu_custom_call" | custom-call | tf_op jit(solution)/shard_map/pallas_call | solution.py:127
  106.6 6.4 %all-to-all-start.2 = ((bf16[16,80,640]{2,1,0:T(8,128)(2,1)}), bf16[16,80,640]{2,1,0:T(8,128)(2,1)}, u32[]{:S(2)}, u32[]{:S(2)}) async-start(bf16[16,80,640]{2,1,0:T(8,128)(2,1)} %bitcast.82), calls=%async_computation.2 | async-start | bytes 3276800 | tf_op jit(solution)/shard_map/all_to_all | solution.py:189
  117.7 3.4 %collective-permute-start.7 = (bf16[80,2048]{1,0:T(8,128)(2,1)S(1)}, bf16[80,2048]{1,0:T(8,128)(2,1)S(1)}, u32[]{:S(2)}, u32[]{:S(2)}) collective-permute-start(bf16[80,2048]{1,0:T(8,128)(2,1)S(1)} %get-tuple-element.17), channel_id=1, source_target_pairs={{0,32},{32,64},{64,96},{96,0},{1,33},{33,65},{65,97},{97,1},{2,34}... | collective-permute-start | bytes 983048 | tf_op jit(solution)/shard_map/ppermute | solution.py:194
  121.1 4.6 %collective-permute-start.8 = (bf16[80,2048]{1,0:T(8,128)(2,1)S(1)}, bf16[80,2048]{1,0:T(8,128)(2,1)S(1)}, u32[]{:S(2)}, u32[]{:S(2)}) collective-permute-start(bf16[80,2048]{1,0:T(8,128)(2,1)S(1)} %get-tuple-element.16), channel_id=1, source_target_pairs={{0,64},{32,96},{64,0},{96,32},{1,65},{33,97},{65,1},{97,33},{2,66}... | collective-permute-start | bytes 983048 | tf_op jit(solution)/shard_map/ppermute | solution.py:194
  125.7 3.4 %collective-permute-start.9 = (bf16[80,2048]{1,0:T(8,128)(2,1)S(1)}, bf16[80,2048]{1,0:T(8,128)(2,1)S(1)}, u32[]{:S(2)}, u32[]{:S(2)}) collective-permute-start(bf16[80,2048]{1,0:T(8,128)(2,1)S(1)} %get-tuple-element.15), channel_id=1, source_target_pairs={{0,96},{32,0},{64,32},{96,64},{1,97},{33,1},{65,33},{97,65},{2,98}... | collective-permute-start | bytes 983048 | tf_op jit(solution)/shard_map/ppermute | solution.py:194
  129.1 12.5 %collective-permute-done.7 = bf16[80,2048]{1,0:T(8,128)(2,1)S(1)} collective-permute-done((bf16[80,2048]{1,0:T(8,128)(2,1)S(1)}, bf16[80,2048]{1,0:T(8,128)(2,1)S(1)}, u32[]{:S(2)}, u32[]{:S(2)}) %collective-permute-start.7) | collective-permute-done | bytes 327712 | tf_op jit(solution)/shard_map/ppermute | solution.py:194
  141.6 6.6 %collective-permute-done.8 = bf16[80,2048]{1,0:T(8,128)(2,1)S(1)} collective-permute-done((bf16[80,2048]{1,0:T(8,128)(2,1)S(1)}, bf16[80,2048]{1,0:T(8,128)(2,1)S(1)}, u32[]{:S(2)}, u32[]{:S(2)}) %collective-permute-start.8) | collective-permute-done | bytes 327712 | tf_op jit(solution)/shard_map/ppermute | solution.py:194
  149.4 5.1 %shard_map.49 = f32[4,80,640]{2,1,0:T(8,128)} custom-call(s32[5]{0:T(128)} %stack.59.place_ref, bf16[4,80,2048]{2,1,0:T(8,128)(2,1)} %pad_maximum_fusion.1.prefix_ref, bf16[4,256,640]{2,1,0:T(8,128)(2,1)} %copy-done, bf16[4,256,640]{2,1,0:T(8,128)(2,1)} %collective-permute-done.13.other_ref), custom_call_target="tpu_custom_call" | custom-call | tf_op jit(solution)/shard_map/pallas_call | solution.py:117
  158.7 3.5 %collective-permute-start.15 = (f32[80,640]{1,0:T(8,128)S(1)}, f32[80,640]{1,0:T(8,128)S(1)}, u32[]{:S(2)}, u32[]{:S(2)}) collective-permute-start(f32[80,640]{1,0:T(8,128)S(1)} %get-tuple-element.19), channel_id=1, source_target_pairs={{0,64},{32,96},{64,0},{96,32},{1,65},{33,97},{65,1},{97,33},{2,66}... | collective-permute-start | bytes 614408 | tf_op jit(solution)/shard_map/ppermute | solution.py:198
  162.2 2.6 %collective-permute-start.16 = (f32[80,640]{1,0:T(8,128)S(1)}, f32[80,640]{1,0:T(8,128)S(1)}, u32[]{:S(2)}, u32[]{:S(2)}) collective-permute-start(f32[80,640]{1,0:T(8,128)S(1)} %get-tuple-element.18), channel_id=1, source_target_pairs={{0,32},{32,64},{64,96},{96,0},{1,33},{33,65},{65,97},{97,1},{2,34}... | collective-permute-start | bytes 614408 | tf_op jit(solution)/shard_map/ppermute | solution.py:198
  166.3 2.3 %collective-permute-done.15.refs_2_ = f32[80,640]{1,0:T(8,128)S(1)} collective-permute-done((f32[80,640]{1,0:T(8,128)S(1)}, f32[80,640]{1,0:T(8,128)S(1)}, u32[]{:S(2)}, u32[]{:S(2)}) %collective-permute-start.15) | collective-permute-done | bytes 204832 | tf_op jit(solution)/shard_map/ppermute | solution.py:198
  168.6 3.7 %collective-permute-done.16.refs_3_ = f32[80,640]{1,0:T(8,128)S(1)} collective-permute-done((f32[80,640]{1,0:T(8,128)S(1)}, f32[80,640]{1,0:T(8,128)S(1)}, u32[]{:S(2)}, u32[]{:S(2)}) %collective-permute-start.16) | collective-permute-done | bytes 204832 | tf_op jit(solution)/shard_map/ppermute | solution.py:198
  173.0 2.8 %shard_map.50 = f32[4,80,640]{2,1,0:T(8,128)} custom-call(s32[5]{0:T(128)} %stack.59.place_ref, bf16[4,4,80,640]{3,2,1,0:T(8,128)(2,1)} %bitcast.9.gram_ref, f32[80,640]{1,0:T(8,128)} %get-tuple-element.21.refs_0_, f32[80,640]{1,0:T(8,128)} %copy-done.5, f32[80,640]{1,0:T(8,128)} %copy-done.6, f32[80,640]{1,0:T(8,128)} %copy-done.7), custom_call_target="tpu_custom_call" | custom-call | tf_op jit(solution)/shard_map/pallas_call | solution.py:136
  (54 shorter events, 30.1 us)
Async XLA Ops:
  0.0 17.4 %copy-start.8 = (bf16[4,16,640]{2,1,0:T(8,128)(2,1)S(1)}, bf16[4,16,640]{2,1,0:T(8,128)(2,1)}, u32[]{:S(2)}) copy-start(bf16[4,16,640]{2,1,0:T(8,128)(2,1)} %param.7) | copy-start | bytes 245764
  2.2 15.2 %all-to-all-start = ((bf16[8,160,224]{2,1,0:T(8,128)(2,1)}), bf16[8,160,224]{2,1,0:T(8,128)(2,1)S(1)}, u32[]{:S(2)}, u32[]{:S(2)}) async-start(bf16[8,160,224]{2,1,0:T(8,128)(2,1)} %shard_map.46), calls=%async_computation | async-start | bytes 1310720 | tf_op jit(solution)/shard_map/all_to_all | solution.py:176
  17.4 9.8 %copy-start.1 = (bf16[8,160,224]{2,1,0:T(8,128)(2,1)}, bf16[8,160,224]{2,1,0:T(8,128)(2,1)S(1)}, u32[]{:S(2)}) copy-start(bf16[8,160,224]{2,1,0:T(8,128)(2,1)S(1)} %all-to-all-done) | copy-start | bytes 1720324
  18.2 24.4 %all-to-all-start.3 = ((bf16[16,16,640]{2,1,0:T(8,128)(2,1)}), bf16[16,16,640]{2,1,0:T(8,128)(2,1)}, u32[]{:S(2)}, u32[]{:S(2)}) async-start(bf16[16,16,640]{2,1,0:T(8,128)(2,1)} %bitcast.25), calls=%async_computation.3 | async-start | bytes 655360 | tf_op jit(solution)/shard_map/all_to_all | solution.py:184
  31.3 10.0 %collective-permute-start = (bf16[224,640]{1,0:T(8,128)(2,1)}, bf16[224,640]{1,0:T(8,128)(2,1)}, u32[]{:S(2)}, u32[]{:S(2)}) collective-permute-start(bf16[224,640]{1,0:T(8,128)(2,1)} %get-tuple-element.8), channel_id=1, source_target_pairs={{408,24},{409,25},{410,26},{411,27},{412,28},{413,29},{414,30},{41... | collective-permute-start | bytes 860168 | tf_op jit(solution)/shard_map/ppermute | solution.py:179
  33.6 27.7 %collective-permute-start.4 = (f32[80,2048]{1,0:T(8,128)}, f32[80,2048]{1,0:T(8,128)S(1)}, u32[]{:S(2)}, u32[]{:S(2)}) collective-permute-start(f32[80,2048]{1,0:T(8,128)} %fusion), channel_id=1, source_target_pairs={{0,24},{1,25},{2,26},{3,27},{4,28},{5,29},{6,30},{7,31},{32,56},{3... | collective-permute-start | bytes 1966088 | tf_op jit(solution)/shard_map/ppermute | solution.py:172
  34.3 32.3 %collective-permute-start.5 = (f32[80,2048]{1,0:T(8,128)}, f32[80,2048]{1,0:T(8,128)}, u32[]{:S(2)}, u32[]{:S(2)}) collective-permute-start(f32[80,2048]{1,0:T(8,128)} %fusion), channel_id=1, source_target_pairs={{0,16},{8,24},{136,152},{1,17},{9,25},{137,153},{2,18},{10,26},{13... | collective-permute-start | bytes 1966088 | tf_op jit(solution)/shard_map/ppermute | solution.py:172
  35.8 64.6 %collective-permute-start.6 = (f32[80,2048]{1,0:T(8,128)}, f32[80,2048]{1,0:T(8,128)}, u32[]{:S(2)}, u32[]{:S(2)}) collective-permute-start(f32[80,2048]{1,0:T(8,128)} %fusion), channel_id=1, source_target_pairs={{0,8},{8,16},{16,24},{136,144},{144,152},{272,280},{1,9},{9,17},{1... | collective-permute-start | bytes 1966088 | tf_op jit(solution)/shard_map/ppermute | solution.py:172
  39.9 7.0 %collective-permute-start.1 = (bf16[224,640]{1,0:T(8,128)(2,1)}, bf16[224,640]{1,0:T(8,128)(2,1)}, u32[]{:S(2)}, u32[]{:S(2)}) collective-permute-start(bf16[224,640]{1,0:T(8,128)(2,1)} %get-tuple-element.8), channel_id=1, source_target_pairs={{272,16},{408,152},{273,17},{409,153},{274,18},{410,154},{275,19},... | collective-permute-start | bytes 860168 | tf_op jit(solution)/shard_map/ppermute | solution.py:179
  41.3 14.8 %collective-permute-start.2 = (bf16[224,640]{1,0:T(8,128)(2,1)}, bf16[224,640]{1,0:T(8,128)(2,1)}, u32[]{:S(2)}, u32[]{:S(2)}) collective-permute-start(bf16[224,640]{1,0:T(8,128)(2,1)} %get-tuple-element.8), channel_id=1, source_target_pairs={{136,8},{272,144},{408,280},{137,9},{273,145},{409,281},{138,10},{... | collective-permute-start | bytes 860168 | tf_op jit(solution)/shard_map/ppermute | solution.py:179
  42.6 60.1 %all-to-all-start.1 = ((bf16[8,320,224]{2,1,0:T(8,128)(2,1)}), bf16[8,320,224]{2,1,0:T(8,128)(2,1)}, u32[]{:S(2)}, u32[]{:S(2)}) async-start(bf16[8,320,224]{2,1,0:T(8,128)(2,1)} %get-tuple-element.7), calls=%async_computation.1 | async-start | bytes 2621440 | tf_op jit(solution)/shard_map/all_to_all | solution.py:187
  57.3 45.5 %copy-start.3 = (bf16[224,640]{1,0:T(8,128)(2,1)}, bf16[224,640]{1,0:T(8,128)(2,1)S(1)}, u32[]{:S(2)}) copy-start(bf16[224,640]{1,0:T(8,128)(2,1)S(1)} %add_select_fusion.own_ref) | copy-start | bytes 860164
  57.3 45.5 %collective-permute-start.3 = (bf16[224,640]{1,0:T(8,128)(2,1)S(1)}, bf16[224,640]{1,0:T(8,128)(2,1)}, u32[]{:S(2)}, u32[]{:S(2)}) collective-permute-start(bf16[224,640]{1,0:T(8,128)(2,1)S(1)} %add_select_fusion.own_ref), channel_id=1, source_target_pairs={{0,1},{1,0},{2,3},{3,2},{4,5},{5,4},{6,7},{7,6},{8,9},{9,8},{10,11... | collective-permute-start | bytes 860168 | tf_op jit(solution)/shard_map/ppermute | solution.py:181
  59.2 53.8 %collective-permute-start.10 = (bf16[256,640]{1,0:T(8,128)(2,1)}, bf16[256,640]{1,0:T(8,128)(2,1)}, u32[]{:S(2)}, u32[]{:S(2)}) collective-permute-start(bf16[256,640]{1,0:T(8,128)(2,1)} %bitcast.27), channel_id=1, source_target_pairs={{0,2},{2,4},{4,6},{6,0},{1,3},{3,5},{5,7},{7,1},{8,10},{10,12},{12... | collective-permute-start | bytes 983048 | tf_op jit(solution)/shard_map/ppermute | solution.py:149
  61.3 51.7 %collective-permute-start.11 = (bf16[256,640]{1,0:T(8,128)(2,1)}, bf16[256,640]{1,0:T(8,128)(2,1)}, u32[]{:S(2)}, u32[]{:S(2)}) collective-permute-start(bf16[256,640]{1,0:T(8,128)(2,1)} %bitcast.27), channel_id=1, source_target_pairs={{0,4},{2,6},{4,0},{6,2},{1,5},{3,7},{5,1},{7,3},{8,12},{10,14},{12... | collective-permute-start | bytes 983048 | tf_op jit(solution)/shard_map/ppermute | solution.py:149
  66.6 46.4 %collective-permute-start.12 = (bf16[256,640]{1,0:T(8,128)(2,1)}, bf16[256,640]{1,0:T(8,128)(2,1)}, u32[]{:S(2)}, u32[]{:S(2)}) collective-permute-start(bf16[256,640]{1,0:T(8,128)(2,1)} %bitcast.27), channel_id=1, source_target_pairs={{0,6},{2,0},{4,2},{6,4},{1,7},{3,1},{5,3},{7,5},{8,14},{10,8},{12,... | collective-permute-start | bytes 983048 | tf_op jit(solution)/shard_map/ppermute | solution.py:149
  106.6 58.2 %all-to-all-start.2 = ((bf16[16,80,640]{2,1,0:T(8,128)(2,1)}), bf16[16,80,640]{2,1,0:T(8,128)(2,1)}, u32[]{:S(2)}, u32[]{:S(2)}) async-start(bf16[16,80,640]{2,1,0:T(8,128)(2,1)} %bitcast.82), calls=%async_computation.2 | async-start | bytes 3276800 | tf_op jit(solution)/shard_map/all_to_all | solution.py:189
  114.5 34.9 %collective-permute-start.13 = (bf16[4,256,640]{2,1,0:T(8,128)(2,1)S(1)}, bf16[4,256,640]{2,1,0:T(8,128)(2,1)}, u32[]{:S(2)}, u32[]{:S(2)}) collective-permute-start(bf16[4,256,640]{2,1,0:T(8,128)(2,1)S(1)} %pad_maximum_fusion.2.own_ref), channel_id=1, source_target_pairs={{0,1},{1,0},{2,3},{3,2},{4,5},{5,4},{6,7},{7,6},{8,9},{9,8},{10,11... | collective-permute-start | bytes 3932168 | tf_op jit(solution)/shard_map/ppermute | solution.py:151
  117.7 23.8 %collective-permute-start.7 = (bf16[80,2048]{1,0:T(8,128)(2,1)S(1)}, bf16[80,2048]{1,0:T(8,128)(2,1)S(1)}, u32[]{:S(2)}, u32[]{:S(2)}) collective-permute-start(bf16[80,2048]{1,0:T(8,128)(2,1)S(1)} %get-tuple-element.17), channel_id=1, source_target_pairs={{0,32},{32,64},{64,96},{96,0},{1,33},{33,65},{65,97},{97,1},{2,34}... | collective-permute-start | bytes 983048 | tf_op jit(solution)/shard_map/ppermute | solution.py:194
  121.1 27.1 %collective-permute-start.8 = (bf16[80,2048]{1,0:T(8,128)(2,1)S(1)}, bf16[80,2048]{1,0:T(8,128)(2,1)S(1)}, u32[]{:S(2)}, u32[]{:S(2)}) collective-permute-start(bf16[80,2048]{1,0:T(8,128)(2,1)S(1)} %get-tuple-element.16), channel_id=1, source_target_pairs={{0,64},{32,96},{64,0},{96,32},{1,65},{33,97},{65,1},{97,33},{2,66}... | collective-permute-start | bytes 983048 | tf_op jit(solution)/shard_map/ppermute | solution.py:194
  125.7 22.5 %collective-permute-start.9 = (bf16[80,2048]{1,0:T(8,128)(2,1)S(1)}, bf16[80,2048]{1,0:T(8,128)(2,1)S(1)}, u32[]{:S(2)}, u32[]{:S(2)}) collective-permute-start(bf16[80,2048]{1,0:T(8,128)(2,1)S(1)} %get-tuple-element.15), channel_id=1, source_target_pairs={{0,96},{32,0},{64,32},{96,64},{1,97},{33,1},{65,33},{97,65},{2,98}... | collective-permute-start | bytes 983048 | tf_op jit(solution)/shard_map/ppermute | solution.py:194
  156.5 9.8 %collective-permute-start.14 = (f32[80,640]{1,0:T(8,128)S(1)}, f32[80,640]{1,0:T(8,128)S(1)}, u32[]{:S(2)}, u32[]{:S(2)}) collective-permute-start(f32[80,640]{1,0:T(8,128)S(1)} %get-tuple-element.20), channel_id=1, source_target_pairs={{0,96},{32,0},{64,32},{96,64},{1,97},{33,1},{65,33},{97,65},{2,98}... | collective-permute-start | bytes 614408 | tf_op jit(solution)/shard_map/ppermute | solution.py:198
  158.7 9.9 %collective-permute-start.15 = (f32[80,640]{1,0:T(8,128)S(1)}, f32[80,640]{1,0:T(8,128)S(1)}, u32[]{:S(2)}, u32[]{:S(2)}) collective-permute-start(f32[80,640]{1,0:T(8,128)S(1)} %get-tuple-element.19), channel_id=1, source_target_pairs={{0,64},{32,96},{64,0},{96,32},{1,65},{33,97},{65,1},{97,33},{2,66}... | collective-permute-start | bytes 614408 | tf_op jit(solution)/shard_map/ppermute | solution.py:198
  162.2 10.1 %collective-permute-start.16 = (f32[80,640]{1,0:T(8,128)S(1)}, f32[80,640]{1,0:T(8,128)S(1)}, u32[]{:S(2)}, u32[]{:S(2)}) collective-permute-start(f32[80,640]{1,0:T(8,128)S(1)} %get-tuple-element.18), channel_id=1, source_target_pairs={{0,32},{32,64},{64,96},{96,0},{1,33},{33,65},{65,97},{97,1},{2,34}... | collective-permute-start | bytes 614408 | tf_op jit(solution)/shard_map/ppermute | solution.py:198
  (6 other events, 21.3 us)
where the time goes:
time: 177 us; the launch traced here: 176 us
  waiting for transfers between devices  77.3 us (44%)
  starting transfers between devices  65.9 us (37%)
  Pallas kernels  18 us (10%)
  other arithmetic  9.27 us (5%)
  local copies, waits for them, and re-layouts  4.96 us (3%)
    ppermute x3, waiting for transfers between devices, per_device(): lax.ppermute(total, ('zlo', 'tgt'), total_pairs(k))  31.3 us
    ppermute x3, waiting for transfers between devices, per_device(): moved = [lax.ppermute(pieces[k], 'x', ring(X, k)) for k in range(1, X)]  19.1 us
    ppermute x3, starting transfers between devices, per_device(): moved = [lax.ppermute(pieces[k], 'x', ring(X, k)) for k in range(1, X)]  11.3 us
    all_to_all x1, waiting for transfers between devices, per_device(): lax.all_to_all(by_tokens, FEAT, 0, 0, tiled=True)  10.3 us
    ppermute x3, starting transfers between devices, over_feat(): others = [lax.ppermute(piece, 'y', ring(Y, k)) for k in range(1, Y)]  9.82 us
    ppermute x3, waiting for transfers between devices, per_device(): lax.ppermute(columns, ('zlo', 'tgt'), window_pairs(k))  9.12 us
    ppermute x3, starting transfers between devices, per_device(): lax.ppermute(virtual[k], 'x', ring(X, X - k))  8.29 us
    ppermute x3, waiting for transfers between devices, per_device(): lax.ppermute(virtual[k], 'x', ring(X, X - k))  7.49 us
  transfers between devices with their start and end apart: 21, of which 8 were waited for; matrix products, arithmetic and copies ran while one was open for 7% of the time, Pallas kernels for 7%

commit v1 on v0

--- a/solution.py
+++ b/solution.py
@@ -27,19 +27,14 @@
     feats, tokens = sliced_ref.shape
     width = ids_ref.shape[1]
     step = 128
-    row = ids_ref[pl.ds(place_ref[4], 1), :]
-    wide = jnp.broadcast_to(row, (step, width))
-    tall = wide.T
+    wide = jnp.broadcast_to(ids_ref[pl.ds(place_ref[4], 1), :], (step, width))
     columns = jnp.zeros((tokens, width), jnp.float32)
-    rows = jnp.zeros((width, tokens), jnp.float32)
     for g in range(feats // step):
         part = sliced_ref[g * step : (g + 1) * step]
         chosen = (wide == g * step + lax.broadcasted_iota(jnp.int32, wide.shape, 0)).astype(jnp.bfloat16)
         columns += lax.dot_general(part, chosen, (((0,), (0,)), ((), ())), preferred_element_type=jnp.float32)
-        chosen = (tall == g * step + lax.broadcasted_iota(jnp.int32, tall.shape, 1)).astype(jnp.bfloat16)
-        rows += jnp.dot(chosen, part, preferred_element_type=jnp.float32)
     columns_ref[...] = columns.astype(columns_ref.dtype)
-    rows = rows.astype(pieces_ref.dtype)
+    rows = columns.T.astype(pieces_ref.dtype)
     height = width // (Y * CORE)
     for y in range(Y):
         for c in range(CORE):
@@ -48,20 +43,50 @@
                 pieces_ref[x * CORE + c, y * height : (y + 1) * height] = rows[f * height : (f + 1) * height]
 
 
-def virtual_kernel(place_ref, prefix_ref, own_ref, other_ref, out_ref, rows_ref):
+def spread_kernel(rows_ref, out_ref):
+    for z in range(ZLO):
+        out_ref[z * X : (z + 1) * X] = rows_ref[...]
+
+
+def prefix_kernel(place_ref, *refs):
+    total_refs, decoders_ref, out_refs = refs[: TGT - 1], refs[TGT - 1], refs[TGT:]
+    step = 16
+    layers = decoders_ref.shape[0]
+
+    def rows(i, carry):
+        at = pl.ds(i * step, step)
+        base = total_refs[0][at].astype(jnp.float32)
+        for ref in total_refs[1:]:
+            base += ref[at].astype(jnp.float32)
+        written = [decoders_ref[k, at].astype(jnp.float32) for k in range(layers - 1)]
+        for r in range(X):
+            layer = (place_ref[0] + r) % X
+            out = base
+            for k in range(layers - 1):
+                counts = jnp.logical_and(k < layer, k >= place_ref[5])
+                out += written[k] * jnp.where(counts, 1.0, 0.0)
+            out_refs[r][at] = out.astype(jnp.bfloat16)
+        return carry
+
+    lax.fori_loop(0, decoders_ref.shape[1] // step, rows, 0)
+
+
+def virtual_kernel(place_ref, *refs):
+    prefix_refs, own_refs, other_ref, out_refs, rows_ref = refs[:X], refs[X : X + Y], refs[X + Y], refs[X + Y + 1 : -1], refs[-1]
     groups, slices, depth, width = rows_ref.shape
     core = place_ref[2]
     for r in range(Y):
         row = (place_ref[1] + Y - r) % Y
-        rows_ref[:, row * CORE + core] = own_ref[r].reshape(groups, depth, width)
+        rows_ref[:, row * CORE + core] = own_refs[r][...].reshape(groups, depth, width)
         rows_ref[:, row * CORE + 1 - core] = other_ref[r].reshape(groups, depth, width)
-    height = prefix_ref.shape[0] * prefix_ref.shape[1]
+    height = prefix_refs[0].shape[0]
     chunk = slices * depth
-    total = jnp.zeros((height, width), jnp.float32)
+    total = jnp.zeros((X * height, width), jnp.float32)
     for g in range(groups):
-        left = prefix_ref[:, :, g * chunk : (g + 1) * chunk].reshape(height, chunk)
+        left = jnp.concatenate([ref[:, g * chunk : (g + 1) * chunk] for ref in prefix_refs], 0)
         total += jnp.dot(left, rows_ref[g].reshape(chunk, width), preferred_element_type=jnp.float32)
-    out_ref[...] = total.reshape(out_ref.shape)
+    for r in range(X):
+        out_refs[r][...] = total[r * height : (r + 1) * height]
 
 
 def gram_kernel(place_ref, window_ref, own_ref, other_ref, out_ref):
@@ -110,17 +135,36 @@
     )(place, window_ids, sliced)
 
 
+def spread_of(rows):
+    return pl.pallas_call(
+        spread_kernel,
+        out_shape=jax.ShapeDtypeStruct((ZLO * rows.shape[0],) + rows.shape[1:], rows.dtype),
+        in_specs=[VMEM],
+        out_specs=VMEM,
+    )(rows)
+
+
+def prefix_of(place, totals, decoders):
+    piece = jax.ShapeDtypeStruct(decoders.shape[1:], jnp.bfloat16)
+    return pl.pallas_call(
+        prefix_kernel,
+        out_shape=[piece] * X,
+        in_specs=[SMEM] + [VMEM] * (len(totals) + 1),
+        out_specs=[VMEM] * X,
+    )(place, *totals, decoders)
+
+
 def virtual_of(place, prefix, own, other):
-    sources, height, depth = prefix.shape
-    width = own.shape[2]
+    height, depth = prefix[0].shape
+    width = other.shape[2]
     groups = ZLO * X
     return pl.pallas_call(
         virtual_kernel,
-        out_shape=jax.ShapeDtypeStruct((sources, height, width), jnp.float32),
-        in_specs=[SMEM, VMEM, VMEM, VMEM],
-        out_specs=VMEM,
+        out_shape=[jax.ShapeDtypeStruct((height, width), jnp.float32)] * X,
+        in_specs=[SMEM] + [VMEM] * (len(prefix) + len(own) + 1),
+        out_specs=[VMEM] * X,
         scratch_shapes=[pltpu.VMEM((groups, Y * CORE, depth // (groups * Y * CORE), width), jnp.bfloat16)],
-    )(place, prefix, own, other)
+    )(place, *prefix, *own, other)
 
 
 def gram_of(place, window, own, other):
@@ -147,8 +191,8 @@
 
 def over_feat(piece):
     others = [lax.ppermute(piece, "y", ring(Y, k)) for k in range(1, Y)]
-    own = jnp.stack([piece] + others)
-    return own, lax.ppermute(own, "core", ring(CORE, 1))
+    own = [piece] + others
+    return own, lax.ppermute(jnp.stack(own), "core", ring(CORE, 1))
 
 
 def per_device(activations, window_ids, decoders, encoders):
@@ -162,16 +206,13 @@
     slices = Y * CORE
     tokens = token_count // slices
 
-    depth = block * targets + jnp.arange(targets)
-    live = (depth >= source).astype(jnp.float32)
-    written = decoders[0].astype(jnp.float32) * live[:, None, None]
-    before = [jnp.zeros_like(written[0])]
-    for k in range(targets):
-        before.append(before[-1] + written[k])
-    total = before.pop()
+    place = [x, lax.axis_index("y"), lax.axis_index("core"), token_count, source, source - block * targets]
+    place = jnp.stack(place).astype(jnp.int32)
+
+    live = (block * targets + jnp.arange(targets) >= source).astype(jnp.float32)
+    total = jnp.sum(decoders[0].astype(jnp.float32) * live[:, None, None], 0).astype(jnp.bfloat16)
     earlier = [lax.ppermute(total, ("zlo", "tgt"), total_pairs(k)) for k in (3, 2, 1)]
 
-    place = jnp.stack([x, lax.axis_index("y"), lax.axis_index("core"), token_count, source]).astype(jnp.int32)
     by_tokens = split(activations[0].T, slices)
     sliced = lax.all_to_all(by_tokens, FEAT, 0, 0, tiled=True).reshape(slices * local_feats, tokens)
     columns, pieces = select(place, window_ids, sliced)
@@ -180,7 +221,7 @@
     target = jnp.where(zlo == block, columns, parts[0] + parts[1] + parts[2])
     swapped = lax.ppermute(target, "core", ring(CORE, 1))
 
-    spread = jnp.broadcast_to(encoders[None], (ZLO,) + encoders.shape).reshape((ZLO * X,) + encoders.shape[1:])
+    spread = spread_of(encoders)
     encoder_rows = lax.all_to_all(spread, ("zlo", "x"), 0, 0, tiled=True).reshape(-1, fw)
     encoder_own, encoder_other = over_feat(encoder_rows)
 
@@ -188,13 +229,9 @@
     partial = gram_of(place, window, target, swapped).reshape(X * Y, height, fw)
     partial = lax.all_to_all(partial, ("x", "y"), 0, 0, tiled=True).reshape(X, Y, height, fw)
 
-    base = earlier[0] + earlier[1] + earlier[2]
-    prefix = jnp.stack([(base + part).astype(jnp.bfloat16) for part in before])
-    pieces = [lax.dynamic_index_in_dim(prefix, (x + k) % X, 0, keepdims=False) for k in range(X)]
+    pieces = prefix_of(place, earlier, decoders[0])
     moved = [lax.ppermute(pieces[k], "x", ring(X, k)) for k in range(1, X)]
-    prefix = jnp.stack([pieces[0]] + moved)
-
-    virtual = virtual_of(place, prefix, encoder_own, encoder_other)
+    virtual = virtual_of(place, [pieces[0]] + moved, encoder_own, encoder_other)
     virtual = [virtual[0]] + [lax.ppermute(virtual[k], "x", ring(X, X - k)) for k in range(1, X)]
     return weigh(place, partial, virtual)[None]
 

time: 177 us -> 173 us (0.977)
  other arithmetic: 9.27 us -> 2.73 us
  Pallas kernels: 18 us -> 22.2 us
  waiting for transfers between devices: 77.3 us -> 74.2 us
    ppermute x3, waiting for transfers between devices: 19.1 us -> 11.2 us  [per_device(): moved = [lax.ppermute(pieces[k], 'x', ring(X, k)) for k in range(1, X)]]
    all_to_all x1, waiting for transfers between devices: 0.01 us -> 6.47 us  [per_device(): lax.all_to_all(spread, ('zlo', 'x'), 0, 0, tiled=True).reshape(-1, fw)]
    pallas_call x1 -> x3, Pallas kernels: 5.05 us -> 10.1 us  [the longest x1 5.04 us: virtual_of(): pl.pallas_call(virtual_kernel, out_shape=[jax.ShapeDtypeStruct((height, w...]
    another operation x5 -> x1, other arithmetic: 5.42 us -> 1.27 us  [over_feat(): return (own, lax.ppermute(jnp.stack(own), 'core', ring(CORE, 1)))]
    ppermute x3, waiting for transfers between devices: 9.12 us -> 5.38 us  [per_device(): lax.ppermute(columns, ('zlo', 'tgt'), window_pairs(k))]
    unnamed x18 -> x42, local copies, waits for them, and re-layouts: 1.44 us -> 4.06 us
    squeeze x1 -> x0, local copies, waits for them, and re-layouts: 1.98 us -> none  [per_device(): virtual[k]]
    ppermute x3, starting transfers between devices: 8.29 us -> 10.1 us  [per_device(): lax.ppermute(virtual[k], 'x', ring(X, X - k))]
  transfers between devices with their start and end apart: 21 -> 21, of which waited for: 8 -> 11; matrix products, arithmetic and copies ran while one was open for 7% -> 2% of each run, Pallas kernels for 7% -> 10%
where the time goes in v1:
time: 173 us; the launch traced here: 172 us
  waiting for transfers between devices  74.2 us (43%)
  starting transfers between devices  67.5 us (39%)
  Pallas kernels  22.2 us (13%)
  local copies, waits for them, and re-layouts  4.68 us (3%)
  other arithmetic  2.73 us (2%)
    ppermute x3, waiting for transfers between devices, per_device(): lax.ppermute(total, ('zlo', 'tgt'), total_pairs(k))  31.9 us
    ppermute x3, starting transfers between devices, per_device(): moved = [lax.ppermute(pieces[k], 'x', ring(X, k)) for k in range(1, X)]  11.3 us
    ppermute x3, waiting for transfers between devices, per_device(): moved = [lax.ppermute(pieces[k], 'x', ring(X, k)) for k in range(1, X)]  11.2 us
    ppermute x3, starting transfers between devices, per_device(): lax.ppermute(virtual[k], 'x', ring(X, X - k))  10.1 us
    ppermute x3, starting transfers between devices, over_feat(): others = [lax.ppermute(piece, 'y', ring(Y, k)) for k in range(1, Y)]  9.82 us
    ppermute x3, waiting for transfers between devices, per_device(): lax.ppermute(virtual[k], 'x', ring(X, X - k))  9.09 us
    all_to_all x1, waiting for transfers between devices, per_device(): lax.all_to_all(by_tokens, FEAT, 0, 0, tiled=True)  8.59 us
    ppermute x3, starting transfers between devices, per_device(): lax.ppermute(total, ('zlo', 'tgt'), total_pairs(k))  7.92 us
  transfers between devices with their start and end apart: 21, of which 11 were waited for; matrix products, arithmetic and copies ran while one was open for 2% of the time, Pallas kernels for 10%

profile of v1, /device:TPU:296, one launch (start us, length us, event | category | flops | bytes accessed | tf_op | source)
XLA Modules:
  0.0 171.7 jit_solution(6006703360108322058)
XLA Ops:
  2.2 4.9 %all-to-all-start = ((bf16[8,160,224]{2,1,0:T(8,128)(2,1)}), bf16[8,160,224]{2,1,0:T(8,128)(2,1)S(1)}, u32[]{:S(2)}, u32[]{:S(2)}) async-start(bf16[8,160,224]{2,1,0:T(8,128)(2,1)} %shard_map.46), calls=%async_computation | async-start | bytes 1310720 | tf_op jit(solution)/shard_map/all_to_all | solution.py:217
  8.8 8.6 %all-to-all-done = bf16[8,160,224]{2,1,0:T(8,128)(2,1)S(1)} async-done(((bf16[8,160,224]{2,1,0:T(8,128)(2,1)}), bf16[8,160,224]{2,1,0:T(8,128)(2,1)S(1)}, u32[]{:S(2)}, u32[]{:S(2)}) %all-to-all-start) | async-done | bytes 573472 | tf_op jit(solution)/shard_map/all_to_all | solution.py:217
  17.4 6.7 %all-to-all-start.3 = ((bf16[16,16,640]{2,1,0:T(8,128)(2,1)}), bf16[16,16,640]{2,1,0:T(8,128)(2,1)S(1)}, u32[]{:S(2)}, u32[]{:S(2)}) async-start(bf16[16,16,640]{2,1,0:T(8,128)(2,1)} %shard_map.50), calls=%async_computation.3 | async-start | bytes 655360 | tf_op jit(solution)/shard_map/all_to_all | solution.py:225
  24.7 3.3 %shard_map.47 = (bf16[224,640]{1,0:T(8,128)(2,1)}, bf16[8,320,224]{2,1,0:T(8,128)(2,1)}) custom-call(s32[6]{0:T(128)} %stack.35.place_ref, s32[16,640]{1,0:T(8,128)} %ids_ref.1, bf16[1280,224]{1,0:T(8,128)(2,1)} %bitcast.29), custom_call_target="tpu_custom_call" | custom-call | tf_op jit(solution)/shard_map/pallas_call | solution.py:127
  28.0 6.5 %all-to-all-done.3 = bf16[16,16,640]{2,1,0:T(8,128)(2,1)S(1)} async-done(((bf16[16,16,640]{2,1,0:T(8,128)(2,1)}), bf16[16,16,640]{2,1,0:T(8,128)(2,1)S(1)}, u32[]{:S(2)}, u32[]{:S(2)}) %all-to-all-start.3) | async-done | bytes 327712 | tf_op jit(solution)/shard_map/all_to_all | solution.py:225
  34.5 3.7 %all-to-all-start.1 = ((bf16[8,320,224]{2,1,0:T(8,128)(2,1)}), bf16[8,320,224]{2,1,0:T(8,128)(2,1)S(1)}, u32[]{:S(2)}, u32[]{:S(2)}) async-start(bf16[8,320,224]{2,1,0:T(8,128)(2,1)} %get-tuple-element.15), calls=%async_computation.1 | async-start | bytes 2621440 | tf_op jit(solution)/shard_map/all_to_all | solution.py:228
  42.9 5.3 %collective-permute-start.11 = (bf16[256,640]{1,0:T(8,128)(2,1)S(1)}, bf16[256,640]{1,0:T(8,128)(2,1)S(1)}, u32[]{:S(2)}, u32[]{:S(2)}) collective-permute-start(bf16[256,640]{1,0:T(8,128)(2,1)S(1)} %bitcast.25), channel_id=1, source_target_pairs={{0,4},{2,6},{4,0},{6,2},{1,5},{3,7},{5,1},{7,3},{8,12},{10,14},{12... | collective-permute-start | bytes 983048 | tf_op jit(solution)/shard_map/ppermute | solution.py:193
  48.2 2.5 %collective-permute-start.12 = (bf16[256,640]{1,0:T(8,128)(2,1)S(1)}, bf16[256,640]{1,0:T(8,128)(2,1)S(1)}, u32[]{:S(2)}, u32[]{:S(2)}) collective-permute-start(bf16[256,640]{1,0:T(8,128)(2,1)S(1)} %bitcast.26), channel_id=1, source_target_pairs={{0,6},{2,0},{4,2},{6,4},{1,7},{3,1},{5,3},{7,5},{8,14},{10,8},{12,... | collective-permute-start | bytes 983048 | tf_op jit(solution)/shard_map/ppermute | solution.py:193
  51.4 5.4 %collective-permute-done.2 = bf16[224,640]{1,0:T(8,128)(2,1)} collective-permute-done((bf16[224,640]{1,0:T(8,128)(2,1)S(1)}, bf16[224,640]{1,0:T(8,128)(2,1)}, u32[]{:S(2)}, u32[]{:S(2)}) %collective-permute-start.2) | collective-permute-done | bytes 286752 | tf_op jit(solution)/shard_map/ppermute | solution.py:220
  62.6 3.8 %shard_map.48 = bf16[4,320,640]{2,1,0:T(8,128)(2,1)} custom-call(s32[6]{0:T(128)} %stack.35.place_ref, bf16[4,2,320,224]{3,2,1,0:T(8,128)(2,1)} %bitcast.23, bf16[224,640]{1,0:T(8,128)(2,1)} %copy-done.8, bf16[224,640]{1,0:T(8,128)(2,1)} %copy-done.17), custom_call_target="tpu_custom_call" | custom-call | tf_op jit(solution)/shard_map/pallas_call | solution.py:171
  66.4 6.5 %all-to-all-start.2 = ((bf16[16,80,640]{2,1,0:T(8,128)(2,1)}), bf16[16,80,640]{2,1,0:T(8,128)(2,1)S(1)}, u32[]{:S(2)}, u32[]{:S(2)}) async-start(bf16[16,80,640]{2,1,0:T(8,128)(2,1)} %bitcast.21), calls=%async_computation.2 | async-start | bytes 3276800 | tf_op jit(solution)/shard_map/all_to_all | solution.py:230
  78.0 6.6 %collective-permute-start.6 = (bf16[80,2048]{1,0:T(8,128)(2,1)S(1)}, bf16[80,2048]{1,0:T(8,128)(2,1)S(1)}, u32[]{:S(2)}, u32[]{:S(2)}) collective-permute-start(bf16[80,2048]{1,0:T(8,128)(2,1)S(1)} %multiply_reduce_fusion), channel_id=1, source_target_pairs={{0,8},{8,16},{16,24},{136,144},{144,152},{272,280},{1,9},{9,17},{1... | collective-permute-start | bytes 983048 | tf_op jit(solution)/shard_map/ppermute | solution.py:214
  84.6 31.9 %collective-permute-done.6.refs_2_ = bf16[80,2048]{1,0:T(8,128)(2,1)S(1)} collective-permute-done((bf16[80,2048]{1,0:T(8,128)(2,1)S(1)}, bf16[80,2048]{1,0:T(8,128)(2,1)S(1)}, u32[]{:S(2)}, u32[]{:S(2)}) %collective-permute-start.6) | collective-permute-done | bytes 327712 | tf_op jit(solution)/shard_map/ppermute | solution.py:214
  117.2 3.4 %shard_map.49 = (bf16[80,2048]{1,0:T(8,128)(2,1)}, bf16[80,2048]{1,0:T(8,128)(2,1)}, bf16[80,2048]{1,0:T(8,128)(2,1)}, bf16[80,2048]{1,0:T(8,128)(2,1)}) custom-call(s32[6]{0:T(128)} %stack.35.place_ref, bf16[80,2048]{1,0:T(8,128)(2,1)} %copy-done.12, bf16[80,2048]{1,0:T(8,128)(2,1)} %copy-done.13, bf16[80,2048]{1,0:T(8,128)(2,1)} %copy-done.14, ...), custom_call_target="tpu_custom_call" | custom-call | tf_op jit(solution)/shard_map/pallas_call | solution.py:149
  120.6 3.4 %collective-permute-start.7 = (bf16[80,2048]{1,0:T(8,128)(2,1)}, bf16[80,2048]{1,0:T(8,128)(2,1)S(1)}, u32[]{:S(2)}, u32[]{:S(2)}) collective-permute-start(bf16[80,2048]{1,0:T(8,128)(2,1)} %get-tuple-element.18), channel_id=1, source_target_pairs={{0,32},{32,64},{64,96},{96,0},{1,33},{33,65},{65,97},{97,1},{2,34}... | collective-permute-start | bytes 983048 | tf_op jit(solution)/shard_map/ppermute | solution.py:233
  123.9 4.6 %collective-permute-start.8 = (bf16[80,2048]{1,0:T(8,128)(2,1)}, bf16[80,2048]{1,0:T(8,128)(2,1)S(1)}, u32[]{:S(2)}, u32[]{:S(2)}) collective-permute-start(bf16[80,2048]{1,0:T(8,128)(2,1)} %get-tuple-element.19), channel_id=1, source_target_pairs={{0,64},{32,96},{64,0},{96,32},{1,65},{33,97},{65,1},{97,33},{2,66}... | collective-permute-start | bytes 983048 | tf_op jit(solution)/shard_map/ppermute | solution.py:233
  128.5 3.4 %collective-permute-start.9 = (bf16[80,2048]{1,0:T(8,128)(2,1)}, bf16[80,2048]{1,0:T(8,128)(2,1)S(1)}, u32[]{:S(2)}, u32[]{:S(2)}) collective-permute-start(bf16[80,2048]{1,0:T(8,128)(2,1)} %get-tuple-element.20), channel_id=1, source_target_pairs={{0,96},{32,0},{64,32},{96,64},{1,97},{33,1},{65,33},{97,65},{2,98}... | collective-permute-start | bytes 983048 | tf_op jit(solution)/shard_map/ppermute | solution.py:233
  133.6 7.9 %collective-permute-done.8.refs_2_ = bf16[80,2048]{1,0:T(8,128)(2,1)S(1)} collective-permute-done((bf16[80,2048]{1,0:T(8,128)(2,1)}, bf16[80,2048]{1,0:T(8,128)(2,1)S(1)}, u32[]{:S(2)}, u32[]{:S(2)}) %collective-permute-start.8) | collective-permute-done | bytes 327712 | tf_op jit(solution)/shard_map/ppermute | solution.py:233
  143.9 5.0 %shard_map.51 = (f32[80,640]{1,0:T(8,128)}, f32[80,640]{1,0:T(8,128)}, f32[80,640]{1,0:T(8,128)}, f32[80,640]{1,0:T(8,128)}) custom-call(s32[6]{0:T(128)} %stack.35.place_ref, bf16[80,2048]{1,0:T(8,128)(2,1)} %get-tuple-element.17.refs_0_, bf16[80,2048]{1,0:T(8,128)(2,1)} %copy-done.9, bf16[80,2048]{1,0:T(8,128)(2,1)} %copy-done.10, ...), custom_call_target="tpu_custom_call" | custom-call | tf_op jit(solution)/shard_map/pallas_call | solution.py:161
  148.9 4.5 %collective-permute-start.14 = (f32[80,640]{1,0:T(8,128)}, f32[80,640]{1,0:T(8,128)S(1)}, u32[]{:S(2)}, u32[]{:S(2)}) collective-permute-start(f32[80,640]{1,0:T(8,128)} %get-tuple-element.22), channel_id=1, source_target_pairs={{0,96},{32,0},{64,32},{96,64},{1,97},{33,1},{65,33},{97,65},{2,98}... | collective-permute-start | bytes 614408 | tf_op jit(solution)/shard_map/ppermute | solution.py:235
  153.4 3.7 %collective-permute-start.15 = (f32[80,640]{1,0:T(8,128)}, f32[80,640]{1,0:T(8,128)S(1)}, u32[]{:S(2)}, u32[]{:S(2)}) collective-permute-start(f32[80,640]{1,0:T(8,128)} %get-tuple-element.23), channel_id=1, source_target_pairs={{0,64},{32,96},{64,0},{96,32},{1,65},{33,97},{65,1},{97,33},{2,66}... | collective-permute-start | bytes 614408 | tf_op jit(solution)/shard_map/ppermute | solution.py:235
  159.1 3.6 %collective-permute-done.14.refs_1_ = f32[80,640]{1,0:T(8,128)S(1)} collective-permute-done((f32[80,640]{1,0:T(8,128)}, f32[80,640]{1,0:T(8,128)S(1)}, u32[]{:S(2)}, u32[]{:S(2)}) %collective-permute-start.14) | collective-permute-done | bytes 204832 | tf_op jit(solution)/shard_map/ppermute | solution.py:235
  165.0 3.2 %collective-permute-done.16.refs_3_ = f32[80,640]{1,0:T(8,128)S(1)} collective-permute-done((f32[80,640]{1,0:T(8,128)}, f32[80,640]{1,0:T(8,128)S(1)}, u32[]{:S(2)}, u32[]{:S(2)}) %collective-permute-start.16) | collective-permute-done | bytes 204832 | tf_op jit(solution)/shard_map/ppermute | solution.py:235
  168.8 2.8 %shard_map.52 = f32[4,80,640]{2,1,0:T(8,128)} custom-call(s32[6]{0:T(128)} %stack.35.place_ref, bf16[4,4,80,640]{3,2,1,0:T(8,128)(2,1)} %bitcast.20, f32[80,640]{1,0:T(8,128)} %get-tuple-element.21.refs_0_, f32[80,640]{1,0:T(8,128)} %copy-done.18, f32[80,640]{1,0:T(8,128)} %copy-done.19, f32[80,640]{1,0:T(8,128)} %copy-done.20), custom_call_target="tpu_custom_call" | custom-call | tf_op jit(solution)/shard_map/pallas_call | solution.py:180
  (72 shorter events, 30.3 us)
Async XLA Ops:
  2.2 15.2 %all-to-all-start = ((bf16[8,160,224]{2,1,0:T(8,128)(2,1)}), bf16[8,160,224]{2,1,0:T(8,128)(2,1)S(1)}, u32[]{:S(2)}, u32[]{:S(2)}) async-start(bf16[8,160,224]{2,1,0:T(8,128)(2,1)} %shard_map.46), calls=%async_computation | async-start | bytes 1310720 | tf_op jit(solution)/shard_map/all_to_all | solution.py:217
  17.4 17.1 %all-to-all-start.3 = ((bf16[16,16,640]{2,1,0:T(8,128)(2,1)}), bf16[16,16,640]{2,1,0:T(8,128)(2,1)S(1)}, u32[]{:S(2)}, u32[]{:S(2)}) async-start(bf16[16,16,640]{2,1,0:T(8,128)(2,1)} %shard_map.50), calls=%async_computation.3 | async-start | bytes 655360 | tf_op jit(solution)/shard_map/all_to_all | solution.py:225
  34.5 38.5 %copy-start.3 = (bf16[16,16,640]{2,1,0:T(8,128)(2,1)}, bf16[16,16,640]{2,1,0:T(8,128)(2,1)S(1)}, u32[]{:S(2)}) copy-start(bf16[16,16,640]{2,1,0:T(8,128)(2,1)S(1)} %all-to-all-done.3) | copy-start | bytes 983044
  34.5 27.0 %all-to-all-start.1 = ((bf16[8,320,224]{2,1,0:T(8,128)(2,1)}), bf16[8,320,224]{2,1,0:T(8,128)(2,1)S(1)}, u32[]{:S(2)}, u32[]{:S(2)}) async-start(bf16[8,320,224]{2,1,0:T(8,128)(2,1)} %get-tuple-element.15), calls=%async_computation.1 | async-start | bytes 2621440 | tf_op jit(solution)/shard_map/all_to_all | solution.py:228
  38.2 10.0 %collective-permute-start = (bf16[224,640]{1,0:T(8,128)(2,1)S(1)}, bf16[224,640]{1,0:T(8,128)(2,1)S(1)}, u32[]{:S(2)}, u32[]{:S(2)}) collective-permute-start(bf16[224,640]{1,0:T(8,128)(2,1)S(1)} %copy-done.15), channel_id=1, source_target_pairs={{408,24},{409,25},{410,26},{411,27},{412,28},{413,29},{414,30},{41... | collective-permute-start | bytes 860168 | tf_op jit(solution)/shard_map/ppermute | solution.py:220
  38.9 11.8 %collective-permute-start.1 = (bf16[224,640]{1,0:T(8,128)(2,1)S(1)}, bf16[224,640]{1,0:T(8,128)(2,1)S(1)}, u32[]{:S(2)}, u32[]{:S(2)}) collective-permute-start(bf16[224,640]{1,0:T(8,128)(2,1)S(1)} %copy-done.15), channel_id=1, source_target_pairs={{272,16},{408,152},{273,17},{409,153},{274,18},{410,154},{275,19},... | collective-permute-start | bytes 860168 | tf_op jit(solution)/shard_map/ppermute | solution.py:220
  39.5 17.3 %collective-permute-start.2 = (bf16[224,640]{1,0:T(8,128)(2,1)S(1)}, bf16[224,640]{1,0:T(8,128)(2,1)}, u32[]{:S(2)}, u32[]{:S(2)}) collective-permute-start(bf16[224,640]{1,0:T(8,128)(2,1)S(1)} %copy-done.15), channel_id=1, source_target_pairs={{136,8},{272,144},{408,280},{137,9},{273,145},{409,281},{138,10},{... | collective-permute-start | bytes 860168 | tf_op jit(solution)/shard_map/ppermute | solution.py:220
  40.9 32.1 %collective-permute-start.10 = (bf16[256,640]{1,0:T(8,128)(2,1)S(1)}, bf16[256,640]{1,0:T(8,128)(2,1)S(1)}, u32[]{:S(2)}, u32[]{:S(2)}) collective-permute-start(bf16[256,640]{1,0:T(8,128)(2,1)S(1)} %bitcast.24), channel_id=1, source_target_pairs={{0,2},{2,4},{4,6},{6,0},{1,3},{3,5},{5,7},{7,1},{8,10},{10,12},{12... | collective-permute-start | bytes 983048 | tf_op jit(solution)/shard_map/ppermute | solution.py:193
  42.9 30.0 %collective-permute-start.11 = (bf16[256,640]{1,0:T(8,128)(2,1)S(1)}, bf16[256,640]{1,0:T(8,128)(2,1)S(1)}, u32[]{:S(2)}, u32[]{:S(2)}) collective-permute-start(bf16[256,640]{1,0:T(8,128)(2,1)S(1)} %bitcast.25), channel_id=1, source_target_pairs={{0,4},{2,6},{4,0},{6,2},{1,5},{3,7},{5,1},{7,3},{8,12},{10,14},{12... | collective-permute-start | bytes 983048 | tf_op jit(solution)/shard_map/ppermute | solution.py:193
  48.2 24.7 %collective-permute-start.12 = (bf16[256,640]{1,0:T(8,128)(2,1)S(1)}, bf16[256,640]{1,0:T(8,128)(2,1)S(1)}, u32[]{:S(2)}, u32[]{:S(2)}) collective-permute-start(bf16[256,640]{1,0:T(8,128)(2,1)S(1)} %bitcast.26), channel_id=1, source_target_pairs={{0,6},{2,0},{4,2},{6,4},{1,7},{3,1},{5,3},{7,5},{8,14},{10,8},{12,... | collective-permute-start | bytes 983048 | tf_op jit(solution)/shard_map/ppermute | solution.py:193
  58.0 3.5 %collective-permute-start.3 = (bf16[224,640]{1,0:T(8,128)(2,1)S(1)}, bf16[224,640]{1,0:T(8,128)(2,1)S(1)}, u32[]{:S(2)}, u32[]{:S(2)}) collective-permute-start(bf16[224,640]{1,0:T(8,128)(2,1)S(1)} %add_select_fusion.own_ref), channel_id=1, source_target_pairs={{0,1},{1,0},{2,3},{3,2},{4,5},{5,4},{6,7},{7,6},{8,9},{9,8},{10,11... | collective-permute-start | bytes 860168 | tf_op jit(solution)/shard_map/ppermute | solution.py:222
  66.4 92.6 %all-to-all-start.2 = ((bf16[16,80,640]{2,1,0:T(8,128)(2,1)}), bf16[16,80,640]{2,1,0:T(8,128)(2,1)S(1)}, u32[]{:S(2)}, u32[]{:S(2)}) async-start(bf16[16,80,640]{2,1,0:T(8,128)(2,1)} %bitcast.21), calls=%async_computation.2 | async-start | bytes 3276800 | tf_op jit(solution)/shard_map/all_to_all | solution.py:230
  74.3 68.8 %collective-permute-start.13 = (bf16[4,256,640]{2,1,0:T(8,128)(2,1)}, bf16[4,256,640]{2,1,0:T(8,128)(2,1)}, u32[]{:S(2)}, u32[]{:S(2)}) collective-permute-start(bf16[4,256,640]{2,1,0:T(8,128)(2,1)} %pad_maximum_fusion), channel_id=1, source_target_pairs={{0,1},{1,0},{2,3},{3,2},{4,5},{5,4},{6,7},{7,6},{8,9},{9,8},{10,11... | collective-permute-start | bytes 3932168 | tf_op jit(solution)/shard_map/ppermute | solution.py:195
  76.6 8.0 %collective-permute-start.4 = (bf16[80,2048]{1,0:T(8,128)(2,1)S(1)}, bf16[80,2048]{1,0:T(8,128)(2,1)S(1)}, u32[]{:S(2)}, u32[]{:S(2)}) collective-permute-start(bf16[80,2048]{1,0:T(8,128)(2,1)S(1)} %multiply_reduce_fusion), channel_id=1, source_target_pairs={{0,24},{1,25},{2,26},{3,27},{4,28},{5,29},{6,30},{7,31},{32,56},{3... | collective-permute-start | bytes 983048 | tf_op jit(solution)/shard_map/ppermute | solution.py:214
  77.3 7.3 %collective-permute-start.5 = (bf16[80,2048]{1,0:T(8,128)(2,1)S(1)}, bf16[80,2048]{1,0:T(8,128)(2,1)S(1)}, u32[]{:S(2)}, u32[]{:S(2)}) collective-permute-start(bf16[80,2048]{1,0:T(8,128)(2,1)S(1)} %multiply_reduce_fusion), channel_id=1, source_target_pairs={{0,16},{8,24},{136,152},{1,17},{9,25},{137,153},{2,18},{10,26},{13... | collective-permute-start | bytes 983048 | tf_op jit(solution)/shard_map/ppermute | solution.py:214
  78.0 38.5 %collective-permute-start.6 = (bf16[80,2048]{1,0:T(8,128)(2,1)S(1)}, bf16[80,2048]{1,0:T(8,128)(2,1)S(1)}, u32[]{:S(2)}, u32[]{:S(2)}) collective-permute-start(bf16[80,2048]{1,0:T(8,128)(2,1)S(1)} %multiply_reduce_fusion), channel_id=1, source_target_pairs={{0,8},{8,16},{16,24},{136,144},{144,152},{272,280},{1,9},{9,17},{1... | collective-permute-start | bytes 983048 | tf_op jit(solution)/shard_map/ppermute | solution.py:214
  84.5 31.9 %copy-start.12 = (bf16[80,2048]{1,0:T(8,128)(2,1)}, bf16[80,2048]{1,0:T(8,128)(2,1)S(1)}, u32[]{:S(2)}) copy-start(bf16[80,2048]{1,0:T(8,128)(2,1)S(1)} %collective-permute-done.4.refs_0_) | copy-start | bytes 983044
  84.6 31.9 %copy-start.13 = (bf16[80,2048]{1,0:T(8,128)(2,1)}, bf16[80,2048]{1,0:T(8,128)(2,1)S(1)}, u32[]{:S(2)}) copy-start(bf16[80,2048]{1,0:T(8,128)(2,1)S(1)} %collective-permute-done.5.refs_1_) | copy-start | bytes 983044
  120.6 13.0 %collective-permute-start.7 = (bf16[80,2048]{1,0:T(8,128)(2,1)}, bf16[80,2048]{1,0:T(8,128)(2,1)S(1)}, u32[]{:S(2)}, u32[]{:S(2)}) collective-permute-start(bf16[80,2048]{1,0:T(8,128)(2,1)} %get-tuple-element.18), channel_id=1, source_target_pairs={{0,32},{32,64},{64,96},{96,0},{1,33},{33,65},{65,97},{97,1},{2,34}... | collective-permute-start | bytes 983048 | tf_op jit(solution)/shard_map/ppermute | solution.py:233
  123.9 17.5 %collective-permute-start.8 = (bf16[80,2048]{1,0:T(8,128)(2,1)}, bf16[80,2048]{1,0:T(8,128)(2,1)S(1)}, u32[]{:S(2)}, u32[]{:S(2)}) collective-permute-start(bf16[80,2048]{1,0:T(8,128)(2,1)} %get-tuple-element.19), channel_id=1, source_target_pairs={{0,64},{32,96},{64,0},{96,32},{1,65},{33,97},{65,1},{97,33},{2,66}... | collective-permute-start | bytes 983048 | tf_op jit(solution)/shard_map/ppermute | solution.py:233
  128.5 14.6 %collective-permute-start.9 = (bf16[80,2048]{1,0:T(8,128)(2,1)}, bf16[80,2048]{1,0:T(8,128)(2,1)S(1)}, u32[]{:S(2)}, u32[]{:S(2)}) collective-permute-start(bf16[80,2048]{1,0:T(8,128)(2,1)} %get-tuple-element.20), channel_id=1, source_target_pairs={{0,96},{32,0},{64,32},{96,64},{1,97},{33,1},{65,33},{97,65},{2,98}... | collective-permute-start | bytes 983048 | tf_op jit(solution)/shard_map/ppermute | solution.py:233
  148.9 13.8 %collective-permute-start.14 = (f32[80,640]{1,0:T(8,128)}, f32[80,640]{1,0:T(8,128)S(1)}, u32[]{:S(2)}, u32[]{:S(2)}) collective-permute-start(f32[80,640]{1,0:T(8,128)} %get-tuple-element.22), channel_id=1, source_target_pairs={{0,96},{32,0},{64,32},{96,64},{1,97},{33,1},{65,33},{97,65},{2,98}... | collective-permute-start | bytes 614408 | tf_op jit(solution)/shard_map/ppermute | solution.py:235
  153.4 11.6 %collective-permute-start.15 = (f32[80,640]{1,0:T(8,128)}, f32[80,640]{1,0:T(8,128)S(1)}, u32[]{:S(2)}, u32[]{:S(2)}) collective-permute-start(f32[80,640]{1,0:T(8,128)} %get-tuple-element.23), channel_id=1, source_target_pairs={{0,64},{32,96},{64,0},{96,32},{1,65},{33,97},{65,1},{97,33},{2,66}... | collective-permute-start | bytes 614408 | tf_op jit(solution)/shard_map/ppermute | solution.py:235
  157.1 11.0 %collective-permute-start.16 = (f32[80,640]{1,0:T(8,128)}, f32[80,640]{1,0:T(8,128)S(1)}, u32[]{:S(2)}, u32[]{:S(2)}) collective-permute-start(f32[80,640]{1,0:T(8,128)} %get-tuple-element.24), channel_id=1, source_target_pairs={{0,32},{32,64},{64,96},{96,0},{1,33},{33,65},{65,97},{97,1},{2,34}... | collective-permute-start | bytes 614408 | tf_op jit(solution)/shard_map/ppermute | solution.py:235
  (18 other events, 55.5 us)

commit v2 on v1

--- a/solution.py
+++ b/solution.py
@@ -1,3 +1,5 @@
+import functools
+
 import jax
 import jax.numpy as jnp
 from jax import lax
@@ -27,7 +29,7 @@
     feats, tokens = sliced_ref.shape
     width = ids_ref.shape[1]
     step = 128
-    wide = jnp.broadcast_to(ids_ref[pl.ds(place_ref[4], 1), :], (step, width))
+    wide = jnp.broadcast_to(ids_ref[pl.ds(place_ref[3], 1), :], (step, width))
     columns = jnp.zeros((tokens, width), jnp.float32)
     for g in range(feats // step):
         part = sliced_ref[g * step : (g + 1) * step]
@@ -63,7 +65,7 @@
             layer = (place_ref[0] + r) % X
             out = base
             for k in range(layers - 1):
-                counts = jnp.logical_and(k < layer, k >= place_ref[5])
+                counts = jnp.logical_and(k < layer, k >= place_ref[4])
                 out += written[k] * jnp.where(counts, 1.0, 0.0)
             out_refs[r][at] = out.astype(jnp.bfloat16)
         return carry
@@ -82,9 +84,10 @@
     height = prefix_refs[0].shape[0]
     chunk = slices * depth
     total = jnp.zeros((X * height, width), jnp.float32)
-    for g in range(groups):
-        left = jnp.concatenate([ref[:, g * chunk : (g + 1) * chunk] for ref in prefix_refs], 0)
-        total += jnp.dot(left, rows_ref[g].reshape(chunk, width), preferred_element_type=jnp.float32)
+    for g in range(0, groups, 2):
+        left = jnp.concatenate([ref[:, g * chunk : (g + 2) * chunk] for ref in prefix_refs], 0)
+        right = rows_ref[g : g + 2].reshape(2 * chunk, width)
+        total += jnp.dot(left, right, preferred_element_type=jnp.float32)
     for r in range(X):
         out_refs[r][...] = total[r * height : (r + 1) * height]
 
@@ -97,15 +100,14 @@
         out_ref[q] = part.astype(out_ref.dtype)
 
 
-def weigh_kernel(place_ref, gram_ref, *refs):
+def weigh_kernel(scale, place_ref, gram_ref, *refs):
     virtual_refs, out_ref = refs[:-1], refs[-1]
-    token_count = place_ref[3].astype(jnp.float32)
     for r in range(X):
         layer = (place_ref[0] + r) % X
         gram = gram_ref[layer, 0].astype(jnp.float32)
         for row in range(1, Y):
             gram += gram_ref[layer, row].astype(jnp.float32)
-        out_ref[layer] = virtual_refs[r][...] * (gram / token_count)
+        out_ref[layer] = virtual_refs[r][...] * (gram * scale)
 
 
 SMEM = pl.BlockSpec(memory_space=pltpu.SMEM)
@@ -176,9 +178,9 @@
     )(place, window, own, other)
 
 
-def weigh(place, gram, virtual):
-    return pl.pallas_call(
-        weigh_kernel,
+def weigh(place, gram, virtual, token_count):
+    return pl.pallas_call(
+        functools.partial(weigh_kernel, 1.0 / token_count),
         out_shape=jax.ShapeDtypeStruct((X,) + virtual[0].shape, jnp.float32),
         in_specs=[SMEM, VMEM] + [VMEM] * len(virtual),
         out_specs=VMEM,
@@ -206,8 +208,12 @@
     slices = Y * CORE
     tokens = token_count // slices
 
-    place = [x, lax.axis_index("y"), lax.axis_index("core"), token_count, source, source - block * targets]
+    place = [x, lax.axis_index("y"), lax.axis_index("core"), source, source - block * targets]
     place = jnp.stack(place).astype(jnp.int32)
+
+    spread = spread_of(encoders)
+    encoder_rows = lax.all_to_all(spread, ("zlo", "x"), 0, 0, tiled=True).reshape(-1, fw)
+    encoder_own, encoder_other = over_feat(encoder_rows)
 
     live = (block * targets + jnp.arange(targets) >= source).astype(jnp.float32)
     total = jnp.sum(decoders[0].astype(jnp.float32) * live[:, None, None], 0).astype(jnp.bfloat16)
@@ -220,10 +226,6 @@
     parts = [lax.ppermute(columns, ("zlo", "tgt"), window_pairs(k)) for k in (3, 2, 1)]
     target = jnp.where(zlo == block, columns, parts[0] + parts[1] + parts[2])
     swapped = lax.ppermute(target, "core", ring(CORE, 1))
-
-    spread = spread_of(encoders)
-    encoder_rows = lax.all_to_all(spread, ("zlo", "x"), 0, 0, tiled=True).reshape(-1, fw)
-    encoder_own, encoder_other = over_feat(encoder_rows)
 
     window = lax.all_to_all(pieces, ("x", "core"), 0, 0, tiled=True).reshape(X, CORE, Y * height, tokens)
     partial = gram_of(place, window, target, swapped).reshape(X * Y, height, fw)
@@ -233,7 +235,7 @@
     moved = [lax.ppermute(pieces[k], "x", ring(X, k)) for k in range(1, X)]
     virtual = virtual_of(place, [pieces[0]] + moved, encoder_own, encoder_other)
     virtual = [virtual[0]] + [lax.ppermute(virtual[k], "x", ring(X, X - k)) for k in range(1, X)]
-    return weigh(place, partial, virtual)[None]
+    return weigh(place, partial, virtual, token_count)[None]
 
 
 def solution(mesh):

time: 173 us -> 172 us (level)
  no operation moved by 1% of the time
where the time goes in v2:
time: 172 us; the launch traced here: 171 us
  waiting for transfers between devices  74.2 us (43%)
  starting transfers between devices  67.5 us (39%)
  Pallas kernels  21.5 us (12%)
  local copies, waits for them, and re-layouts  4.68 us (3%)
  other arithmetic  2.73 us (2%)
    ppermute x3, waiting for transfers between devices, per_device(): lax.ppermute(total, ('zlo', 'tgt'), total_pairs(k))  31.9 us
    ppermute x3, starting transfers between devices, per_device(): moved = [lax.ppermute(pieces[k], 'x', ring(X, k)) for k in range(1, X)]  11.3 us
    ppermute x3, waiting for transfers between devices, per_device(): moved = [lax.ppermute(pieces[k], 'x', ring(X, k)) for k in range(1, X)]  11.2 us
    ppermute x3, starting transfers between devices, per_device(): lax.ppermute(virtual[k], 'x', ring(X, X - k))  10.1 us
    ppermute x3, starting transfers between devices, over_feat(): others = [lax.ppermute(piece, 'y', ring(Y, k)) for k in range(1, Y)]  9.82 us
    ppermute x3, waiting for transfers between devices, per_device(): lax.ppermute(virtual[k], 'x', ring(X, X - k))  9.09 us
    all_to_all x1, waiting for transfers between devices, per_device(): lax.all_to_all(by_tokens, FEAT, 0, 0, tiled=True)  8.59 us
    ppermute x3, starting transfers between devices, per_device(): lax.ppermute(total, ('zlo', 'tgt'), total_pairs(k))  7.92 us
  transfers between devices with their start and end apart: 21, of which 11 were waited for; matrix products, arithmetic and copies ran while one was open for 2% of the time, Pallas kernels for 10%

profile of v2, /device:TPU:296, one launch (start us, length us, event | category | flops | bytes accessed | tf_op | source)
XLA Modules:
  0.0 171.0 jit_solution(8105050336395388415)
XLA Ops:
  2.2 4.9 %all-to-all-start = ((bf16[8,160,224]{2,1,0:T(8,128)(2,1)}), bf16[8,160,224]{2,1,0:T(8,128)(2,1)S(1)}, u32[]{:S(2)}, u32[]{:S(2)}) async-start(bf16[8,160,224]{2,1,0:T(8,128)(2,1)} %shard_map.46), calls=%async_computation | async-start | bytes 1310720 | tf_op jit(solution)/shard_map/all_to_all | solution.py:223
  8.8 8.6 %all-to-all-done = bf16[8,160,224]{2,1,0:T(8,128)(2,1)S(1)} async-done(((bf16[8,160,224]{2,1,0:T(8,128)(2,1)}), bf16[8,160,224]{2,1,0:T(8,128)(2,1)S(1)}, u32[]{:S(2)}, u32[]{:S(2)}) %all-to-all-start) | async-done | bytes 573472 | tf_op jit(solution)/shard_map/all_to_all | solution.py:223
  17.4 6.7 %all-to-all-start.3 = ((bf16[16,16,640]{2,1,0:T(8,128)(2,1)}), bf16[16,16,640]{2,1,0:T(8,128)(2,1)S(1)}, u32[]{:S(2)}, u32[]{:S(2)}) async-start(bf16[16,16,640]{2,1,0:T(8,128)(2,1)} %shard_map.50), calls=%async_computation.3 | async-start | bytes 655360 | tf_op jit(solution)/shard_map/all_to_all | solution.py:215
  24.7 3.3 %shard_map.47 = (bf16[224,640]{1,0:T(8,128)(2,1)}, bf16[8,320,224]{2,1,0:T(8,128)(2,1)}) custom-call(s32[5]{0:T(128)} %stack.35.place_ref, s32[16,640]{1,0:T(8,128)} %ids_ref.1, bf16[1280,224]{1,0:T(8,128)(2,1)} %bitcast.29), custom_call_target="tpu_custom_call" | custom-call | tf_op jit(solution)/shard_map/pallas_call | solution.py:129
  28.0 6.5 %all-to-all-done.3 = bf16[16,16,640]{2,1,0:T(8,128)(2,1)S(1)} async-done(((bf16[16,16,640]{2,1,0:T(8,128)(2,1)}), bf16[16,16,640]{2,1,0:T(8,128)(2,1)S(1)}, u32[]{:S(2)}, u32[]{:S(2)}) %all-to-all-start.3) | async-done | bytes 327712 | tf_op jit(solution)/shard_map/all_to_all | solution.py:215
  34.5 3.7 %all-to-all-start.1 = ((bf16[8,320,224]{2,1,0:T(8,128)(2,1)}), bf16[8,320,224]{2,1,0:T(8,128)(2,1)S(1)}, u32[]{:S(2)}, u32[]{:S(2)}) async-start(bf16[8,320,224]{2,1,0:T(8,128)(2,1)} %get-tuple-element.15), calls=%async_computation.1 | async-start | bytes 2621440 | tf_op jit(solution)/shard_map/all_to_all | solution.py:230
  42.9 5.3 %collective-permute-start.11 = (bf16[256,640]{1,0:T(8,128)(2,1)S(1)}, bf16[256,640]{1,0:T(8,128)(2,1)S(1)}, u32[]{:S(2)}, u32[]{:S(2)}) collective-permute-start(bf16[256,640]{1,0:T(8,128)(2,1)S(1)} %bitcast.25), channel_id=1, source_target_pairs={{0,4},{2,6},{4,0},{6,2},{1,5},{3,7},{5,1},{7,3},{8,12},{10,14},{12... | collective-permute-start | bytes 983048 | tf_op jit(solution)/shard_map/ppermute | solution.py:195
  48.2 2.5 %collective-permute-start.12 = (bf16[256,640]{1,0:T(8,128)(2,1)S(1)}, bf16[256,640]{1,0:T(8,128)(2,1)S(1)}, u32[]{:S(2)}, u32[]{:S(2)}) collective-permute-start(bf16[256,640]{1,0:T(8,128)(2,1)S(1)} %bitcast.26), channel_id=1, source_target_pairs={{0,6},{2,0},{4,2},{6,4},{1,7},{3,1},{5,3},{7,5},{8,14},{10,8},{12,... | collective-permute-start | bytes 983048 | tf_op jit(solution)/shard_map/ppermute | solution.py:195
  51.4 5.4 %collective-permute-done.2 = bf16[224,640]{1,0:T(8,128)(2,1)} collective-permute-done((bf16[224,640]{1,0:T(8,128)(2,1)S(1)}, bf16[224,640]{1,0:T(8,128)(2,1)}, u32[]{:S(2)}, u32[]{:S(2)}) %collective-permute-start.2) | collective-permute-done | bytes 286752 | tf_op jit(solution)/shard_map/ppermute | solution.py:226
  62.6 3.8 %shard_map.48 = bf16[4,320,640]{2,1,0:T(8,128)(2,1)} custom-call(s32[5]{0:T(128)} %stack.35.place_ref, bf16[4,2,320,224]{3,2,1,0:T(8,128)(2,1)} %bitcast.23, bf16[224,640]{1,0:T(8,128)(2,1)} %copy-done.8, bf16[224,640]{1,0:T(8,128)(2,1)} %copy-done.17), custom_call_target="tpu_custom_call" | custom-call | tf_op jit(solution)/shard_map/pallas_call | solution.py:173
  66.4 6.5 %all-to-all-start.2 = ((bf16[16,80,640]{2,1,0:T(8,128)(2,1)}), bf16[16,80,640]{2,1,0:T(8,128)(2,1)S(1)}, u32[]{:S(2)}, u32[]{:S(2)}) async-start(bf16[16,80,640]{2,1,0:T(8,128)(2,1)} %bitcast.21), calls=%async_computation.2 | async-start | bytes 3276800 | tf_op jit(solution)/shard_map/all_to_all | solution.py:232
  78.0 6.6 %collective-permute-start.6 = (bf16[80,2048]{1,0:T(8,128)(2,1)S(1)}, bf16[80,2048]{1,0:T(8,128)(2,1)S(1)}, u32[]{:S(2)}, u32[]{:S(2)}) collective-permute-start(bf16[80,2048]{1,0:T(8,128)(2,1)S(1)} %multiply_reduce_fusion), channel_id=1, source_target_pairs={{0,8},{8,16},{16,24},{136,144},{144,152},{272,280},{1,9},{9,17},{1... | collective-permute-start | bytes 983048 | tf_op jit(solution)/shard_map/ppermute | solution.py:220
  84.6 31.9 %collective-permute-done.6.refs_2_ = bf16[80,2048]{1,0:T(8,128)(2,1)S(1)} collective-permute-done((bf16[80,2048]{1,0:T(8,128)(2,1)S(1)}, bf16[80,2048]{1,0:T(8,128)(2,1)S(1)}, u32[]{:S(2)}, u32[]{:S(2)}) %collective-permute-start.6) | collective-permute-done | bytes 327712 | tf_op jit(solution)/shard_map/ppermute | solution.py:220
  117.2 3.4 %shard_map.49 = (bf16[80,2048]{1,0:T(8,128)(2,1)}, bf16[80,2048]{1,0:T(8,128)(2,1)}, bf16[80,2048]{1,0:T(8,128)(2,1)}, bf16[80,2048]{1,0:T(8,128)(2,1)}) custom-call(s32[5]{0:T(128)} %stack.35.place_ref, bf16[80,2048]{1,0:T(8,128)(2,1)} %copy-done.12, bf16[80,2048]{1,0:T(8,128)(2,1)} %copy-done.13, bf16[80,2048]{1,0:T(8,128)(2,1)} %copy-done.14, ...), custom_call_target="tpu_custom_call" | custom-call | tf_op jit(solution)/shard_map/pallas_call | solution.py:151
  120.6 3.4 %collective-permute-start.7 = (bf16[80,2048]{1,0:T(8,128)(2,1)}, bf16[80,2048]{1,0:T(8,128)(2,1)S(1)}, u32[]{:S(2)}, u32[]{:S(2)}) collective-permute-start(bf16[80,2048]{1,0:T(8,128)(2,1)} %get-tuple-element.18), channel_id=1, source_target_pairs={{0,32},{32,64},{64,96},{96,0},{1,33},{33,65},{65,97},{97,1},{2,34}... | collective-permute-start | bytes 983048 | tf_op jit(solution)/shard_map/ppermute | solution.py:235
  123.9 4.6 %collective-permute-start.8 = (bf16[80,2048]{1,0:T(8,128)(2,1)}, bf16[80,2048]{1,0:T(8,128)(2,1)S(1)}, u32[]{:S(2)}, u32[]{:S(2)}) collective-permute-start(bf16[80,2048]{1,0:T(8,128)(2,1)} %get-tuple-element.19), channel_id=1, source_target_pairs={{0,64},{32,96},{64,0},{96,32},{1,65},{33,97},{65,1},{97,33},{2,66}... | collective-permute-start | bytes 983048 | tf_op jit(solution)/shard_map/ppermute | solution.py:235
  128.5 3.4 %collective-permute-start.9 = (bf16[80,2048]{1,0:T(8,128)(2,1)}, bf16[80,2048]{1,0:T(8,128)(2,1)S(1)}, u32[]{:S(2)}, u32[]{:S(2)}) collective-permute-start(bf16[80,2048]{1,0:T(8,128)(2,1)} %get-tuple-element.20), channel_id=1, source_target_pairs={{0,96},{32,0},{64,32},{96,64},{1,97},{33,1},{65,33},{97,65},{2,98}... | collective-permute-start | bytes 983048 | tf_op jit(solution)/shard_map/ppermute | solution.py:235
  133.6 7.9 %collective-permute-done.8.refs_2_ = bf16[80,2048]{1,0:T(8,128)(2,1)S(1)} collective-permute-done((bf16[80,2048]{1,0:T(8,128)(2,1)}, bf16[80,2048]{1,0:T(8,128)(2,1)S(1)}, u32[]{:S(2)}, u32[]{:S(2)}) %collective-permute-start.8) | collective-permute-done | bytes 327712 | tf_op jit(solution)/shard_map/ppermute | solution.py:235
  143.9 4.4 %shard_map.51 = (f32[80,640]{1,0:T(8,128)}, f32[80,640]{1,0:T(8,128)}, f32[80,640]{1,0:T(8,128)}, f32[80,640]{1,0:T(8,128)}) custom-call(s32[5]{0:T(128)} %stack.35.place_ref, bf16[80,2048]{1,0:T(8,128)(2,1)} %get-tuple-element.17.refs_0_, bf16[80,2048]{1,0:T(8,128)(2,1)} %copy-done.9, bf16[80,2048]{1,0:T(8,128)(2,1)} %copy-done.10, ...), custom_call_target="tpu_custom_call" | custom-call | tf_op jit(solution)/shard_map/pallas_call | solution.py:163
  148.2 4.5 %collective-permute-start.14 = (f32[80,640]{1,0:T(8,128)}, f32[80,640]{1,0:T(8,128)S(1)}, u32[]{:S(2)}, u32[]{:S(2)}) collective-permute-start(f32[80,640]{1,0:T(8,128)} %get-tuple-element.22), channel_id=1, source_target_pairs={{0,96},{32,0},{64,32},{96,64},{1,97},{33,1},{65,33},{97,65},{2,98}... | collective-permute-start | bytes 614408 | tf_op jit(solution)/shard_map/ppermute | solution.py:237
  152.7 3.7 %collective-permute-start.15 = (f32[80,640]{1,0:T(8,128)}, f32[80,640]{1,0:T(8,128)S(1)}, u32[]{:S(2)}, u32[]{:S(2)}) collective-permute-start(f32[80,640]{1,0:T(8,128)} %get-tuple-element.23), channel_id=1, source_target_pairs={{0,64},{32,96},{64,0},{96,32},{1,65},{33,97},{65,1},{97,33},{2,66}... | collective-permute-start | bytes 614408 | tf_op jit(solution)/shard_map/ppermute | solution.py:237
  158.4 3.6 %collective-permute-done.14.refs_1_ = f32[80,640]{1,0:T(8,128)S(1)} collective-permute-done((f32[80,640]{1,0:T(8,128)}, f32[80,640]{1,0:T(8,128)S(1)}, u32[]{:S(2)}, u32[]{:S(2)}) %collective-permute-start.14) | collective-permute-done | bytes 204832 | tf_op jit(solution)/shard_map/ppermute | solution.py:237
  164.3 3.2 %collective-permute-done.16.refs_3_ = f32[80,640]{1,0:T(8,128)S(1)} collective-permute-done((f32[80,640]{1,0:T(8,128)}, f32[80,640]{1,0:T(8,128)S(1)}, u32[]{:S(2)}, u32[]{:S(2)}) %collective-permute-start.16) | collective-permute-done | bytes 204832 | tf_op jit(solution)/shard_map/ppermute | solution.py:237
  168.1 2.8 %shard_map.52 = f32[4,80,640]{2,1,0:T(8,128)} custom-call(s32[5]{0:T(128)} %stack.35.place_ref, bf16[4,4,80,640]{3,2,1,0:T(8,128)(2,1)} %bitcast.20, f32[80,640]{1,0:T(8,128)} %get-tuple-element.21.refs_0_, f32[80,640]{1,0:T(8,128)} %copy-done.18, f32[80,640]{1,0:T(8,128)} %copy-done.19, f32[80,640]{1,0:T(8,128)} %copy-done.20), custom_call_target="tpu_custom_call" | custom-call | tf_op jit(solution)/shard_map/pallas_call | solution.py:182
  (72 shorter events, 30.3 us)
Async XLA Ops:
  2.2 15.2 %all-to-all-start = ((bf16[8,160,224]{2,1,0:T(8,128)(2,1)}), bf16[8,160,224]{2,1,0:T(8,128)(2,1)S(1)}, u32[]{:S(2)}, u32[]{:S(2)}) async-start(bf16[8,160,224]{2,1,0:T(8,128)(2,1)} %shard_map.46), calls=%async_computation | async-start | bytes 1310720 | tf_op jit(solution)/shard_map/all_to_all | solution.py:223
  17.4 17.1 %all-to-all-start.3 = ((bf16[16,16,640]{2,1,0:T(8,128)(2,1)}), bf16[16,16,640]{2,1,0:T(8,128)(2,1)S(1)}, u32[]{:S(2)}, u32[]{:S(2)}) async-start(bf16[16,16,640]{2,1,0:T(8,128)(2,1)} %shard_map.50), calls=%async_computation.3 | async-start | bytes 655360 | tf_op jit(solution)/shard_map/all_to_all | solution.py:215
  34.5 38.5 %copy-start.3 = (bf16[16,16,640]{2,1,0:T(8,128)(2,1)}, bf16[16,16,640]{2,1,0:T(8,128)(2,1)S(1)}, u32[]{:S(2)}) copy-start(bf16[16,16,640]{2,1,0:T(8,128)(2,1)S(1)} %all-to-all-done.3) | copy-start | bytes 983044
  34.5 27.0 %all-to-all-start.1 = ((bf16[8,320,224]{2,1,0:T(8,128)(2,1)}), bf16[8,320,224]{2,1,0:T(8,128)(2,1)S(1)}, u32[]{:S(2)}, u32[]{:S(2)}) async-start(bf16[8,320,224]{2,1,0:T(8,128)(2,1)} %get-tuple-element.15), calls=%async_computation.1 | async-start | bytes 2621440 | tf_op jit(solution)/shard_map/all_to_all | solution.py:230
  38.2 10.0 %collective-permute-start = (bf16[224,640]{1,0:T(8,128)(2,1)S(1)}, bf16[224,640]{1,0:T(8,128)(2,1)S(1)}, u32[]{:S(2)}, u32[]{:S(2)}) collective-permute-start(bf16[224,640]{1,0:T(8,128)(2,1)S(1)} %copy-done.15), channel_id=1, source_target_pairs={{408,24},{409,25},{410,26},{411,27},{412,28},{413,29},{414,30},{41... | collective-permute-start | bytes 860168 | tf_op jit(solution)/shard_map/ppermute | solution.py:226
  38.9 11.8 %collective-permute-start.1 = (bf16[224,640]{1,0:T(8,128)(2,1)S(1)}, bf16[224,640]{1,0:T(8,128)(2,1)S(1)}, u32[]{:S(2)}, u32[]{:S(2)}) collective-permute-start(bf16[224,640]{1,0:T(8,128)(2,1)S(1)} %copy-done.15), channel_id=1, source_target_pairs={{272,16},{408,152},{273,17},{409,153},{274,18},{410,154},{275,19},... | collective-permute-start | bytes 860168 | tf_op jit(solution)/shard_map/ppermute | solution.py:226
  39.5 17.3 %collective-permute-start.2 = (bf16[224,640]{1,0:T(8,128)(2,1)S(1)}, bf16[224,640]{1,0:T(8,128)(2,1)}, u32[]{:S(2)}, u32[]{:S(2)}) collective-permute-start(bf16[224,640]{1,0:T(8,128)(2,1)S(1)} %copy-done.15), channel_id=1, source_target_pairs={{136,8},{272,144},{408,280},{137,9},{273,145},{409,281},{138,10},{... | collective-permute-start | bytes 860168 | tf_op jit(solution)/shard_map/ppermute | solution.py:226
  40.9 32.1 %collective-permute-start.10 = (bf16[256,640]{1,0:T(8,128)(2,1)S(1)}, bf16[256,640]{1,0:T(8,128)(2,1)S(1)}, u32[]{:S(2)}, u32[]{:S(2)}) collective-permute-start(bf16[256,640]{1,0:T(8,128)(2,1)S(1)} %bitcast.24), channel_id=1, source_target_pairs={{0,2},{2,4},{4,6},{6,0},{1,3},{3,5},{5,7},{7,1},{8,10},{10,12},{12... | collective-permute-start | bytes 983048 | tf_op jit(solution)/shard_map/ppermute | solution.py:195
  42.9 30.0 %collective-permute-start.11 = (bf16[256,640]{1,0:T(8,128)(2,1)S(1)}, bf16[256,640]{1,0:T(8,128)(2,1)S(1)}, u32[]{:S(2)}, u32[]{:S(2)}) collective-permute-start(bf16[256,640]{1,0:T(8,128)(2,1)S(1)} %bitcast.25), channel_id=1, source_target_pairs={{0,4},{2,6},{4,0},{6,2},{1,5},{3,7},{5,1},{7,3},{8,12},{10,14},{12... | collective-permute-start | bytes 983048 | tf_op jit(solution)/shard_map/ppermute | solution.py:195
  48.2 24.7 %collective-permute-start.12 = (bf16[256,640]{1,0:T(8,128)(2,1)S(1)}, bf16[256,640]{1,0:T(8,128)(2,1)S(1)}, u32[]{:S(2)}, u32[]{:S(2)}) collective-permute-start(bf16[256,640]{1,0:T(8,128)(2,1)S(1)} %bitcast.26), channel_id=1, source_target_pairs={{0,6},{2,0},{4,2},{6,4},{1,7},{3,1},{5,3},{7,5},{8,14},{10,8},{12,... | collective-permute-start | bytes 983048 | tf_op jit(solution)/shard_map/ppermute | solution.py:195
  58.0 3.5 %collective-permute-start.3 = (bf16[224,640]{1,0:T(8,128)(2,1)S(1)}, bf16[224,640]{1,0:T(8,128)(2,1)S(1)}, u32[]{:S(2)}, u32[]{:S(2)}) collective-permute-start(bf16[224,640]{1,0:T(8,128)(2,1)S(1)} %add_select_fusion.own_ref), channel_id=1, source_target_pairs={{0,1},{1,0},{2,3},{3,2},{4,5},{5,4},{6,7},{7,6},{8,9},{9,8},{10,11... | collective-permute-start | bytes 860168 | tf_op jit(solution)/shard_map/ppermute | solution.py:228
  66.4 91.9 %all-to-all-start.2 = ((bf16[16,80,640]{2,1,0:T(8,128)(2,1)}), bf16[16,80,640]{2,1,0:T(8,128)(2,1)S(1)}, u32[]{:S(2)}, u32[]{:S(2)}) async-start(bf16[16,80,640]{2,1,0:T(8,128)(2,1)} %bitcast.21), calls=%async_computation.2 | async-start | bytes 3276800 | tf_op jit(solution)/shard_map/all_to_all | solution.py:232
  74.3 68.8 %collective-permute-start.13 = (bf16[4,256,640]{2,1,0:T(8,128)(2,1)}, bf16[4,256,640]{2,1,0:T(8,128)(2,1)}, u32[]{:S(2)}, u32[]{:S(2)}) collective-permute-start(bf16[4,256,640]{2,1,0:T(8,128)(2,1)} %pad_maximum_fusion), channel_id=1, source_target_pairs={{0,1},{1,0},{2,3},{3,2},{4,5},{5,4},{6,7},{7,6},{8,9},{9,8},{10,11... | collective-permute-start | bytes 3932168 | tf_op jit(solution)/shard_map/ppermute | solution.py:197
  76.6 8.0 %collective-permute-start.4 = (bf16[80,2048]{1,0:T(8,128)(2,1)S(1)}, bf16[80,2048]{1,0:T(8,128)(2,1)S(1)}, u32[]{:S(2)}, u32[]{:S(2)}) collective-permute-start(bf16[80,2048]{1,0:T(8,128)(2,1)S(1)} %multiply_reduce_fusion), channel_id=1, source_target_pairs={{0,24},{1,25},{2,26},{3,27},{4,28},{5,29},{6,30},{7,31},{32,56},{3... | collective-permute-start | bytes 983048 | tf_op jit(solution)/shard_map/ppermute | solution.py:220
  77.3 7.3 %collective-permute-start.5 = (bf16[80,2048]{1,0:T(8,128)(2,1)S(1)}, bf16[80,2048]{1,0:T(8,128)(2,1)S(1)}, u32[]{:S(2)}, u32[]{:S(2)}) collective-permute-start(bf16[80,2048]{1,0:T(8,128)(2,1)S(1)} %multiply_reduce_fusion), channel_id=1, source_target_pairs={{0,16},{8,24},{136,152},{1,17},{9,25},{137,153},{2,18},{10,26},{13... | collective-permute-start | bytes 983048 | tf_op jit(solution)/shard_map/ppermute | solution.py:220
  78.0 38.5 %collective-permute-start.6 = (bf16[80,2048]{1,0:T(8,128)(2,1)S(1)}, bf16[80,2048]{1,0:T(8,128)(2,1)S(1)}, u32[]{:S(2)}, u32[]{:S(2)}) collective-permute-start(bf16[80,2048]{1,0:T(8,128)(2,1)S(1)} %multiply_reduce_fusion), channel_id=1, source_target_pairs={{0,8},{8,16},{16,24},{136,144},{144,152},{272,280},{1,9},{9,17},{1... | collective-permute-start | bytes 983048 | tf_op jit(solution)/shard_map/ppermute | solution.py:220
  84.5 31.9 %copy-start.12 = (bf16[80,2048]{1,0:T(8,128)(2,1)}, bf16[80,2048]{1,0:T(8,128)(2,1)S(1)}, u32[]{:S(2)}) copy-start(bf16[80,2048]{1,0:T(8,128)(2,1)S(1)} %collective-permute-done.4.refs_0_) | copy-start | bytes 983044
  84.6 31.9 %copy-start.13 = (bf16[80,2048]{1,0:T(8,128)(2,1)}, bf16[80,2048]{1,0:T(8,128)(2,1)S(1)}, u32[]{:S(2)}) copy-start(bf16[80,2048]{1,0:T(8,128)(2,1)S(1)} %collective-permute-done.5.refs_1_) | copy-start | bytes 983044
  120.6 13.0 %collective-permute-start.7 = (bf16[80,2048]{1,0:T(8,128)(2,1)}, bf16[80,2048]{1,0:T(8,128)(2,1)S(1)}, u32[]{:S(2)}, u32[]{:S(2)}) collective-permute-start(bf16[80,2048]{1,0:T(8,128)(2,1)} %get-tuple-element.18), channel_id=1, source_target_pairs={{0,32},{32,64},{64,96},{96,0},{1,33},{33,65},{65,97},{97,1},{2,34}... | collective-permute-start | bytes 983048 | tf_op jit(solution)/shard_map/ppermute | solution.py:235
  123.9 17.5 %collective-permute-start.8 = (bf16[80,2048]{1,0:T(8,128)(2,1)}, bf16[80,2048]{1,0:T(8,128)(2,1)S(1)}, u32[]{:S(2)}, u32[]{:S(2)}) collective-permute-start(bf16[80,2048]{1,0:T(8,128)(2,1)} %get-tuple-element.19), channel_id=1, source_target_pairs={{0,64},{32,96},{64,0},{96,32},{1,65},{33,97},{65,1},{97,33},{2,66}... | collective-permute-start | bytes 983048 | tf_op jit(solution)/shard_map/ppermute | solution.py:235
  128.5 14.6 %collective-permute-start.9 = (bf16[80,2048]{1,0:T(8,128)(2,1)}, bf16[80,2048]{1,0:T(8,128)(2,1)S(1)}, u32[]{:S(2)}, u32[]{:S(2)}) collective-permute-start(bf16[80,2048]{1,0:T(8,128)(2,1)} %get-tuple-element.20), channel_id=1, source_target_pairs={{0,96},{32,0},{64,32},{96,64},{1,97},{33,1},{65,33},{97,65},{2,98}... | collective-permute-start | bytes 983048 | tf_op jit(solution)/shard_map/ppermute | solution.py:235
  148.2 13.8 %collective-permute-start.14 = (f32[80,640]{1,0:T(8,128)}, f32[80,640]{1,0:T(8,128)S(1)}, u32[]{:S(2)}, u32[]{:S(2)}) collective-permute-start(f32[80,640]{1,0:T(8,128)} %get-tuple-element.22), channel_id=1, source_target_pairs={{0,96},{32,0},{64,32},{96,64},{1,97},{33,1},{65,33},{97,65},{2,98}... | collective-permute-start | bytes 614408 | tf_op jit(solution)/shard_map/ppermute | solution.py:237
  152.7 11.6 %collective-permute-start.15 = (f32[80,640]{1,0:T(8,128)}, f32[80,640]{1,0:T(8,128)S(1)}, u32[]{:S(2)}, u32[]{:S(2)}) collective-permute-start(f32[80,640]{1,0:T(8,128)} %get-tuple-element.23), channel_id=1, source_target_pairs={{0,64},{32,96},{64,0},{96,32},{1,65},{33,97},{65,1},{97,33},{2,66}... | collective-permute-start | bytes 614408 | tf_op jit(solution)/shard_map/ppermute | solution.py:237
  156.4 11.0 %collective-permute-start.16 = (f32[80,640]{1,0:T(8,128)}, f32[80,640]{1,0:T(8,128)S(1)}, u32[]{:S(2)}, u32[]{:S(2)}) collective-permute-start(f32[80,640]{1,0:T(8,128)} %get-tuple-element.24), channel_id=1, source_target_pairs={{0,32},{32,64},{64,96},{96,0},{1,33},{33,65},{65,97},{97,1},{2,34}... | collective-permute-start | bytes 614408 | tf_op jit(solution)/shard_map/ppermute | solution.py:237
  (18 other events, 55.5 us)

commit v3 on v2

--- a/solution.py
+++ b/solution.py
@@ -45,13 +45,8 @@
                 pieces_ref[x * CORE + c, y * height : (y + 1) * height] = rows[f * height : (f + 1) * height]
 
 
-def spread_kernel(rows_ref, out_ref):
-    for z in range(ZLO):
-        out_ref[z * X : (z + 1) * X] = rows_ref[...]
-
-
 def prefix_kernel(place_ref, *refs):
-    total_refs, decoders_ref, out_refs = refs[: TGT - 1], refs[TGT - 1], refs[TGT:]
+    total_refs, decoders_ref, out_ref = refs[:-2], refs[-2], refs[-1]
     step = 16
     layers = decoders_ref.shape[0]
 
@@ -61,31 +56,30 @@
         for ref in total_refs[1:]:
             base += ref[at].astype(jnp.float32)
         written = [decoders_ref[k, at].astype(jnp.float32) for k in range(layers - 1)]
-        for r in range(X):
-            layer = (place_ref[0] + r) % X
-            out = base
-            for k in range(layers - 1):
-                counts = jnp.logical_and(k < layer, k >= place_ref[4])
-                out += written[k] * jnp.where(counts, 1.0, 0.0)
-            out_refs[r][at] = out.astype(jnp.bfloat16)
+        out_ref[0, at] = base.astype(jnp.bfloat16)
+        for k in range(layers - 1):
+            base += written[k] * jnp.where(k >= place_ref[4], 1.0, 0.0)
+            out_ref[k + 1, at] = base.astype(jnp.bfloat16)
         return carry
 
     lax.fori_loop(0, decoders_ref.shape[1] // step, rows, 0)
 
 
-def virtual_kernel(place_ref, *refs):
-    prefix_refs, own_refs, other_ref, out_refs, rows_ref = refs[:X], refs[X : X + Y], refs[X + Y], refs[X + Y + 1 : -1], refs[-1]
+def virtual_kernel(place_ref, prefix_ref, near_ref, far_ref, other_ref, *refs):
+    out_refs, rows_ref = refs[:-1], refs[-1]
     groups, slices, depth, width = rows_ref.shape
-    core = place_ref[2]
+    x, y, core = place_ref[0], place_ref[1], place_ref[2]
     for r in range(Y):
-        row = (place_ref[1] + Y - r) % Y
-        rows_ref[:, row * CORE + core] = own_refs[r][...].reshape(groups, depth, width)
+        row = jnp.bitwise_xor(y, r)
+        own = near_ref[r] if r < Y // 2 else far_ref[r - Y // 2]
+        rows_ref[:, row * CORE + core] = own.reshape(groups, depth, width)
         rows_ref[:, row * CORE + 1 - core] = other_ref[r].reshape(groups, depth, width)
-    height = prefix_refs[0].shape[0]
+    height = prefix_ref.shape[1]
     chunk = slices * depth
+    order = [(x + X - r) % X for r in range(X)]
     total = jnp.zeros((X * height, width), jnp.float32)
     for g in range(0, groups, 2):
-        left = jnp.concatenate([ref[:, g * chunk : (g + 2) * chunk] for ref in prefix_refs], 0)
+        left = jnp.concatenate([prefix_ref[q, :, g * chunk : (g + 2) * chunk] for q in order], 0)
         right = rows_ref[g : g + 2].reshape(2 * chunk, width)
         total += jnp.dot(left, right, preferred_element_type=jnp.float32)
     for r in range(X):
@@ -137,36 +131,26 @@
     )(place, window_ids, sliced)
 
 
-def spread_of(rows):
-    return pl.pallas_call(
-        spread_kernel,
-        out_shape=jax.ShapeDtypeStruct((ZLO * rows.shape[0],) + rows.shape[1:], rows.dtype),
-        in_specs=[VMEM],
-        out_specs=VMEM,
-    )(rows)
-
-
 def prefix_of(place, totals, decoders):
-    piece = jax.ShapeDtypeStruct(decoders.shape[1:], jnp.bfloat16)
     return pl.pallas_call(
         prefix_kernel,
-        out_shape=[piece] * X,
+        out_shape=jax.ShapeDtypeStruct(decoders.shape, jnp.bfloat16),
         in_specs=[SMEM] + [VMEM] * (len(totals) + 1),
-        out_specs=[VMEM] * X,
+        out_specs=VMEM,
     )(place, *totals, decoders)
 
 
-def virtual_of(place, prefix, own, other):
-    height, depth = prefix[0].shape
+def virtual_of(place, prefix, near, far, other):
+    height, depth = prefix.shape[1:]
     width = other.shape[2]
     groups = ZLO * X
     return pl.pallas_call(
         virtual_kernel,
         out_shape=[jax.ShapeDtypeStruct((height, width), jnp.float32)] * X,
-        in_specs=[SMEM] + [VMEM] * (len(prefix) + len(own) + 1),
+        in_specs=[SMEM] + [VMEM] * 4,
         out_specs=[VMEM] * X,
         scratch_shapes=[pltpu.VMEM((groups, Y * CORE, depth // (groups * Y * CORE), width), jnp.bfloat16)],
-    )(place, *prefix, *own, other)
+    )(place, prefix, near, far, other)
 
 
 def gram_of(place, window, own, other):
@@ -192,9 +176,10 @@
 
 
 def over_feat(piece):
-    others = [lax.ppermute(piece, "y", ring(Y, k)) for k in range(1, Y)]
-    own = [piece] + others
-    return own, lax.ppermute(jnp.stack(own), "core", ring(CORE, 1))
+    near = jnp.stack([piece, lax.ppermute(piece, "y", [(i, i ^ 1) for i in range(Y)])])
+    far = lax.ppermute(near, "y", [(i, i ^ 2) for i in range(Y)])
+    other = lax.ppermute(jnp.concatenate([near, far]), "core", ring(CORE, 1))
+    return near, far, other
 
 
 def per_device(activations, window_ids, decoders, encoders):
@@ -211,9 +196,9 @@
     place = [x, lax.axis_index("y"), lax.axis_index("core"), source, source - block * targets]
     place = jnp.stack(place).astype(jnp.int32)
 
-    spread = spread_of(encoders)
+    spread = jnp.broadcast_to(encoders[None], (ZLO,) + encoders.shape).reshape((ZLO * X,) + encoders.shape[1:])
     encoder_rows = lax.all_to_all(spread, ("zlo", "x"), 0, 0, tiled=True).reshape(-1, fw)
-    encoder_own, encoder_other = over_feat(encoder_rows)
+    encoder = over_feat(encoder_rows)
 
     live = (block * targets + jnp.arange(targets) >= source).astype(jnp.float32)
     total = jnp.sum(decoders[0].astype(jnp.float32) * live[:, None, None], 0).astype(jnp.bfloat16)
@@ -231,9 +216,9 @@
     partial = gram_of(place, window, target, swapped).reshape(X * Y, height, fw)
     partial = lax.all_to_all(partial, ("x", "y"), 0, 0, tiled=True).reshape(X, Y, height, fw)
 
-    pieces = prefix_of(place, earlier, decoders[0])
-    moved = [lax.ppermute(pieces[k], "x", ring(X, k)) for k in range(1, X)]
-    virtual = virtual_of(place, [pieces[0]] + moved, encoder_own, encoder_other)
+    prefix = prefix_of(place, earlier, decoders[0])
+    prefix = lax.all_to_all(prefix, "x", 0, 0, tiled=True)
+    virtual = virtual_of(place, prefix, *encoder)
     virtual = [virtual[0]] + [lax.ppermute(virtual[k], "x", ring(X, X - k)) for k in range(1, X)]
     return weigh(place, partial, virtual, token_count)[None]
 

time: 172 us -> 153 us (0.89)
  the two profiles are of different devices: /device:TPU:296 before, /device:TPU:289 now
where the time goes in v3:
time: 153 us; the launch traced here: 152 us
  waiting for transfers between devices  55.8 us (36%)
  starting transfers between devices  50.8 us (33%)
  Pallas kernels  19.6 us (13%)
  blocking collectives  16.1 us (11%)
  local copies, waits for them, and re-layouts  6.75 us (4%)
  other arithmetic  2.66 us (2%)
    ppermute x3, waiting for transfers between devices, per_device(): lax.ppermute(total, ('zlo', 'tgt'), total_pairs(k))  32.1 us
    all_to_all x1, blocking collectives, per_device(): lax.all_to_all(by_tokens, FEAT, 0, 0, tiled=True)  16.1 us
    ppermute x3, starting transfers between devices, per_device(): lax.ppermute(virtual[k], 'x', ring(X, X - k))  9.72 us
    ppermute x3, waiting for transfers between devices, per_device(): lax.ppermute(virtual[k], 'x', ring(X, X - k))  8.77 us
    all_to_all x1, starting transfers between devices, per_device(): lax.all_to_all(pieces, ('x', 'core'), 0, 0, tiled=True)  6.41 us
    all_to_all x1, starting transfers between devices, per_device(): lax.all_to_all(spread, ('zlo', 'x'), 0, 0, tiled=True).reshape(-1, fw)  6.12 us
    ppermute x3, starting transfers between devices, per_device(): lax.ppermute(total, ('zlo', 'tgt'), total_pairs(k))  5.98 us
    unnamed x32, local copies, waits for them, and re-layouts  5.39 us
  transfers between devices with their start and end apart: 17, of which 9 were waited for; matrix products, arithmetic and copies ran while one was open for 2% of the time, Pallas kernels for 10%

profile of v3, /device:TPU:289, one launch (start us, length us, event | category | flops | bytes accessed | tf_op | source)
XLA Modules:
  0.0 152.0 jit_solution(5881323667274213509)
XLA Ops:
  0.0 2.2 %shard_map.46 = bf16[8,160,224]{2,1,0:T(8,128)(2,1)} custom-call(bf16[160,1792]{1,0:T(8,128)(2,1)} %bitcast.29), custom_call_target="tpu_custom_call" | custom-call | tf_op jit(solution)/shard_map/pallas_call | solution.py:113
  2.2 16.1 %all_to_all.25 = bf16[8,160,224]{2,1,0:T(8,128)(2,1)} all-to-all(bf16[8,160,224]{2,1,0:T(8,128)(2,1)} %shard_map.46), channel_id=1, replica_groups=mesh['zlo'=4,'x'=4,'tgt'=4,'y'=4,'core'=2] {'y','core'}, dimensions={0} | all-to-all | bytes 1146880 | tf_op jit(solution)/shard_map/all_to_all | solution.py:208
  19.1 6.1 %all-to-all-start.4 = ((bf16[16,16,640]{2,1,0:T(8,128)(2,1)}), bf16[16,16,640]{2,1,0:T(8,128)(2,1)S(1)}, u32[]{:S(2)}, u32[]{:S(2)}) async-start(bf16[16,16,640]{2,1,0:T(8,128)(2,1)} %bitcast.12), calls=%async_computation.4 | async-start | bytes 655360 | tf_op jit(solution)/shard_map/all_to_all | solution.py:200
  25.8 3.3 %shard_map.47 = (bf16[224,640]{1,0:T(8,128)(2,1)}, bf16[8,320,224]{2,1,0:T(8,128)(2,1)}) custom-call(s32[5]{0:T(128)} %stack.29.place_ref, s32[16,640]{1,0:T(8,128)} %ids_ref.1, bf16[1280,224]{1,0:T(8,128)(2,1)} %bitcast.26), custom_call_target="tpu_custom_call" | custom-call | tf_op jit(solution)/shard_map/pallas_call | solution.py:123
  29.1 5.3 %all-to-all-done.4 = bf16[16,16,640]{2,1,0:T(8,128)(2,1)S(1)} async-done(((bf16[16,16,640]{2,1,0:T(8,128)(2,1)}), bf16[16,16,640]{2,1,0:T(8,128)(2,1)S(1)}, u32[]{:S(2)}, u32[]{:S(2)}) %all-to-all-start.4) | async-done | bytes 327712 | tf_op jit(solution)/shard_map/all_to_all | solution.py:200
  34.4 6.4 %all-to-all-start.1 = ((bf16[8,320,224]{2,1,0:T(8,128)(2,1)}), bf16[8,320,224]{2,1,0:T(8,128)(2,1)S(1)}, u32[]{:S(2)}, u32[]{:S(2)}) async-start(bf16[8,320,224]{2,1,0:T(8,128)(2,1)} %get-tuple-element.11), calls=%async_computation.1 | async-start | bytes 2621440 | tf_op jit(solution)/shard_map/all_to_all | solution.py:215
  42.5 4.6 %collective-permute-start.6 = (bf16[80,2048]{1,0:T(8,128)(2,1)S(1)}, bf16[80,2048]{1,0:T(8,128)(2,1)S(1)}, u32[]{:S(2)}, u32[]{:S(2)}) collective-permute-start(bf16[80,2048]{1,0:T(8,128)(2,1)S(1)} %multiply_reduce_fusion), channel_id=1, source_target_pairs={{0,8},{8,16},{16,24},{136,144},{144,152},{272,280},{1,9},{9,17},{1... | collective-permute-start | bytes 983048 | tf_op jit(solution)/shard_map/ppermute | solution.py:205
  49.4 32.1 %collective-permute-done.6.refs_2_ = bf16[80,2048]{1,0:T(8,128)(2,1)S(1)} collective-permute-done((bf16[80,2048]{1,0:T(8,128)(2,1)S(1)}, bf16[80,2048]{1,0:T(8,128)(2,1)S(1)}, u32[]{:S(2)}, u32[]{:S(2)}) %collective-permute-start.6) | collective-permute-done | bytes 327712 | tf_op jit(solution)/shard_map/ppermute | solution.py:205
  82.2 3.1 %shard_map.49 = bf16[4,80,2048]{2,1,0:T(8,128)(2,1)} custom-call(s32[5]{0:T(128)} %stack.29.place_ref, bf16[80,2048]{1,0:T(8,128)(2,1)} %copy-done.7, bf16[80,2048]{1,0:T(8,128)(2,1)} %copy-done.8, bf16[80,2048]{1,0:T(8,128)(2,1)} %copy-done.9, bf16[4,80,2048]{2,1,0:T(8,128)(2,1)} %bitcast.21), custom_call_target="tpu_custom_call" | custom-call | tf_op jit(solution)/shard_map/pallas_call | solution.py:135
  86.4 4.1 %all-to-all-start.3 = ((bf16[4,80,2048]{2,1,0:T(8,128)(2,1)}), bf16[4,80,2048]{2,1,0:T(8,128)(2,1)S(1)}, u32[]{:S(2)}, u32[]{:S(2)}) async-start(bf16[4,80,2048]{2,1,0:T(8,128)(2,1)} %shard_map.49), calls=%async_computation.3 | async-start | bytes 2621440 | tf_op jit(solution)/shard_map/all_to_all | solution.py:220
  94.1 2.5 %collective-permute-start.8 = (bf16[2,256,640]{2,1,0:T(8,128)(2,1)}, bf16[2,256,640]{2,1,0:T(8,128)(2,1)}, u32[]{:S(2)}, u32[]{:S(2)}) collective-permute-start(bf16[2,256,640]{2,1,0:T(8,128)(2,1)} %pad_maximum_fusion.1.near_ref), channel_id=1, source_target_pairs={{0,4},{2,6},{4,0},{6,2},{1,5},{3,7},{5,1},{7,3},{8,12},{10,14},{12... | collective-permute-start | bytes 1966088 | tf_op jit(solution)/shard_map/ppermute | solution.py:180
  96.7 4.7 %collective-permute-done.2 = bf16[224,640]{1,0:T(8,128)(2,1)S(1)} collective-permute-done((bf16[224,640]{1,0:T(8,128)(2,1)S(1)}, bf16[224,640]{1,0:T(8,128)(2,1)S(1)}, u32[]{:S(2)}, u32[]{:S(2)}) %collective-permute-start.2) | collective-permute-done | bytes 286752 | tf_op jit(solution)/shard_map/ppermute | solution.py:211
  101.4 3.6 %collective-permute-start.3 = (bf16[224,640]{1,0:T(8,128)(2,1)S(1)}, bf16[224,640]{1,0:T(8,128)(2,1)S(1)}, u32[]{:S(2)}, u32[]{:S(2)}) collective-permute-start(bf16[224,640]{1,0:T(8,128)(2,1)S(1)} %add_select_fusion.own_ref), channel_id=1, source_target_pairs={{0,1},{1,0},{2,3},{3,2},{4,5},{5,4},{6,7},{7,6},{8,9},{9,8},{10,11... | collective-permute-start | bytes 860168 | tf_op jit(solution)/shard_map/ppermute | solution.py:213
  106.9 3.8 %shard_map.48 = bf16[4,320,640]{2,1,0:T(8,128)(2,1)} custom-call(s32[5]{0:T(128)} %stack.29.place_ref, bf16[4,2,320,224]{3,2,1,0:T(8,128)(2,1)} %bitcast.22, bf16[224,640]{1,0:T(8,128)(2,1)} %copy-done.6, bf16[224,640]{1,0:T(8,128)(2,1)} %copy-done.11), custom_call_target="tpu_custom_call" | custom-call | tf_op jit(solution)/shard_map/pallas_call | solution.py:157
  111.8 5.0 %all-to-all-start.2 = ((bf16[16,80,640]{2,1,0:T(8,128)(2,1)}), bf16[16,80,640]{2,1,0:T(8,128)(2,1)S(1)}, u32[]{:S(2)}, u32[]{:S(2)}) async-start(bf16[16,80,640]{2,1,0:T(8,128)(2,1)} %bitcast.20), calls=%async_computation.2 | async-start | bytes 3276800 | tf_op jit(solution)/shard_map/all_to_all | solution.py:217
  118.1 2.6 %collective-permute-start.9 = (bf16[4,256,640]{2,1,0:T(8,128)(2,1)S(1)}, bf16[4,256,640]{2,1,0:T(8,128)(2,1)S(1)}, u32[]{:S(2)}, u32[]{:S(2)}) collective-permute-start(bf16[4,256,640]{2,1,0:T(8,128)(2,1)S(1)} %pad_maximum_fusion), channel_id=1, source_target_pairs={{0,1},{1,0},{2,3},{3,2},{4,5},{5,4},{6,7},{7,6},{8,9},{9,8},{10,11... | collective-permute-start | bytes 3932168 | tf_op jit(solution)/shard_map/ppermute | solution.py:181
  120.7 2.6 %collective-permute-done.9.other_ref = bf16[4,256,640]{2,1,0:T(8,128)(2,1)S(1)} collective-permute-done((bf16[4,256,640]{2,1,0:T(8,128)(2,1)S(1)}, bf16[4,256,640]{2,1,0:T(8,128)(2,1)S(1)}, u32[]{:S(2)}, u32[]{:S(2)}) %collective-permute-start.9) | collective-permute-done | bytes 1310752 | tf_op jit(solution)/shard_map/ppermute | solution.py:181
  124.4 4.4 %shard_map.50 = (f32[80,640]{1,0:T(8,128)}, f32[80,640]{1,0:T(8,128)}, f32[80,640]{1,0:T(8,128)}, f32[80,640]{1,0:T(8,128)}) custom-call(s32[5]{0:T(128)} %stack.29.place_ref, bf16[4,80,2048]{2,1,0:T(8,128)(2,1)} %copy-done.1, bf16[2,256,640]{2,1,0:T(8,128)(2,1)} %pad_maximum_fusion.1.near_ref, bf16[2,256,640]{2,1,0:T(8,128)(2,1)} %collective-permute-done.8.far_ref, ...), custom_call_target="tpu_custom_call" | custom-call | tf_op jit(solution)/shard_map/pallas_call | solution.py:147
  128.8 4.8 %collective-permute-start.10 = (f32[80,640]{1,0:T(8,128)}, f32[80,640]{1,0:T(8,128)S(1)}, u32[]{:S(2)}, u32[]{:S(2)}) collective-permute-start(f32[80,640]{1,0:T(8,128)} %get-tuple-element.14), channel_id=1, source_target_pairs={{0,96},{32,0},{64,32},{96,64},{1,97},{33,1},{65,33},{97,65},{2,98}... | collective-permute-start | bytes 614408 | tf_op jit(solution)/shard_map/ppermute | solution.py:222
  133.5 2.5 %collective-permute-start.11 = (f32[80,640]{1,0:T(8,128)}, f32[80,640]{1,0:T(8,128)S(1)}, u32[]{:S(2)}, u32[]{:S(2)}) collective-permute-start(f32[80,640]{1,0:T(8,128)} %get-tuple-element.15), channel_id=1, source_target_pairs={{0,64},{32,96},{64,0},{96,32},{1,65},{33,97},{65,1},{97,33},{2,66}... | collective-permute-start | bytes 614408 | tf_op jit(solution)/shard_map/ppermute | solution.py:222
  136.0 2.5 %collective-permute-start.12 = (f32[80,640]{1,0:T(8,128)}, f32[80,640]{1,0:T(8,128)S(1)}, u32[]{:S(2)}, u32[]{:S(2)}) collective-permute-start(f32[80,640]{1,0:T(8,128)} %get-tuple-element.16), channel_id=1, source_target_pairs={{0,32},{32,64},{64,96},{96,0},{1,33},{33,65},{65,97},{97,1},{2,34}... | collective-permute-start | bytes 614408 | tf_op jit(solution)/shard_map/ppermute | solution.py:222
  140.5 2.6 %collective-permute-done.11.refs_2_ = f32[80,640]{1,0:T(8,128)S(1)} collective-permute-done((f32[80,640]{1,0:T(8,128)}, f32[80,640]{1,0:T(8,128)S(1)}, u32[]{:S(2)}, u32[]{:S(2)}) %collective-permute-start.11) | collective-permute-done | bytes 204832 | tf_op jit(solution)/shard_map/ppermute | solution.py:222
  143.1 5.3 %collective-permute-done.12.refs_3_ = f32[80,640]{1,0:T(8,128)S(1)} collective-permute-done((f32[80,640]{1,0:T(8,128)}, f32[80,640]{1,0:T(8,128)S(1)}, u32[]{:S(2)}, u32[]{:S(2)}) %collective-permute-start.12) | collective-permute-done | bytes 204832 | tf_op jit(solution)/shard_map/ppermute | solution.py:222
  149.2 2.8 %shard_map.51 = f32[4,80,640]{2,1,0:T(8,128)} custom-call(s32[5]{0:T(128)} %stack.29.place_ref, bf16[4,4,80,640]{3,2,1,0:T(8,128)(2,1)} %bitcast.19, f32[80,640]{1,0:T(8,128)} %get-tuple-element.13.refs_0_, f32[80,640]{1,0:T(8,128)} %copy-done.12, f32[80,640]{1,0:T(8,128)} %copy-done.13, f32[80,640]{1,0:T(8,128)} %copy-done.14), custom_call_target="tpu_custom_call" | custom-call | tf_op jit(solution)/shard_map/pallas_call | solution.py:166
  (56 shorter events, 18.8 us)
Async XLA Ops:
  0.0 18.4 %copy-start.15 = (bf16[4,16,640]{2,1,0:T(8,128)(2,1)S(1)}, bf16[4,16,640]{2,1,0:T(8,128)(2,1)}, u32[]{:S(2)}) copy-start(bf16[4,16,640]{2,1,0:T(8,128)(2,1)} %param.7) | copy-start | bytes 245764
  19.1 15.3 %all-to-all-start.4 = ((bf16[16,16,640]{2,1,0:T(8,128)(2,1)}), bf16[16,16,640]{2,1,0:T(8,128)(2,1)S(1)}, u32[]{:S(2)}, u32[]{:S(2)}) async-start(bf16[16,16,640]{2,1,0:T(8,128)(2,1)} %bitcast.12), calls=%async_computation.4 | async-start | bytes 655360 | tf_op jit(solution)/shard_map/all_to_all | solution.py:200
  34.4 6.4 %copy-start.2 = (bf16[1,4,80,2048]{3,2,1,0:T(8,128)(2,1)S(1)}, bf16[1,4,80,2048]{3,2,1,0:T(8,128)(2,1)}, u32[]{:S(2)}) copy-start(bf16[1,4,80,2048]{3,2,1,0:T(8,128)(2,1)} %param.6) | copy-start | bytes 3932164
  34.4 50.9 %all-to-all-start.1 = ((bf16[8,320,224]{2,1,0:T(8,128)(2,1)}), bf16[8,320,224]{2,1,0:T(8,128)(2,1)S(1)}, u32[]{:S(2)}, u32[]{:S(2)}) async-start(bf16[8,320,224]{2,1,0:T(8,128)(2,1)} %get-tuple-element.11), calls=%async_computation.1 | async-start | bytes 2621440 | tf_op jit(solution)/shard_map/all_to_all | solution.py:215
  41.1 8.2 %collective-permute-start.4 = (bf16[80,2048]{1,0:T(8,128)(2,1)S(1)}, bf16[80,2048]{1,0:T(8,128)(2,1)S(1)}, u32[]{:S(2)}, u32[]{:S(2)}) collective-permute-start(bf16[80,2048]{1,0:T(8,128)(2,1)S(1)} %multiply_reduce_fusion), channel_id=1, source_target_pairs={{0,24},{1,25},{2,26},{3,27},{4,28},{5,29},{6,30},{7,31},{32,56},{3... | collective-permute-start | bytes 983048 | tf_op jit(solution)/shard_map/ppermute | solution.py:205
  41.8 7.5 %collective-permute-start.5 = (bf16[80,2048]{1,0:T(8,128)(2,1)S(1)}, bf16[80,2048]{1,0:T(8,128)(2,1)S(1)}, u32[]{:S(2)}, u32[]{:S(2)}) collective-permute-start(bf16[80,2048]{1,0:T(8,128)(2,1)S(1)} %multiply_reduce_fusion), channel_id=1, source_target_pairs={{0,16},{8,24},{136,152},{1,17},{9,25},{137,153},{2,18},{10,26},{13... | collective-permute-start | bytes 983048 | tf_op jit(solution)/shard_map/ppermute | solution.py:205
  42.5 39.0 %collective-permute-start.6 = (bf16[80,2048]{1,0:T(8,128)(2,1)S(1)}, bf16[80,2048]{1,0:T(8,128)(2,1)S(1)}, u32[]{:S(2)}, u32[]{:S(2)}) collective-permute-start(bf16[80,2048]{1,0:T(8,128)(2,1)S(1)} %multiply_reduce_fusion), channel_id=1, source_target_pairs={{0,8},{8,16},{16,24},{136,144},{144,152},{272,280},{1,9},{9,17},{1... | collective-permute-start | bytes 983048 | tf_op jit(solution)/shard_map/ppermute | solution.py:205
  47.1 46.0 %collective-permute-start.7 = (bf16[256,640]{1,0:T(8,128)(2,1)S(1)}, bf16[256,640]{1,0:T(8,128)(2,1)S(1)}, u32[]{:S(2)}, u32[]{:S(2)}) collective-permute-start(bf16[256,640]{1,0:T(8,128)(2,1)S(1)} %bitcast.23), channel_id=1, source_target_pairs={{0,2},{2,0},{4,6},{6,4},{1,3},{3,1},{5,7},{7,5},{8,10},{10,8},{12,... | collective-permute-start | bytes 983048 | tf_op jit(solution)/shard_map/ppermute | solution.py:179
  49.3 32.1 %copy-start.7 = (bf16[80,2048]{1,0:T(8,128)(2,1)}, bf16[80,2048]{1,0:T(8,128)(2,1)S(1)}, u32[]{:S(2)}) copy-start(bf16[80,2048]{1,0:T(8,128)(2,1)S(1)} %collective-permute-done.4.refs_0_) | copy-start | bytes 983044
  49.4 32.1 %copy-start.8 = (bf16[80,2048]{1,0:T(8,128)(2,1)}, bf16[80,2048]{1,0:T(8,128)(2,1)S(1)}, u32[]{:S(2)}) copy-start(bf16[80,2048]{1,0:T(8,128)(2,1)S(1)} %collective-permute-done.5.refs_1_) | copy-start | bytes 983044
  86.4 24.4 %all-to-all-start.3 = ((bf16[4,80,2048]{2,1,0:T(8,128)(2,1)}), bf16[4,80,2048]{2,1,0:T(8,128)(2,1)S(1)}, u32[]{:S(2)}, u32[]{:S(2)}) async-start(bf16[4,80,2048]{2,1,0:T(8,128)(2,1)} %shard_map.49), calls=%async_computation.3 | async-start | bytes 2621440 | tf_op jit(solution)/shard_map/all_to_all | solution.py:220
  90.5 6.2 %collective-permute-start = (bf16[224,640]{1,0:T(8,128)(2,1)S(1)}, bf16[224,640]{1,0:T(8,128)(2,1)S(1)}, u32[]{:S(2)}, u32[]{:S(2)}) collective-permute-start(bf16[224,640]{1,0:T(8,128)(2,1)S(1)} %copy-done.10), channel_id=1, source_target_pairs={{408,24},{409,25},{410,26},{411,27},{412,28},{413,29},{414,30},{41... | collective-permute-start | bytes 860168 | tf_op jit(solution)/shard_map/ppermute | solution.py:211
  91.2 5.5 %collective-permute-start.1 = (bf16[224,640]{1,0:T(8,128)(2,1)S(1)}, bf16[224,640]{1,0:T(8,128)(2,1)S(1)}, u32[]{:S(2)}, u32[]{:S(2)}) collective-permute-start(bf16[224,640]{1,0:T(8,128)(2,1)S(1)} %copy-done.10), channel_id=1, source_target_pairs={{272,16},{408,152},{273,17},{409,153},{274,18},{410,154},{275,19},... | collective-permute-start | bytes 860168 | tf_op jit(solution)/shard_map/ppermute | solution.py:211
  91.8 9.5 %collective-permute-start.2 = (bf16[224,640]{1,0:T(8,128)(2,1)S(1)}, bf16[224,640]{1,0:T(8,128)(2,1)S(1)}, u32[]{:S(2)}, u32[]{:S(2)}) collective-permute-start(bf16[224,640]{1,0:T(8,128)(2,1)S(1)} %copy-done.10), channel_id=1, source_target_pairs={{136,8},{272,144},{408,280},{137,9},{273,145},{409,281},{138,10},{... | collective-permute-start | bytes 860168 | tf_op jit(solution)/shard_map/ppermute | solution.py:211
  93.2 8.3 %copy-start.4 = (bf16[256,640]{1,0:T(8,128)(2,1)}, bf16[256,640]{1,0:T(8,128)(2,1)S(1)}, u32[]{:S(2)}) copy-start(bf16[256,640]{1,0:T(8,128)(2,1)S(1)} %collective-permute-done.7) | copy-start | bytes 983044
  94.1 22.7 %collective-permute-start.8 = (bf16[2,256,640]{2,1,0:T(8,128)(2,1)}, bf16[2,256,640]{2,1,0:T(8,128)(2,1)}, u32[]{:S(2)}, u32[]{:S(2)}) collective-permute-start(bf16[2,256,640]{2,1,0:T(8,128)(2,1)} %pad_maximum_fusion.1.near_ref), channel_id=1, source_target_pairs={{0,4},{2,6},{4,0},{6,2},{1,5},{3,7},{5,1},{7,3},{8,12},{10,14},{12... | collective-permute-start | bytes 1966088 | tf_op jit(solution)/shard_map/ppermute | solution.py:180
  101.4 4.7 %collective-permute-start.3 = (bf16[224,640]{1,0:T(8,128)(2,1)S(1)}, bf16[224,640]{1,0:T(8,128)(2,1)S(1)}, u32[]{:S(2)}, u32[]{:S(2)}) collective-permute-start(bf16[224,640]{1,0:T(8,128)(2,1)S(1)} %add_select_fusion.own_ref), channel_id=1, source_target_pairs={{0,1},{1,0},{2,3},{3,2},{4,5},{5,4},{6,7},{7,6},{8,9},{9,8},{10,11... | collective-permute-start | bytes 860168 | tf_op jit(solution)/shard_map/ppermute | solution.py:213
  111.8 27.9 %all-to-all-start.2 = ((bf16[16,80,640]{2,1,0:T(8,128)(2,1)}), bf16[16,80,640]{2,1,0:T(8,128)(2,1)S(1)}, u32[]{:S(2)}, u32[]{:S(2)}) async-start(bf16[16,80,640]{2,1,0:T(8,128)(2,1)} %bitcast.20), calls=%async_computation.2 | async-start | bytes 3276800 | tf_op jit(solution)/shard_map/all_to_all | solution.py:217
  118.1 5.2 %collective-permute-start.9 = (bf16[4,256,640]{2,1,0:T(8,128)(2,1)S(1)}, bf16[4,256,640]{2,1,0:T(8,128)(2,1)S(1)}, u32[]{:S(2)}, u32[]{:S(2)}) collective-permute-start(bf16[4,256,640]{2,1,0:T(8,128)(2,1)S(1)} %pad_maximum_fusion), channel_id=1, source_target_pairs={{0,1},{1,0},{2,3},{3,2},{4,5},{5,4},{6,7},{7,6},{8,9},{9,8},{10,11... | collective-permute-start | bytes 3932168 | tf_op jit(solution)/shard_map/ppermute | solution.py:181
  128.8 11.7 %collective-permute-start.10 = (f32[80,640]{1,0:T(8,128)}, f32[80,640]{1,0:T(8,128)S(1)}, u32[]{:S(2)}, u32[]{:S(2)}) collective-permute-start(f32[80,640]{1,0:T(8,128)} %get-tuple-element.14), channel_id=1, source_target_pairs={{0,96},{32,0},{64,32},{96,64},{1,97},{33,1},{65,33},{97,65},{2,98}... | collective-permute-start | bytes 614408 | tf_op jit(solution)/shard_map/ppermute | solution.py:222
  133.5 9.6 %collective-permute-start.11 = (f32[80,640]{1,0:T(8,128)}, f32[80,640]{1,0:T(8,128)S(1)}, u32[]{:S(2)}, u32[]{:S(2)}) collective-permute-start(f32[80,640]{1,0:T(8,128)} %get-tuple-element.15), channel_id=1, source_target_pairs={{0,64},{32,96},{64,0},{96,32},{1,65},{33,97},{65,1},{97,33},{2,66}... | collective-permute-start | bytes 614408 | tf_op jit(solution)/shard_map/ppermute | solution.py:222
  136.0 12.4 %collective-permute-start.12 = (f32[80,640]{1,0:T(8,128)}, f32[80,640]{1,0:T(8,128)S(1)}, u32[]{:S(2)}, u32[]{:S(2)}) collective-permute-start(f32[80,640]{1,0:T(8,128)} %get-tuple-element.16), channel_id=1, source_target_pairs={{0,32},{32,64},{64,96},{96,0},{1,33},{33,65},{65,97},{97,1},{2,34}... | collective-permute-start | bytes 614408 | tf_op jit(solution)/shard_map/ppermute | solution.py:222
  139.7 8.8 %copy-start = (bf16[16,80,640]{2,1,0:T(8,128)(2,1)}, bf16[16,80,640]{2,1,0:T(8,128)(2,1)S(1)}, u32[]{:S(2)}) copy-start(bf16[16,80,640]{2,1,0:T(8,128)(2,1)S(1)} %all-to-all-done.2) | copy-start | bytes 4915204
  140.5 8.0 %copy-start.12 = (f32[80,640]{1,0:T(8,128)}, f32[80,640]{1,0:T(8,128)S(1)}, u32[]{:S(2)}) copy-start(f32[80,640]{1,0:T(8,128)S(1)} %collective-permute-done.10.refs_1_) | copy-start | bytes 614404
  (9 other events, 20.7 us)

commit v4 on v2

v4 whole, which is shorter than its diff:
```python
import functools

import jax
import jax.numpy as jnp
from jax import lax
from jax.experimental import pallas as pl
from jax.experimental.pallas import tpu as pltpu
from jax.sharding import Mesh, PartitionSpec as P

ZLO, X, TGT, Y, CORE = 4, 4, 4, 4, 2
FEAT = ("y", "core")


def total_pairs(k):
    return [(z * TGT + b, z * TGT + b + k) for z in range(ZLO) for b in range(z, TGT - k)]


def window_pairs(k):
    return [(b * TGT + b, (b - k) * TGT + b) for b in range(k, TGT)]


def split_kernel(wide_ref, out_ref):
    tokens = out_ref.shape[2]
    for f in range(out_ref.shape[0]):
        out_ref[f] = wide_ref[:, f * tokens : (f + 1) * tokens]


def select_kernel(ids_ref, sliced_ref, columns_ref, pieces_ref):
    feats, tokens = sliced_ref.shape
    width = ids_ref.shape[1]
    step = 128
    wide = jnp.broadcast_to(ids_ref[pl.ds(lax.axis_index("zlo") * X + lax.axis_index("x"), 1), :], (step, width))
    columns = jnp.zeros((tokens, width), jnp.float32)
    for g in range(feats // step):
        part = sliced_ref[g * step : (g + 1) * step]
        chosen = (wide == g * step + lax.broadcasted_iota(jnp.int32, wide.shape, 0)).astype(jnp.bfloat16)
        columns += lax.dot_general(part, chosen, (((0,), (0,)), ((), ())), preferred_element_type=jnp.float32)
    columns_ref[...] = columns.astype(columns_ref.dtype)
    rows = columns.T.astype(pieces_ref.dtype)
    height = width // (Y * CORE)
    for y in range(Y):
        for c in range(CORE):
            f = y * CORE + c
            for x in range(X):
                pieces_ref[x * CORE + c, y * height : (y + 1) * height] = rows[f * height : (f + 1) * height]


def prefix_kernel(*refs):
    total_refs, decoders_ref, out_refs = refs[: TGT - 1], refs[TGT - 1], refs[TGT:]
    layers = decoders_ref.shape[0]
    x = lax.axis_index("x")
    first = lax.axis_index("zlo") * X + x - lax.axis_index("tgt") * layers
    base = total_refs[0][...].astype(jnp.float32)
    for ref in total_refs[1:]:
        base += ref[...].astype(jnp.float32)
    written = [decoders_ref[k].astype(jnp.float32) for k in range(layers - 1)]
    for r in range(X):
        layer = (x + r) % X
        out = base
        for k in range(layers - 1):
            counts = jnp.logical_and(k < layer, k >= first)
            out += written[k] * jnp.where(counts, 1.0, 0.0)
        out_refs[r][...] = out.astype(jnp.bfloat16)


def virtual_kernel(*refs):
    prefix_refs, own_refs, other_ref, out_refs, rows_ref = refs[:X], refs[X : X + Y], refs[X + Y], refs[X + Y + 1 : -1], refs[-1]
    groups, slices, depth, width = rows_ref.shape
    y, core = lax.axis_index("y"), lax.axis_index("core")
    for r in range(Y):
        row = (y + Y - r) % Y
        rows_ref[:, row * CORE + core] = own_refs[r][...].reshape(groups, depth, width)
        rows_ref[:, row * CORE + 1 - core] = other_ref[r].reshape(groups, depth, width)
    height = prefix_refs[0].shape[0]
    chunk = slices * depth
    total = jnp.zeros((X * height, width), jnp.float32)
    for g in range(0, groups, 2):
        left = jnp.concatenate([ref[:, g * chunk : (g + 2) * chunk] for ref in prefix_refs], 0)
        right = rows_ref[g : g + 2].reshape(2 * chunk, width)
        total += jnp.dot(left, right, preferred_element_type=jnp.float32)
    for r in range(X):
        out_refs[r][...] = total[r * height : (r + 1) * height]


def gram_kernel(window_ref, own_ref, other_ref, out_ref):
    core = lax.axis_index("core")
    part = jnp.dot(window_ref[0, core], own_ref[...], preferred_element_type=jnp.float32)
    part += jnp.dot(window_ref[0, 1 - core], other_ref[...], preferred_element_type=jnp.float32)
    out_ref[0] = part.astype(out_ref.dtype)


def weigh_kernel(scale, gram_ref, *refs):
    virtual_refs, out_ref = refs[:-1], refs[-1]
    gram = gram_ref[0, 0].astype(jnp.float32)
    for row in range(1, Y):
        gram += gram_ref[0, row].astype(jnp.float32)
    gram = gram * scale
    piece = (pl.program_id(0) + X - lax.axis_index("x")) % X
    for r in range(X):

        @pl.when(piece == r)
        def _(r=r):
            out_ref[0] = virtual_refs[r][...] * gram


VMEM = pl.BlockSpec(memory_space=pltpu.VMEM)


def split(wide, slices):
    feats, token_count = wide.shape
    return pl.pallas_call(
        split_kernel,
        out_shape=jax.ShapeDtypeStruct((slices, feats, token_count // slices), wide.dtype),
        in_specs=[VMEM],
        out_specs=VMEM,
    )(wide)


def select(window_ids, sliced):
    tokens, width = sliced.shape[1], window_ids.shape[1]
    return pl.pallas_call(
        select_kernel,
        out_shape=(
            jax.ShapeDtypeStruct((tokens, width), jnp.bfloat16),
            jax.ShapeDtypeStruct((X * CORE, width // CORE, tokens), jnp.bfloat16),
        ),
        in_specs=[VMEM, VMEM],
        out_specs=(VMEM, VMEM),
    )(window_ids, sliced)


def prefix_of(totals, decoders):
    layers, height, depth = decoders.shape
    step = 16
    rows = pl.BlockSpec((step, depth), lambda i: (i, 0))
    return pl.pallas_call(
        prefix_kernel,
        grid=(height // step,),
        out_shape=[jax.ShapeDtypeStruct((height, depth), jnp.bfloat16)] * X,
        in_specs=[rows] * len(totals) + [pl.BlockSpec((layers, step, depth), lambda i: (0, i, 0))],
        out_specs=[rows] * X,
    )(*totals, decoders)


def virtual_of(prefix, own, other):
    height, depth = prefix[0].shape
    width = other.shape[2]
    groups = ZLO * X
    return pl.pallas_call(
        virtual_kernel,
        out_shape=[jax.ShapeDtypeStruct((height, width), jnp.float32)] * X,
        in_specs=[VMEM] * (len(prefix) + len(own) + 1),
        out_specs=[VMEM] * X,
        scratch_shapes=[pltpu.VMEM((groups, Y * CORE, depth // (groups * Y * CORE), width), jnp.bfloat16)],
    )(*prefix, *own, other)


def gram_of(window, own, other):
    sources, halves, height, tokens = window.shape
    width = own.shape[1]
    return pl.pallas_call(
        gram_kernel,
        grid=(sources,),
        out_shape=jax.ShapeDtypeStruct((sources, height, width), jnp.bfloat16),
        in_specs=[pl.BlockSpec((1, halves, height, tokens), lambda q: (q, 0, 0, 0)), VMEM, VMEM],
        out_specs=pl.BlockSpec((1, height, width), lambda q: (q, 0, 0)),
    )(window, own, other)


def weigh(gram, virtual, token_count):
    layers, rows, height, width = gram.shape
    return pl.pallas_call(
        functools.partial(weigh_kernel, 1.0 / token_count),
        grid=(layers,),
        out_shape=jax.ShapeDtypeStruct((layers, height, width), jnp.float32),
        in_specs=[pl.BlockSpec((1, rows, height, width), lambda k: (k, 0, 0, 0))] + [VMEM] * len(virtual),
        out_specs=pl.BlockSpec((1, height, width), lambda k: (k, 0, 0)),
    )(gram, *virtual)


def ring(n, k):
    return [(i, (i + k) % n) for i in range(n)]


def over_feat(piece):
    others = [lax.ppermute(piece, "y", ring(Y, k)) for k in range(1, Y)]
    own = [piece] + others
    return own, lax.ppermute(jnp.stack(own), "core", ring(CORE, 1))


def per_device(activations, window_ids, decoders, encoders):
    zlo = lax.axis_index("zlo")
    block = lax.axis_index("tgt")
    x = lax.axis_index("x")
    source = zlo * X + x
    token_count, local_feats = activations.shape[1:]
    targets, height = decoders.shape[1:3]
    fw = window_ids.shape[1]
    slices = Y * CORE
    tokens = token_count // slices

    spread = jnp.broadcast_to(encoders[None], (ZLO,) + encoders.shape).reshape((ZLO * X,) + encoders.shape[1:])
    encoder_rows = lax.all_to_all(spread, ("zlo", "x"), 0, 0, tiled=True).reshape(-1, fw)
    encoder_own, encoder_other = over_feat(encoder_rows)

    live = (block * targets + jnp.arange(targets) >= source).astype(jnp.float32)
    total = jnp.sum(decoders[0].astype(jnp.float32) * live[:, None, None], 0).astype(jnp.bfloat16)
    earlier = [lax.ppermute(total, ("zlo", "tgt"), total_pairs(k)) for k in (3, 2, 1)]

    by_tokens = split(activations[0].T, slices)
    sliced = lax.all_to_all(by_tokens, FEAT, 0, 0, tiled=True).reshape(slices * local_feats, tokens)
    columns, pieces = select(window_ids, sliced)

    parts = [lax.ppermute(columns, ("zlo", "tgt"), window_pairs(k)) for k in (3, 2, 1)]
    target = jnp.where(zlo == block, columns, parts[0] + parts[1] + parts[2])
    swapped = lax.ppermute(target, "core", ring(CORE, 1))

    window = lax.all_to_all(pieces, ("x", "core"), 0, 0, tiled=True).reshape(X, CORE, Y * height, tokens)
    partial = gram_of(window, target, swapped).reshape(X * Y, height, fw)
    partial = lax.all_to_all(partial, ("x", "y"), 0, 0, tiled=True).reshape(X, Y, height, fw)

    pieces = prefix_of(earlier, decoders[0])
    moved = [lax.ppermute(pieces[k], "x", ring(X, k)) for k in range(1, X)]
    virtual = virtual_of([pieces[0]] + moved, encoder_own, encoder_other)
    virtual = [virtual[0]] + [lax.ppermute(virtual[k], "x", ring(X, X - k)) for k in range(1, X)]
    return weigh(partial, virtual, token_count)[None]


def solution(mesh):
    fine = Mesh(mesh.devices.reshape(ZLO, X, TGT, Y, CORE), ("zlo", "x", "tgt", "y", "core"))
    src = ("zlo", "x")
    in_specs = (
        P(src, None, FEAT),
        P(),
        P(src, "tgt", FEAT, None),
        P("tgt", src + FEAT, None),
    )
    out_specs = P(src, "tgt", FEAT, None)

    return jax.shard_map(per_device, mesh=fine, in_specs=in_specs, out_specs=out_specs, check_vma=False)
```

time: 172 us -> 178 us (1.035)
  blocking collectives: 0 us -> 15.3 us
  waiting for transfers between devices: 74.2 us -> 66.4 us
  starting transfers between devices: 67.5 us -> 62.6 us
    all_to_all x0 -> x1, blocking collectives: none -> 15.3 us  [per_device(): lax.all_to_all(by_tokens, FEAT, 0, 0, tiled=True)]
    all_to_all x1 -> x0, waiting for transfers between devices: 8.59 us -> none  [per_device(): lax.all_to_all(by_tokens, FEAT, 0, 0, tiled=True)]
    all_to_all x1 -> x0, starting transfers between devices: 4.92 us -> none  [per_device(): lax.all_to_all(by_tokens, FEAT, 0, 0, tiled=True)]
    pallas_call x4 -> x3, Pallas kernels: 11.7 us -> 12.8 us  [the longest x1 4.51 us: gram_of(): pl.pallas_call(gram_kernel, grid=(sources,), out_shape=jax.ShapeDtypeStru...]
  transfers between devices with their start and end apart: 21 -> 20, of which waited for: 11 -> 10; matrix products, arithmetic and copies ran while one was open for 2% -> 2% of each run, Pallas kernels for 10% -> 9%
where the time goes in v4:
time: 178 us; the launch traced here: 177 us
  waiting for transfers between devices  66.4 us (37%)
  starting transfers between devices  62.6 us (35%)
  Pallas kernels  22.6 us (13%)
  blocking collectives  15.3 us (9%)
  local copies, waits for them, and re-layouts  5.69 us (3%)
  other arithmetic  3.99 us (2%)
    ppermute x3, waiting for transfers between devices, per_device(): lax.ppermute(total, ('zlo', 'tgt'), total_pairs(k))  31.9 us
    all_to_all x1, blocking collectives, per_device(): lax.all_to_all(by_tokens, FEAT, 0, 0, tiled=True)  15.3 us
    ppermute x3, starting transfers between devices, per_device(): moved = [lax.ppermute(pieces[k], 'x', ring(X, k)) for k in range(1, X)]  11.3 us
    ppermute x3, waiting for transfers between devices, per_device(): moved = [lax.ppermute(pieces[k], 'x', ring(X, k)) for k in range(1, X)]  11.2 us
    ppermute x3, starting transfers between devices, per_device(): lax.ppermute(virtual[k], 'x', ring(X, X - k))  10.1 us
    ppermute x3, starting transfers between devices, over_feat(): others = [lax.ppermute(piece, 'y', ring(Y, k)) for k in range(1, Y)]  9.82 us
    ppermute x3, waiting for transfers between devices, per_device(): lax.ppermute(virtual[k], 'x', ring(X, X - k))  9.09 us
    ppermute x3, starting transfers between devices, per_device(): lax.ppermute(total, ('zlo', 'tgt'), total_pairs(k))  7.94 us
  transfers between devices with their start and end apart: 20, of which 10 were waited for; matrix products, arithmetic and copies ran while one was open for 2% of the time, Pallas kernels for 9%

profile of v4, /device:TPU:296, one launch (start us, length us, event | category | flops | bytes accessed | tf_op | source)
XLA Modules:
  0.0 176.9 jit_solution(15249012112007506554)
XLA Ops:
  2.2 15.3 %all_to_all.20 = bf16[8,160,224]{2,1,0:T(8,128)(2,1)} all-to-all(bf16[8,160,224]{2,1,0:T(8,128)(2,1)} %shard_map.46), channel_id=1, replica_groups=mesh['zlo'=4,'x'=4,'tgt'=4,'y'=4,'core'=2] {'y','core'}, dimensions={0} | all-to-all | bytes 1146880 | tf_op jit(solution)/shard_map/all_to_all | solution.py:211
  18.3 6.7 %all-to-all-start.3 = ((bf16[16,16,640]{2,1,0:T(8,128)(2,1)}), bf16[16,16,640]{2,1,0:T(8,128)(2,1)S(1)}, u32[]{:S(2)}, u32[]{:S(2)}) async-start(bf16[16,16,640]{2,1,0:T(8,128)(2,1)} %bitcast.7), calls=%async_computation.3 | async-start | bytes 655360 | tf_op jit(solution)/shard_map/all_to_all | solution.py:203
  25.0 3.3 %shard_map.47 = (bf16[224,640]{1,0:T(8,128)(2,1)}, bf16[8,320,224]{2,1,0:T(8,128)(2,1)}) custom-call(s32[16,640]{1,0:T(8,128)} %ids_ref.1, bf16[1280,224]{1,0:T(8,128)(2,1)} %bitcast.25), custom_call_target="tpu_custom_call" | custom-call | tf_op jit(solution)/shard_map/pallas_call | solution.py:121
  28.2 7.2 %all-to-all-done.3 = bf16[16,16,640]{2,1,0:T(8,128)(2,1)S(1)} async-done(((bf16[16,16,640]{2,1,0:T(8,128)(2,1)}), bf16[16,16,640]{2,1,0:T(8,128)(2,1)S(1)}, u32[]{:S(2)}, u32[]{:S(2)}) %all-to-all-start.3) | async-done | bytes 327712 | tf_op jit(solution)/shard_map/all_to_all | solution.py:203
  35.5 3.7 %all-to-all-start.1 = ((bf16[8,320,224]{2,1,0:T(8,128)(2,1)}), bf16[8,320,224]{2,1,0:T(8,128)(2,1)S(1)}, u32[]{:S(2)}, u32[]{:S(2)}) async-start(bf16[8,320,224]{2,1,0:T(8,128)(2,1)} %get-tuple-element.15), calls=%async_computation.1 | async-start | bytes 2621440 | tf_op jit(solution)/shard_map/all_to_all | solution.py:218
  44.1 5.1 %collective-permute-start.11 = (bf16[256,640]{1,0:T(8,128)(2,1)S(1)}, bf16[256,640]{1,0:T(8,128)(2,1)S(1)}, u32[]{:S(2)}, u32[]{:S(2)}) collective-permute-start(bf16[256,640]{1,0:T(8,128)(2,1)S(1)} %bitcast.21), channel_id=1, source_target_pairs={{0,4},{2,6},{4,0},{6,2},{1,5},{3,7},{5,1},{7,3},{8,12},{10,14},{12... | collective-permute-start | bytes 983048 | tf_op jit(solution)/shard_map/ppermute | solution.py:186
  49.3 2.5 %collective-permute-start.12 = (bf16[256,640]{1,0:T(8,128)(2,1)S(1)}, bf16[256,640]{1,0:T(8,128)(2,1)S(1)}, u32[]{:S(2)}, u32[]{:S(2)}) collective-permute-start(bf16[256,640]{1,0:T(8,128)(2,1)S(1)} %bitcast.22), channel_id=1, source_target_pairs={{0,6},{2,0},{4,2},{6,4},{1,7},{3,1},{5,3},{7,5},{8,14},{10,8},{12,... | collective-permute-start | bytes 983048 | tf_op jit(solution)/shard_map/ppermute | solution.py:186
  52.5 5.4 %collective-permute-done.2 = bf16[224,640]{1,0:T(8,128)(2,1)} collective-permute-done((bf16[224,640]{1,0:T(8,128)(2,1)S(1)}, bf16[224,640]{1,0:T(8,128)(2,1)}, u32[]{:S(2)}, u32[]{:S(2)}) %collective-permute-start.2) | collective-permute-done | bytes 286752 | tf_op jit(solution)/shard_map/ppermute | solution.py:214
  63.6 4.5 %shard_map.48 = bf16[4,320,640]{2,1,0:T(8,128)(2,1)} custom-call(bf16[4,2,320,224]{3,2,1,0:T(8,128)(2,1)} %bitcast.18, bf16[224,640]{1,0:T(8,128)(2,1)} %copy-done.7, bf16[224,640]{1,0:T(8,128)(2,1)} %copy-done.14), custom_call_target="tpu_custom_call" | custom-call | tf_op jit(solution)/shard_map/pallas_call | solution.py:161
  68.1 6.5 %all-to-all-start.2 = ((bf16[16,80,640]{2,1,0:T(8,128)(2,1)}), bf16[16,80,640]{2,1,0:T(8,128)(2,1)S(1)}, u32[]{:S(2)}, u32[]{:S(2)}) async-start(bf16[16,80,640]{2,1,0:T(8,128)(2,1)} %bitcast.17), calls=%async_computation.2 | async-start | bytes 3276800 | tf_op jit(solution)/shard_map/all_to_all | solution.py:220
  75.6 2.5 %pad_maximum_fusion = bf16[4,256,640]{2,1,0:T(8,128)(2,1)} fusion(bf16[1,256,640]{2,1,0:T(8,128)(2,1)} %bitcast.28, bf16[1,256,640]{2,1,0:T(8,128)(2,1)} %bitcast.27, bf16[1,256,640]{2,1,0:T(8,128)(2,1)} %bitcast.26, bf16[1,256,640]{2,1,0:T(8,128)(2,1)S(1)} %bitcast.23), kind=kLoop, calls=%fused_computation.1 | loop fusion | flops 1966080 | bytes 2621440 | tf_op jit(solution)/shard_map/stack | solution.py:188
  81.8 6.6 %collective-permute-start.6 = (bf16[80,2048]{1,0:T(8,128)(2,1)S(1)}, bf16[80,2048]{1,0:T(8,128)(2,1)S(1)}, u32[]{:S(2)}, u32[]{:S(2)}) collective-permute-start(bf16[80,2048]{1,0:T(8,128)(2,1)S(1)} %multiply_reduce_fusion), channel_id=1, source_target_pairs={{0,8},{8,16},{16,24},{136,144},{144,152},{272,280},{1,9},{9,17},{1... | collective-permute-start | bytes 983048 | tf_op jit(solution)/shard_map/ppermute | solution.py:208
  88.4 31.9 %collective-permute-done.6.refs_2_ = bf16[80,2048]{1,0:T(8,128)(2,1)S(1)} collective-permute-done((bf16[80,2048]{1,0:T(8,128)(2,1)S(1)}, bf16[80,2048]{1,0:T(8,128)(2,1)S(1)}, u32[]{:S(2)}, u32[]{:S(2)}) %collective-permute-start.6) | collective-permute-done | bytes 327712 | tf_op jit(solution)/shard_map/ppermute | solution.py:208
  121.1 4.4 %shard_map.49 = (bf16[80,2048]{1,0:T(8,128)(2,1)}, bf16[80,2048]{1,0:T(8,128)(2,1)}, bf16[80,2048]{1,0:T(8,128)(2,1)}, bf16[80,2048]{1,0:T(8,128)(2,1)}) custom-call(bf16[80,2048]{1,0:T(8,128)(2,1)} %copy-done.8, bf16[80,2048]{1,0:T(8,128)(2,1)} %copy-done.9, bf16[80,2048]{1,0:T(8,128)(2,1)} %copy-done.10, bf16[4,80,2048]{2,1,0:T(8,128)(2,1)} %bitcast.19), custom_call_target="tpu_custom_call" | custom-call | tf_op jit(solution)/shard_map/pallas_call | solution.py:136
  125.5 3.4 %collective-permute-start.7 = (bf16[80,2048]{1,0:T(8,128)(2,1)}, bf16[80,2048]{1,0:T(8,128)(2,1)S(1)}, u32[]{:S(2)}, u32[]{:S(2)}) collective-permute-start(bf16[80,2048]{1,0:T(8,128)(2,1)} %get-tuple-element.18), channel_id=1, source_target_pairs={{0,32},{32,64},{64,96},{96,0},{1,33},{33,65},{65,97},{97,1},{2,34}... | collective-permute-start | bytes 983048 | tf_op jit(solution)/shard_map/ppermute | solution.py:223
  128.9 4.6 %collective-permute-start.8 = (bf16[80,2048]{1,0:T(8,128)(2,1)}, bf16[80,2048]{1,0:T(8,128)(2,1)S(1)}, u32[]{:S(2)}, u32[]{:S(2)}) collective-permute-start(bf16[80,2048]{1,0:T(8,128)(2,1)} %get-tuple-element.19), channel_id=1, source_target_pairs={{0,64},{32,96},{64,0},{96,32},{1,65},{33,97},{65,1},{97,33},{2,66}... | collective-permute-start | bytes 983048 | tf_op jit(solution)/shard_map/ppermute | solution.py:223
  133.5 3.4 %collective-permute-start.9 = (bf16[80,2048]{1,0:T(8,128)(2,1)}, bf16[80,2048]{1,0:T(8,128)(2,1)S(1)}, u32[]{:S(2)}, u32[]{:S(2)}) collective-permute-start(bf16[80,2048]{1,0:T(8,128)(2,1)} %get-tuple-element.20), channel_id=1, source_target_pairs={{0,96},{32,0},{64,32},{96,64},{1,97},{33,1},{65,33},{97,65},{2,98}... | collective-permute-start | bytes 983048 | tf_op jit(solution)/shard_map/ppermute | solution.py:223
  138.5 7.9 %collective-permute-done.8.refs_2_ = bf16[80,2048]{1,0:T(8,128)(2,1)S(1)} collective-permute-done((bf16[80,2048]{1,0:T(8,128)(2,1)}, bf16[80,2048]{1,0:T(8,128)(2,1)S(1)}, u32[]{:S(2)}, u32[]{:S(2)}) %collective-permute-start.8) | collective-permute-done | bytes 327712 | tf_op jit(solution)/shard_map/ppermute | solution.py:223
  148.8 4.4 %shard_map.50 = (f32[80,640]{1,0:T(8,128)}, f32[80,640]{1,0:T(8,128)}, f32[80,640]{1,0:T(8,128)}, f32[80,640]{1,0:T(8,128)}) custom-call(bf16[80,2048]{1,0:T(8,128)(2,1)} %get-tuple-element.17.refs_0_, bf16[80,2048]{1,0:T(8,128)(2,1)} %copy-done.11, bf16[80,2048]{1,0:T(8,128)(2,1)} %copy-done.12, bf16[80,2048]{1,0:T(8,128)(2,1)} %copy-done.13, ...), custom_call_target="tpu_custom_call" | custom-call | tf_op jit(solution)/shard_map/pallas_call | solution.py:149
  153.2 4.5 %collective-permute-start.14 = (f32[80,640]{1,0:T(8,128)}, f32[80,640]{1,0:T(8,128)S(1)}, u32[]{:S(2)}, u32[]{:S(2)}) collective-permute-start(f32[80,640]{1,0:T(8,128)} %get-tuple-element.22), channel_id=1, source_target_pairs={{0,96},{32,0},{64,32},{96,64},{1,97},{33,1},{65,33},{97,65},{2,98}... | collective-permute-start | bytes 614408 | tf_op jit(solution)/shard_map/ppermute | solution.py:225
  157.7 3.7 %collective-permute-start.15 = (f32[80,640]{1,0:T(8,128)}, f32[80,640]{1,0:T(8,128)S(1)}, u32[]{:S(2)}, u32[]{:S(2)}) collective-permute-start(f32[80,640]{1,0:T(8,128)} %get-tuple-element.23), channel_id=1, source_target_pairs={{0,64},{32,96},{64,0},{96,32},{1,65},{33,97},{65,1},{97,33},{2,66}... | collective-permute-start | bytes 614408 | tf_op jit(solution)/shard_map/ppermute | solution.py:225
  163.3 3.6 %collective-permute-done.14.refs_1_ = f32[80,640]{1,0:T(8,128)S(1)} collective-permute-done((f32[80,640]{1,0:T(8,128)}, f32[80,640]{1,0:T(8,128)S(1)}, u32[]{:S(2)}, u32[]{:S(2)}) %collective-permute-start.14) | collective-permute-done | bytes 204832 | tf_op jit(solution)/shard_map/ppermute | solution.py:225
  169.3 3.2 %collective-permute-done.16.refs_3_ = f32[80,640]{1,0:T(8,128)S(1)} collective-permute-done((f32[80,640]{1,0:T(8,128)}, f32[80,640]{1,0:T(8,128)S(1)}, u32[]{:S(2)}, u32[]{:S(2)}) %collective-permute-start.16) | collective-permute-done | bytes 204832 | tf_op jit(solution)/shard_map/ppermute | solution.py:225
  173.1 3.8 %shard_map.51 = f32[4,80,640]{2,1,0:T(8,128)} custom-call(bf16[4,4,80,640]{3,2,1,0:T(8,128)(2,1)} %bitcast.16, f32[80,640]{1,0:T(8,128)} %get-tuple-element.21.refs_0_, f32[80,640]{1,0:T(8,128)} %copy-done.17, f32[80,640]{1,0:T(8,128)} %copy-done.18, f32[80,640]{1,0:T(8,128)} %copy-done.19), custom_call_target="tpu_custom_call" | custom-call | tf_op jit(solution)/shard_map/pallas_call | solution.py:172
  (70 shorter events, 28.5 us)
Async XLA Ops:
  0.0 17.5 %copy-start.20 = (bf16[4,16,640]{2,1,0:T(8,128)(2,1)S(1)}, bf16[4,16,640]{2,1,0:T(8,128)(2,1)}, u32[]{:S(2)}) copy-start(bf16[4,16,640]{2,1,0:T(8,128)(2,1)} %param.7) | copy-start | bytes 245764
  18.3 17.2 %all-to-all-start.3 = ((bf16[16,16,640]{2,1,0:T(8,128)(2,1)}), bf16[16,16,640]{2,1,0:T(8,128)(2,1)S(1)}, u32[]{:S(2)}, u32[]{:S(2)}) async-start(bf16[16,16,640]{2,1,0:T(8,128)(2,1)} %bitcast.7), calls=%async_computation.3 | async-start | bytes 655360 | tf_op jit(solution)/shard_map/all_to_all | solution.py:203
  35.5 40.1 %copy-start.3 = (bf16[16,16,640]{2,1,0:T(8,128)(2,1)}, bf16[16,16,640]{2,1,0:T(8,128)(2,1)S(1)}, u32[]{:S(2)}) copy-start(bf16[16,16,640]{2,1,0:T(8,128)(2,1)S(1)} %all-to-all-done.3) | copy-start | bytes 983044
  35.5 27.0 %all-to-all-start.1 = ((bf16[8,320,224]{2,1,0:T(8,128)(2,1)}), bf16[8,320,224]{2,1,0:T(8,128)(2,1)S(1)}, u32[]{:S(2)}, u32[]{:S(2)}) async-start(bf16[8,320,224]{2,1,0:T(8,128)(2,1)} %get-tuple-element.15), calls=%async_computation.1 | async-start | bytes 2621440 | tf_op jit(solution)/shard_map/all_to_all | solution.py:218
  39.2 10.0 %collective-permute-start = (bf16[224,640]{1,0:T(8,128)(2,1)S(1)}, bf16[224,640]{1,0:T(8,128)(2,1)S(1)}, u32[]{:S(2)}, u32[]{:S(2)}) collective-permute-start(bf16[224,640]{1,0:T(8,128)(2,1)S(1)} %copy-done.15), channel_id=1, source_target_pairs={{408,24},{409,25},{410,26},{411,27},{412,28},{413,29},{414,30},{41... | collective-permute-start | bytes 860168 | tf_op jit(solution)/shard_map/ppermute | solution.py:214
  39.9 11.8 %collective-permute-start.1 = (bf16[224,640]{1,0:T(8,128)(2,1)S(1)}, bf16[224,640]{1,0:T(8,128)(2,1)S(1)}, u32[]{:S(2)}, u32[]{:S(2)}) collective-permute-start(bf16[224,640]{1,0:T(8,128)(2,1)S(1)} %copy-done.15), channel_id=1, source_target_pairs={{272,16},{408,152},{273,17},{409,153},{274,18},{410,154},{275,19},... | collective-permute-start | bytes 860168 | tf_op jit(solution)/shard_map/ppermute | solution.py:214
  40.6 17.3 %collective-permute-start.2 = (bf16[224,640]{1,0:T(8,128)(2,1)S(1)}, bf16[224,640]{1,0:T(8,128)(2,1)}, u32[]{:S(2)}, u32[]{:S(2)}) collective-permute-start(bf16[224,640]{1,0:T(8,128)(2,1)S(1)} %copy-done.15), channel_id=1, source_target_pairs={{136,8},{272,144},{408,280},{137,9},{273,145},{409,281},{138,10},{... | collective-permute-start | bytes 860168 | tf_op jit(solution)/shard_map/ppermute | solution.py:214
  41.9 32.7 %collective-permute-start.10 = (bf16[256,640]{1,0:T(8,128)(2,1)S(1)}, bf16[256,640]{1,0:T(8,128)(2,1)S(1)}, u32[]{:S(2)}, u32[]{:S(2)}) collective-permute-start(bf16[256,640]{1,0:T(8,128)(2,1)S(1)} %bitcast.20), channel_id=1, source_target_pairs={{0,2},{2,4},{4,6},{6,0},{1,3},{3,5},{5,7},{7,1},{8,10},{10,12},{12... | collective-permute-start | bytes 983048 | tf_op jit(solution)/shard_map/ppermute | solution.py:186
  44.1 30.5 %collective-permute-start.11 = (bf16[256,640]{1,0:T(8,128)(2,1)S(1)}, bf16[256,640]{1,0:T(8,128)(2,1)S(1)}, u32[]{:S(2)}, u32[]{:S(2)}) collective-permute-start(bf16[256,640]{1,0:T(8,128)(2,1)S(1)} %bitcast.21), channel_id=1, source_target_pairs={{0,4},{2,6},{4,0},{6,2},{1,5},{3,7},{5,1},{7,3},{8,12},{10,14},{12... | collective-permute-start | bytes 983048 | tf_op jit(solution)/shard_map/ppermute | solution.py:186
  49.3 25.4 %collective-permute-start.12 = (bf16[256,640]{1,0:T(8,128)(2,1)S(1)}, bf16[256,640]{1,0:T(8,128)(2,1)S(1)}, u32[]{:S(2)}, u32[]{:S(2)}) collective-permute-start(bf16[256,640]{1,0:T(8,128)(2,1)S(1)} %bitcast.22), channel_id=1, source_target_pairs={{0,6},{2,0},{4,2},{6,4},{1,7},{3,1},{5,3},{7,5},{8,14},{10,8},{12,... | collective-permute-start | bytes 983048 | tf_op jit(solution)/shard_map/ppermute | solution.py:186
  59.0 3.5 %collective-permute-start.3 = (bf16[224,640]{1,0:T(8,128)(2,1)S(1)}, bf16[224,640]{1,0:T(8,128)(2,1)S(1)}, u32[]{:S(2)}, u32[]{:S(2)}) collective-permute-start(bf16[224,640]{1,0:T(8,128)(2,1)S(1)} %add_select_fusion.own_ref), channel_id=1, source_target_pairs={{0,1},{1,0},{2,3},{3,2},{4,5},{5,4},{6,7},{7,6},{8,9},{9,8},{10,11... | collective-permute-start | bytes 860168 | tf_op jit(solution)/shard_map/ppermute | solution.py:216
  68.1 95.2 %all-to-all-start.2 = ((bf16[16,80,640]{2,1,0:T(8,128)(2,1)}), bf16[16,80,640]{2,1,0:T(8,128)(2,1)S(1)}, u32[]{:S(2)}, u32[]{:S(2)}) async-start(bf16[16,80,640]{2,1,0:T(8,128)(2,1)} %bitcast.17), calls=%async_computation.2 | async-start | bytes 3276800 | tf_op jit(solution)/shard_map/all_to_all | solution.py:220
  78.2 69.9 %collective-permute-start.13 = (bf16[4,256,640]{2,1,0:T(8,128)(2,1)}, bf16[4,256,640]{2,1,0:T(8,128)(2,1)}, u32[]{:S(2)}, u32[]{:S(2)}) collective-permute-start(bf16[4,256,640]{2,1,0:T(8,128)(2,1)} %pad_maximum_fusion), channel_id=1, source_target_pairs={{0,1},{1,0},{2,3},{3,2},{4,5},{5,4},{6,7},{7,6},{8,9},{9,8},{10,11... | collective-permute-start | bytes 3932168 | tf_op jit(solution)/shard_map/ppermute | solution.py:188
  80.4 8.0 %collective-permute-start.4 = (bf16[80,2048]{1,0:T(8,128)(2,1)S(1)}, bf16[80,2048]{1,0:T(8,128)(2,1)S(1)}, u32[]{:S(2)}, u32[]{:S(2)}) collective-permute-start(bf16[80,2048]{1,0:T(8,128)(2,1)S(1)} %multiply_reduce_fusion), channel_id=1, source_target_pairs={{0,24},{1,25},{2,26},{3,27},{4,28},{5,29},{6,30},{7,31},{32,56},{3... | collective-permute-start | bytes 983048 | tf_op jit(solution)/shard_map/ppermute | solution.py:208
  81.1 7.3 %collective-permute-start.5 = (bf16[80,2048]{1,0:T(8,128)(2,1)S(1)}, bf16[80,2048]{1,0:T(8,128)(2,1)S(1)}, u32[]{:S(2)}, u32[]{:S(2)}) collective-permute-start(bf16[80,2048]{1,0:T(8,128)(2,1)S(1)} %multiply_reduce_fusion), channel_id=1, source_target_pairs={{0,16},{8,24},{136,152},{1,17},{9,25},{137,153},{2,18},{10,26},{13... | collective-permute-start | bytes 983048 | tf_op jit(solution)/shard_map/ppermute | solution.py:208
  81.8 38.5 %collective-permute-start.6 = (bf16[80,2048]{1,0:T(8,128)(2,1)S(1)}, bf16[80,2048]{1,0:T(8,128)(2,1)S(1)}, u32[]{:S(2)}, u32[]{:S(2)}) collective-permute-start(bf16[80,2048]{1,0:T(8,128)(2,1)S(1)} %multiply_reduce_fusion), channel_id=1, source_target_pairs={{0,8},{8,16},{16,24},{136,144},{144,152},{272,280},{1,9},{9,17},{1... | collective-permute-start | bytes 983048 | tf_op jit(solution)/shard_map/ppermute | solution.py:208
  88.4 31.9 %copy-start.8 = (bf16[80,2048]{1,0:T(8,128)(2,1)}, bf16[80,2048]{1,0:T(8,128)(2,1)S(1)}, u32[]{:S(2)}) copy-start(bf16[80,2048]{1,0:T(8,128)(2,1)S(1)} %collective-permute-done.4.refs_0_) | copy-start | bytes 983044
  88.4 31.9 %copy-start.9 = (bf16[80,2048]{1,0:T(8,128)(2,1)}, bf16[80,2048]{1,0:T(8,128)(2,1)S(1)}, u32[]{:S(2)}) copy-start(bf16[80,2048]{1,0:T(8,128)(2,1)S(1)} %collective-permute-done.5.refs_1_) | copy-start | bytes 983044
  125.5 13.0 %collective-permute-start.7 = (bf16[80,2048]{1,0:T(8,128)(2,1)}, bf16[80,2048]{1,0:T(8,128)(2,1)S(1)}, u32[]{:S(2)}, u32[]{:S(2)}) collective-permute-start(bf16[80,2048]{1,0:T(8,128)(2,1)} %get-tuple-element.18), channel_id=1, source_target_pairs={{0,32},{32,64},{64,96},{96,0},{1,33},{33,65},{65,97},{97,1},{2,34}... | collective-permute-start | bytes 983048 | tf_op jit(solution)/shard_map/ppermute | solution.py:223
  128.9 17.5 %collective-permute-start.8 = (bf16[80,2048]{1,0:T(8,128)(2,1)}, bf16[80,2048]{1,0:T(8,128)(2,1)S(1)}, u32[]{:S(2)}, u32[]{:S(2)}) collective-permute-start(bf16[80,2048]{1,0:T(8,128)(2,1)} %get-tuple-element.19), channel_id=1, source_target_pairs={{0,64},{32,96},{64,0},{96,32},{1,65},{33,97},{65,1},{97,33},{2,66}... | collective-permute-start | bytes 983048 | tf_op jit(solution)/shard_map/ppermute | solution.py:223
  133.5 14.6 %collective-permute-start.9 = (bf16[80,2048]{1,0:T(8,128)(2,1)}, bf16[80,2048]{1,0:T(8,128)(2,1)S(1)}, u32[]{:S(2)}, u32[]{:S(2)}) collective-permute-start(bf16[80,2048]{1,0:T(8,128)(2,1)} %get-tuple-element.20), channel_id=1, source_target_pairs={{0,96},{32,0},{64,32},{96,64},{1,97},{33,1},{65,33},{97,65},{2,98}... | collective-permute-start | bytes 983048 | tf_op jit(solution)/shard_map/ppermute | solution.py:223
  153.2 13.8 %collective-permute-start.14 = (f32[80,640]{1,0:T(8,128)}, f32[80,640]{1,0:T(8,128)S(1)}, u32[]{:S(2)}, u32[]{:S(2)}) collective-permute-start(f32[80,640]{1,0:T(8,128)} %get-tuple-element.22), channel_id=1, source_target_pairs={{0,96},{32,0},{64,32},{96,64},{1,97},{33,1},{65,33},{97,65},{2,98}... | collective-permute-start | bytes 614408 | tf_op jit(solution)/shard_map/ppermute | solution.py:225
  157.7 11.6 %collective-permute-start.15 = (f32[80,640]{1,0:T(8,128)}, f32[80,640]{1,0:T(8,128)S(1)}, u32[]{:S(2)}, u32[]{:S(2)}) collective-permute-start(f32[80,640]{1,0:T(8,128)} %get-tuple-element.23), channel_id=1, source_target_pairs={{0,64},{32,96},{64,0},{96,32},{1,65},{33,97},{65,1},{97,33},{2,66}... | collective-permute-start | bytes 614408 | tf_op jit(solution)/shard_map/ppermute | solution.py:225
  161.4 11.0 %collective-permute-start.16 = (f32[80,640]{1,0:T(8,128)}, f32[80,640]{1,0:T(8,128)S(1)}, u32[]{:S(2)}, u32[]{:S(2)}) collective-permute-start(f32[80,640]{1,0:T(8,128)} %get-tuple-element.24), channel_id=1, source_target_pairs={{0,32},{32,64},{64,96},{96,0},{1,33},{33,65},{65,97},{97,1},{2,34}... | collective-permute-start | bytes 614408 | tf_op jit(solution)/shard_map/ppermute | solution.py:225
  (17 other events, 47.9 us)

commit v5 on v2

--- a/solution.py
+++ b/solution.py
@@ -25,11 +25,11 @@
         out_ref[f] = wide_ref[:, f * tokens : (f + 1) * tokens]
 
 
-def select_kernel(place_ref, ids_ref, sliced_ref, columns_ref, pieces_ref):
+def select_kernel(ids_ref, sliced_ref, columns_ref, pieces_ref):
     feats, tokens = sliced_ref.shape
     width = ids_ref.shape[1]
     step = 128
-    wide = jnp.broadcast_to(ids_ref[pl.ds(place_ref[3], 1), :], (step, width))
+    wide = jnp.broadcast_to(ids_ref[pl.ds(lax.axis_index("zlo") * X + lax.axis_index("x"), 1), :], (step, width))
     columns = jnp.zeros((tokens, width), jnp.float32)
     for g in range(feats // step):
         part = sliced_ref[g * step : (g + 1) * step]
@@ -50,10 +50,12 @@
         out_ref[z * X : (z + 1) * X] = rows_ref[...]
 
 
-def prefix_kernel(place_ref, *refs):
+def prefix_kernel(*refs):
     total_refs, decoders_ref, out_refs = refs[: TGT - 1], refs[TGT - 1], refs[TGT:]
     step = 16
     layers = decoders_ref.shape[0]
+    x = lax.axis_index("x")
+    first = lax.axis_index("zlo") * X + x - lax.axis_index("tgt") * layers
 
     def rows(i, carry):
         at = pl.ds(i * step, step)
@@ -62,10 +64,10 @@
             base += ref[at].astype(jnp.float32)
         written = [decoders_ref[k, at].astype(jnp.float32) for k in range(layers - 1)]
         for r in range(X):
-            layer = (place_ref[0] + r) % X
+            layer = (x + r) % X
             out = base
             for k in range(layers - 1):
-                counts = jnp.logical_and(k < layer, k >= place_ref[4])
+                counts = jnp.logical_and(k < layer, k >= first)
                 out += written[k] * jnp.where(counts, 1.0, 0.0)
             out_refs[r][at] = out.astype(jnp.bfloat16)
         return carry
@@ -73,12 +75,12 @@
     lax.fori_loop(0, decoders_ref.shape[1] // step, rows, 0)
 
 
-def virtual_kernel(place_ref, *refs):
+def virtual_kernel(*refs):
     prefix_refs, own_refs, other_ref, out_refs, rows_ref = refs[:X], refs[X : X + Y], refs[X + Y], refs[X + Y + 1 : -1], refs[-1]
     groups, slices, depth, width = rows_ref.shape
-    core = place_ref[2]
+    y, core = lax.axis_index("y"), lax.axis_index("core")
     for r in range(Y):
-        row = (place_ref[1] + Y - r) % Y
+        row = (y + Y - r) % Y
         rows_ref[:, row * CORE + core] = own_refs[r][...].reshape(groups, depth, width)
         rows_ref[:, row * CORE + 1 - core] = other_ref[r].reshape(groups, depth, width)
     height = prefix_refs[0].shape[0]
@@ -92,25 +94,24 @@
         out_refs[r][...] = total[r * height : (r + 1) * height]
 
 
-def gram_kernel(place_ref, window_ref, own_ref, other_ref, out_ref):
-    core = place_ref[2]
+def gram_kernel(window_ref, own_ref, other_ref, out_ref):
+    core = lax.axis_index("core")
     for q in range(window_ref.shape[0]):
         part = jnp.dot(window_ref[q, core], own_ref[...], preferred_element_type=jnp.float32)
         part += jnp.dot(window_ref[q, 1 - core], other_ref[...], preferred_element_type=jnp.float32)
         out_ref[q] = part.astype(out_ref.dtype)
 
 
-def weigh_kernel(scale, place_ref, gram_ref, *refs):
+def weigh_kernel(scale, gram_ref, *refs):
     virtual_refs, out_ref = refs[:-1], refs[-1]
     for r in range(X):
-        layer = (place_ref[0] + r) % X
+        layer = (lax.axis_index("x") + r) % X
         gram = gram_ref[layer, 0].astype(jnp.float32)
         for row in range(1, Y):
             gram += gram_ref[layer, row].astype(jnp.float32)
         out_ref[layer] = virtual_refs[r][...] * (gram * scale)
 
 
-SMEM = pl.BlockSpec(memory_space=pltpu.SMEM)
 VMEM = pl.BlockSpec(memory_space=pltpu.VMEM)
 
 
@@ -124,7 +125,7 @@
     )(wide)
 
 
-def select(place, window_ids, sliced):
+def select(window_ids, sliced):
     tokens, width = sliced.shape[1], window_ids.shape[1]
     return pl.pallas_call(
         select_kernel,
@@ -132,9 +133,9 @@
             jax.ShapeDtypeStruct((tokens, width), jnp.bfloat16),
             jax.ShapeDtypeStruct((X * CORE, width // CORE, tokens), jnp.bfloat16),
         ),
-        in_specs=[SMEM, VMEM, VMEM],
+        in_specs=[VMEM, VMEM],
         out_specs=(VMEM, VMEM),
-    )(place, window_ids, sliced)
+    )(window_ids, sliced)
 
 
 def spread_of(rows):
@@ -146,45 +147,45 @@
     )(rows)
 
 
-def prefix_of(place, totals, decoders):
+def prefix_of(totals, decoders):
     piece = jax.ShapeDtypeStruct(decoders.shape[1:], jnp.bfloat16)
     return pl.pallas_call(
         prefix_kernel,
         out_shape=[piece] * X,
-        in_specs=[SMEM] + [VMEM] * (len(totals) + 1),
+        in_specs=[VMEM] * (len(totals) + 1),
         out_specs=[VMEM] * X,
-    )(place, *totals, decoders)
-
-
-def virtual_of(place, prefix, own, other):
+    )(*totals, decoders)
+
+
+def virtual_of(prefix, own, other):
     height, depth = prefix[0].shape
     width = other.shape[2]
     groups = ZLO * X
     return pl.pallas_call(
         virtual_kernel,
         out_shape=[jax.ShapeDtypeStruct((height, width), jnp.float32)] * X,
-        in_specs=[SMEM] + [VMEM] * (len(prefix) + len(own) + 1),
+        in_specs=[VMEM] * (len(prefix) + len(own) + 1),
         out_specs=[VMEM] * X,
         scratch_shapes=[pltpu.VMEM((groups, Y * CORE, depth // (groups * Y * CORE), width), jnp.bfloat16)],
-    )(place, *prefix, *own, other)
-
-
-def gram_of(place, window, own, other):
+    )(*prefix, *own, other)
+
+
+def gram_of(window, own, other):
     return pl.pallas_call(
         gram_kernel,
         out_shape=jax.ShapeDtypeStruct((X, window.shape[2], own.shape[1]), jnp.bfloat16),
-        in_specs=[SMEM, VMEM, VMEM, VMEM],
-        out_specs=VMEM,
-    )(place, window, own, other)
-
-
-def weigh(place, gram, virtual, token_count):
+        in_specs=[VMEM, VMEM, VMEM],
+        out_specs=VMEM,
+    )(window, own, other)
+
+
+def weigh(gram, virtual, token_count):
     return pl.pallas_call(
         functools.partial(weigh_kernel, 1.0 / token_count),
         out_shape=jax.ShapeDtypeStruct((X,) + virtual[0].shape, jnp.float32),
-        in_specs=[SMEM, VMEM] + [VMEM] * len(virtual),
-        out_specs=VMEM,
-    )(place, gram, *virtual)
+        in_specs=[VMEM] + [VMEM] * len(virtual),
+        out_specs=VMEM,
+    )(gram, *virtual)
 
 
 def ring(n, k):
@@ -208,34 +209,32 @@
     slices = Y * CORE
     tokens = token_count // slices
 
-    place = [x, lax.axis_index("y"), lax.axis_index("core"), source, source - block * targets]
-    place = jnp.stack(place).astype(jnp.int32)
-
     spread = spread_of(encoders)
     encoder_rows = lax.all_to_all(spread, ("zlo", "x"), 0, 0, tiled=True).reshape(-1, fw)
     encoder_own, encoder_other = over_feat(encoder_rows)
 
     live = (block * targets + jnp.arange(targets) >= source).astype(jnp.float32)
     total = jnp.sum(decoders[0].astype(jnp.float32) * live[:, None, None], 0).astype(jnp.bfloat16)
-    earlier = [lax.ppermute(total, ("zlo", "tgt"), total_pairs(k)) for k in (3, 2, 1)]
+    earlier = [lax.ppermute(total, ("zlo", "tgt"), total_pairs(1))]
+    earlier += [lax.ppermute(total, ("zlo", "tgt"), total_pairs(k)) for k in (2, 3)]
 
     by_tokens = split(activations[0].T, slices)
     sliced = lax.all_to_all(by_tokens, FEAT, 0, 0, tiled=True).reshape(slices * local_feats, tokens)
-    columns, pieces = select(place, window_ids, sliced)
+    columns, pieces = select(window_ids, sliced)
 
     parts = [lax.ppermute(columns, ("zlo", "tgt"), window_pairs(k)) for k in (3, 2, 1)]
     target = jnp.where(zlo == block, columns, parts[0] + parts[1] + parts[2])
     swapped = lax.ppermute(target, "core", ring(CORE, 1))
 
     window = lax.all_to_all(pieces, ("x", "core"), 0, 0, tiled=True).reshape(X, CORE, Y * height, tokens)
-    partial = gram_of(place, window, target, swapped).reshape(X * Y, height, fw)
+    partial = gram_of(window, target, swapped).reshape(X * Y, height, fw)
     partial = lax.all_to_all(partial, ("x", "y"), 0, 0, tiled=True).reshape(X, Y, height, fw)
 
-    pieces = prefix_of(place, earlier, decoders[0])
+    pieces = prefix_of(earlier, decoders[0])
     moved = [lax.ppermute(pieces[k], "x", ring(X, k)) for k in range(1, X)]
-    virtual = virtual_of(place, [pieces[0]] + moved, encoder_own, encoder_other)
+    virtual = virtual_of([pieces[0]] + moved, encoder_own, encoder_other)
     virtual = [virtual[0]] + [lax.ppermute(virtual[k], "x", ring(X, X - k)) for k in range(1, X)]
-    return weigh(place, partial, virtual, token_count)[None]
+    return weigh(partial, virtual, token_count)[None]
 
 
 def solution(mesh):

time: 172 us -> 172 us (level)
  the two profiles are of different devices: /device:TPU:296 before, /device:TPU:456 now
where the time goes in v5:
time: 172 us; the launch traced here: 171 us
  waiting for transfers between devices  78.2 us (45%)
  starting transfers between devices  62 us (36%)
  Pallas kernels  21.5 us (12%)
  local copies, waits for them, and re-layouts  5.14 us (3%)
  other arithmetic  4 us (2%)
    ppermute x1, waiting for transfers between devices, per_device(): earlier = [lax.ppermute(total, ('zlo', 'tgt'), total_pairs(1))]  29.3 us
    ppermute x3, waiting for transfers between devices, per_device(): lax.ppermute(columns, ('zlo', 'tgt'), window_pairs(k))  11.8 us
    ppermute x3, starting transfers between devices, per_device(): moved = [lax.ppermute(pieces[k], 'x', ring(X, k)) for k in range(1, X)]  11.3 us
    ppermute x3, waiting for transfers between devices, per_device(): moved = [lax.ppermute(pieces[k], 'x', ring(X, k)) for k in range(1, X)]  11.2 us
    ppermute x3, starting transfers between devices, per_device(): lax.ppermute(virtual[k], 'x', ring(X, X - k))  10.1 us
    ppermute x3, starting transfers between devices, over_feat(): others = [lax.ppermute(piece, 'y', ring(Y, k)) for k in range(1, Y)]  9.21 us
    ppermute x3, waiting for transfers between devices, per_device(): lax.ppermute(virtual[k], 'x', ring(X, X - k))  9.09 us
    all_to_all x1, waiting for transfers between devices, per_device(): lax.all_to_all(by_tokens, FEAT, 0, 0, tiled=True)  8.59 us
  transfers between devices with their start and end apart: 21, of which 11 were waited for; matrix products, arithmetic and copies ran while one was open for 2% of the time, Pallas kernels for 10%

profile of v5, /device:TPU:456, one launch (start us, length us, event | category | flops | bytes accessed | tf_op | source)
XLA Modules:
  0.0 171.3 jit_solution(9822313762617318856)
XLA Ops:
  2.2 4.9 %all-to-all-start = ((bf16[8,160,224]{2,1,0:T(8,128)(2,1)}), bf16[8,160,224]{2,1,0:T(8,128)(2,1)S(1)}, u32[]{:S(2)}, u32[]{:S(2)}) async-start(bf16[8,160,224]{2,1,0:T(8,128)(2,1)} %shard_map.46), calls=%async_computation | async-start | bytes 1310720 | tf_op jit(solution)/shard_map/all_to_all | solution.py:222
  8.8 8.6 %all-to-all-done = bf16[8,160,224]{2,1,0:T(8,128)(2,1)S(1)} async-done(((bf16[8,160,224]{2,1,0:T(8,128)(2,1)}), bf16[8,160,224]{2,1,0:T(8,128)(2,1)S(1)}, u32[]{:S(2)}, u32[]{:S(2)}) %all-to-all-start) | async-done | bytes 573472 | tf_op jit(solution)/shard_map/all_to_all | solution.py:222
  17.4 7.1 %all-to-all-start.3 = ((bf16[16,16,640]{2,1,0:T(8,128)(2,1)}), bf16[16,16,640]{2,1,0:T(8,128)(2,1)S(1)}, u32[]{:S(2)}, u32[]{:S(2)}) async-start(bf16[16,16,640]{2,1,0:T(8,128)(2,1)} %shard_map.50), calls=%async_computation.3 | async-start | bytes 655360 | tf_op jit(solution)/shard_map/all_to_all | solution.py:213
  24.5 3.3 %shard_map.47 = (bf16[224,640]{1,0:T(8,128)(2,1)}, bf16[8,320,224]{2,1,0:T(8,128)(2,1)}) custom-call(s32[16,640]{1,0:T(8,128)} %ids_ref.1, bf16[1280,224]{1,0:T(8,128)(2,1)} %bitcast.24), custom_call_target="tpu_custom_call" | custom-call | tf_op jit(solution)/shard_map/pallas_call | solution.py:130
  27.8 6.7 %all-to-all-done.3 = bf16[16,16,640]{2,1,0:T(8,128)(2,1)S(1)} async-done(((bf16[16,16,640]{2,1,0:T(8,128)(2,1)}), bf16[16,16,640]{2,1,0:T(8,128)(2,1)S(1)}, u32[]{:S(2)}, u32[]{:S(2)}) %all-to-all-start.3) | async-done | bytes 327712 | tf_op jit(solution)/shard_map/all_to_all | solution.py:213
  34.5 3.7 %all-to-all-start.1 = ((bf16[8,320,224]{2,1,0:T(8,128)(2,1)}), bf16[8,320,224]{2,1,0:T(8,128)(2,1)S(1)}, u32[]{:S(2)}, u32[]{:S(2)}) async-start(bf16[8,320,224]{2,1,0:T(8,128)(2,1)} %get-tuple-element.15), calls=%async_computation.1 | async-start | bytes 2621440 | tf_op jit(solution)/shard_map/all_to_all | solution.py:229
  40.9 3.4 %collective-permute-start.11 = (bf16[256,640]{1,0:T(8,128)(2,1)S(1)}, bf16[256,640]{1,0:T(8,128)(2,1)S(1)}, u32[]{:S(2)}, u32[]{:S(2)}) collective-permute-start(bf16[256,640]{1,0:T(8,128)(2,1)S(1)} %bitcast.19), channel_id=1, source_target_pairs={{0,4},{2,6},{4,0},{6,2},{1,5},{3,7},{5,1},{7,3},{8,12},{10,14},{12... | collective-permute-start | bytes 983048 | tf_op jit(solution)/shard_map/ppermute | solution.py:196
  44.3 2.7 %collective-permute-start.12 = (bf16[256,640]{1,0:T(8,128)(2,1)S(1)}, bf16[256,640]{1,0:T(8,128)(2,1)S(1)}, u32[]{:S(2)}, u32[]{:S(2)}) collective-permute-start(bf16[256,640]{1,0:T(8,128)(2,1)S(1)} %bitcast.20), channel_id=1, source_target_pairs={{0,6},{2,0},{4,2},{6,4},{1,7},{3,1},{5,3},{7,5},{8,14},{10,8},{12,... | collective-permute-start | bytes 983048 | tf_op jit(solution)/shard_map/ppermute | solution.py:196
  47.0 3.2 %collective-permute-start.10 = (bf16[256,640]{1,0:T(8,128)(2,1)S(1)}, bf16[256,640]{1,0:T(8,128)(2,1)S(1)}, u32[]{:S(2)}, u32[]{:S(2)}) collective-permute-start(bf16[256,640]{1,0:T(8,128)(2,1)S(1)} %bitcast.21), channel_id=1, source_target_pairs={{0,2},{2,4},{4,6},{6,0},{1,3},{3,5},{5,7},{7,1},{8,10},{10,12},{12... | collective-permute-start | bytes 983048 | tf_op jit(solution)/shard_map/ppermute | solution.py:196
  50.9 11.8 %collective-permute-done.2 = bf16[224,640]{1,0:T(8,128)(2,1)} collective-permute-done((bf16[224,640]{1,0:T(8,128)(2,1)S(1)}, bf16[224,640]{1,0:T(8,128)(2,1)}, u32[]{:S(2)}, u32[]{:S(2)}) %collective-permute-start.2) | collective-permute-done | bytes 286752 | tf_op jit(solution)/shard_map/ppermute | solution.py:225
  68.5 3.8 %shard_map.48 = bf16[4,320,640]{2,1,0:T(8,128)(2,1)} custom-call(bf16[4,2,320,224]{3,2,1,0:T(8,128)(2,1)} %bitcast.17, bf16[224,640]{1,0:T(8,128)(2,1)} %copy-done.8, bf16[224,640]{1,0:T(8,128)(2,1)} %copy-done.15), custom_call_target="tpu_custom_call" | custom-call | tf_op jit(solution)/shard_map/pallas_call | solution.py:174
  72.3 6.5 %all-to-all-start.2 = ((bf16[16,80,640]{2,1,0:T(8,128)(2,1)}), bf16[16,80,640]{2,1,0:T(8,128)(2,1)S(1)}, u32[]{:S(2)}, u32[]{:S(2)}) async-start(bf16[16,80,640]{2,1,0:T(8,128)(2,1)} %bitcast.16), calls=%async_computation.2 | async-start | bytes 3276800 | tf_op jit(solution)/shard_map/all_to_all | solution.py:231
  87.3 29.3 %collective-permute-done.4.refs_0_ = bf16[80,2048]{1,0:T(8,128)(2,1)S(1)} collective-permute-done((bf16[80,2048]{1,0:T(8,128)(2,1)S(1)}, bf16[80,2048]{1,0:T(8,128)(2,1)S(1)}, u32[]{:S(2)}, u32[]{:S(2)}) %collective-permute-start.4) | collective-permute-done | bytes 327712 | tf_op jit(solution)/shard_map/ppermute | solution.py:218
  117.5 3.4 %shard_map.49 = (bf16[80,2048]{1,0:T(8,128)(2,1)}, bf16[80,2048]{1,0:T(8,128)(2,1)}, bf16[80,2048]{1,0:T(8,128)(2,1)}, bf16[80,2048]{1,0:T(8,128)(2,1)}) custom-call(bf16[80,2048]{1,0:T(8,128)(2,1)} %copy-done.9, bf16[80,2048]{1,0:T(8,128)(2,1)} %copy-done.10, bf16[80,2048]{1,0:T(8,128)(2,1)} %copy-done.11, bf16[4,80,2048]{2,1,0:T(8,128)(2,1)} %bitcast.18), custom_call_target="tpu_custom_call" | custom-call | tf_op jit(solution)/shard_map/pallas_call | solution.py:152
  120.8 3.4 %collective-permute-start.7 = (bf16[80,2048]{1,0:T(8,128)(2,1)}, bf16[80,2048]{1,0:T(8,128)(2,1)S(1)}, u32[]{:S(2)}, u32[]{:S(2)}) collective-permute-start(bf16[80,2048]{1,0:T(8,128)(2,1)} %get-tuple-element.18), channel_id=1, source_target_pairs={{0,32},{32,64},{64,96},{96,0},{1,33},{33,65},{65,97},{97,1},{2,34}... | collective-permute-start | bytes 983048 | tf_op jit(solution)/shard_map/ppermute | solution.py:234
  124.2 4.6 %collective-permute-start.8 = (bf16[80,2048]{1,0:T(8,128)(2,1)}, bf16[80,2048]{1,0:T(8,128)(2,1)S(1)}, u32[]{:S(2)}, u32[]{:S(2)}) collective-permute-start(bf16[80,2048]{1,0:T(8,128)(2,1)} %get-tuple-element.19), channel_id=1, source_target_pairs={{0,64},{32,96},{64,0},{96,32},{1,65},{33,97},{65,1},{97,33},{2,66}... | collective-permute-start | bytes 983048 | tf_op jit(solution)/shard_map/ppermute | solution.py:234
  128.8 3.4 %collective-permute-start.9 = (bf16[80,2048]{1,0:T(8,128)(2,1)}, bf16[80,2048]{1,0:T(8,128)(2,1)S(1)}, u32[]{:S(2)}, u32[]{:S(2)}) collective-permute-start(bf16[80,2048]{1,0:T(8,128)(2,1)} %get-tuple-element.20), channel_id=1, source_target_pairs={{0,96},{32,0},{64,32},{96,64},{1,97},{33,1},{65,33},{97,65},{2,98}... | collective-permute-start | bytes 983048 | tf_op jit(solution)/shard_map/ppermute | solution.py:234
  133.8 7.9 %collective-permute-done.8.refs_2_ = bf16[80,2048]{1,0:T(8,128)(2,1)S(1)} collective-permute-done((bf16[80,2048]{1,0:T(8,128)(2,1)}, bf16[80,2048]{1,0:T(8,128)(2,1)S(1)}, u32[]{:S(2)}, u32[]{:S(2)}) %collective-permute-start.8) | collective-permute-done | bytes 327712 | tf_op jit(solution)/shard_map/ppermute | solution.py:234
  144.1 4.4 %shard_map.51 = (f32[80,640]{1,0:T(8,128)}, f32[80,640]{1,0:T(8,128)}, f32[80,640]{1,0:T(8,128)}, f32[80,640]{1,0:T(8,128)}) custom-call(bf16[80,2048]{1,0:T(8,128)(2,1)} %get-tuple-element.17.refs_0_, bf16[80,2048]{1,0:T(8,128)(2,1)} %copy-done.12, bf16[80,2048]{1,0:T(8,128)(2,1)} %copy-done.13, bf16[80,2048]{1,0:T(8,128)(2,1)} %copy-done.14, ...), custom_call_target="tpu_custom_call" | custom-call | tf_op jit(solution)/shard_map/pallas_call | solution.py:164
  148.5 4.5 %collective-permute-start.14 = (f32[80,640]{1,0:T(8,128)}, f32[80,640]{1,0:T(8,128)S(1)}, u32[]{:S(2)}, u32[]{:S(2)}) collective-permute-start(f32[80,640]{1,0:T(8,128)} %get-tuple-element.22), channel_id=1, source_target_pairs={{0,96},{32,0},{64,32},{96,64},{1,97},{33,1},{65,33},{97,65},{2,98}... | collective-permute-start | bytes 614408 | tf_op jit(solution)/shard_map/ppermute | solution.py:236
  153.0 3.7 %collective-permute-start.15 = (f32[80,640]{1,0:T(8,128)}, f32[80,640]{1,0:T(8,128)S(1)}, u32[]{:S(2)}, u32[]{:S(2)}) collective-permute-start(f32[80,640]{1,0:T(8,128)} %get-tuple-element.23), channel_id=1, source_target_pairs={{0,64},{32,96},{64,0},{96,32},{1,65},{33,97},{65,1},{97,33},{2,66}... | collective-permute-start | bytes 614408 | tf_op jit(solution)/shard_map/ppermute | solution.py:236
  158.6 3.6 %collective-permute-done.14.refs_1_ = f32[80,640]{1,0:T(8,128)S(1)} collective-permute-done((f32[80,640]{1,0:T(8,128)}, f32[80,640]{1,0:T(8,128)S(1)}, u32[]{:S(2)}, u32[]{:S(2)}) %collective-permute-start.14) | collective-permute-done | bytes 204832 | tf_op jit(solution)/shard_map/ppermute | solution.py:236
  164.6 3.2 %collective-permute-done.16.refs_3_ = f32[80,640]{1,0:T(8,128)S(1)} collective-permute-done((f32[80,640]{1,0:T(8,128)}, f32[80,640]{1,0:T(8,128)S(1)}, u32[]{:S(2)}, u32[]{:S(2)}) %collective-permute-start.16) | collective-permute-done | bytes 204832 | tf_op jit(solution)/shard_map/ppermute | solution.py:236
  168.4 2.8 %shard_map.52 = f32[4,80,640]{2,1,0:T(8,128)} custom-call(bf16[4,4,80,640]{3,2,1,0:T(8,128)(2,1)} %bitcast.15, f32[80,640]{1,0:T(8,128)} %get-tuple-element.21.refs_0_, f32[80,640]{1,0:T(8,128)} %copy-done.18, f32[80,640]{1,0:T(8,128)} %copy-done.19, f32[80,640]{1,0:T(8,128)} %copy-done.20), custom_call_target="tpu_custom_call" | custom-call | tf_op jit(solution)/shard_map/pallas_call | solution.py:183
  (71 shorter events, 31.2 us)
Async XLA Ops:
  2.2 15.2 %all-to-all-start = ((bf16[8,160,224]{2,1,0:T(8,128)(2,1)}), bf16[8,160,224]{2,1,0:T(8,128)(2,1)S(1)}, u32[]{:S(2)}, u32[]{:S(2)}) async-start(bf16[8,160,224]{2,1,0:T(8,128)(2,1)} %shard_map.46), calls=%async_computation | async-start | bytes 1310720 | tf_op jit(solution)/shard_map/all_to_all | solution.py:222
  17.4 17.1 %all-to-all-start.3 = ((bf16[16,16,640]{2,1,0:T(8,128)(2,1)}), bf16[16,16,640]{2,1,0:T(8,128)(2,1)S(1)}, u32[]{:S(2)}, u32[]{:S(2)}) async-start(bf16[16,16,640]{2,1,0:T(8,128)(2,1)} %shard_map.50), calls=%async_computation.3 | async-start | bytes 655360 | tf_op jit(solution)/shard_map/all_to_all | solution.py:213
  34.5 45.3 %copy-start.3 = (bf16[16,16,640]{2,1,0:T(8,128)(2,1)}, bf16[16,16,640]{2,1,0:T(8,128)(2,1)S(1)}, u32[]{:S(2)}) copy-start(bf16[16,16,640]{2,1,0:T(8,128)(2,1)S(1)} %all-to-all-done.3) | copy-start | bytes 983044
  34.5 32.8 %all-to-all-start.1 = ((bf16[8,320,224]{2,1,0:T(8,128)(2,1)}), bf16[8,320,224]{2,1,0:T(8,128)(2,1)S(1)}, u32[]{:S(2)}, u32[]{:S(2)}) async-start(bf16[8,320,224]{2,1,0:T(8,128)(2,1)} %get-tuple-element.15), calls=%async_computation.1 | async-start | bytes 2621440 | tf_op jit(solution)/shard_map/all_to_all | solution.py:229
  38.2 8.8 %collective-permute-start = (bf16[224,640]{1,0:T(8,128)(2,1)S(1)}, bf16[224,640]{1,0:T(8,128)(2,1)S(1)}, u32[]{:S(2)}, u32[]{:S(2)}) collective-permute-start(bf16[224,640]{1,0:T(8,128)(2,1)S(1)} %copy-done.16), channel_id=1, source_target_pairs={{408,24},{409,25},{410,26},{411,27},{412,28},{413,29},{414,30},{41... | collective-permute-start | bytes 860168 | tf_op jit(solution)/shard_map/ppermute | solution.py:225
  38.9 11.2 %collective-permute-start.1 = (bf16[224,640]{1,0:T(8,128)(2,1)S(1)}, bf16[224,640]{1,0:T(8,128)(2,1)S(1)}, u32[]{:S(2)}, u32[]{:S(2)}) collective-permute-start(bf16[224,640]{1,0:T(8,128)(2,1)S(1)} %copy-done.16), channel_id=1, source_target_pairs={{272,16},{408,152},{273,17},{409,153},{274,18},{410,154},{275,19},... | collective-permute-start | bytes 860168 | tf_op jit(solution)/shard_map/ppermute | solution.py:225
  39.6 23.1 %collective-permute-start.2 = (bf16[224,640]{1,0:T(8,128)(2,1)S(1)}, bf16[224,640]{1,0:T(8,128)(2,1)}, u32[]{:S(2)}, u32[]{:S(2)}) collective-permute-start(bf16[224,640]{1,0:T(8,128)(2,1)S(1)} %copy-done.16), channel_id=1, source_target_pairs={{136,8},{272,144},{408,280},{137,9},{273,145},{409,281},{138,10},{... | collective-permute-start | bytes 860168 | tf_op jit(solution)/shard_map/ppermute | solution.py:225
  40.9 37.9 %collective-permute-start.11 = (bf16[256,640]{1,0:T(8,128)(2,1)S(1)}, bf16[256,640]{1,0:T(8,128)(2,1)S(1)}, u32[]{:S(2)}, u32[]{:S(2)}) collective-permute-start(bf16[256,640]{1,0:T(8,128)(2,1)S(1)} %bitcast.19), channel_id=1, source_target_pairs={{0,4},{2,6},{4,0},{6,2},{1,5},{3,7},{5,1},{7,3},{8,12},{10,14},{12... | collective-permute-start | bytes 983048 | tf_op jit(solution)/shard_map/ppermute | solution.py:196
  44.3 34.5 %collective-permute-start.12 = (bf16[256,640]{1,0:T(8,128)(2,1)S(1)}, bf16[256,640]{1,0:T(8,128)(2,1)S(1)}, u32[]{:S(2)}, u32[]{:S(2)}) collective-permute-start(bf16[256,640]{1,0:T(8,128)(2,1)S(1)} %bitcast.20), channel_id=1, source_target_pairs={{0,6},{2,0},{4,2},{6,4},{1,7},{3,1},{5,3},{7,5},{8,14},{10,8},{12,... | collective-permute-start | bytes 983048 | tf_op jit(solution)/shard_map/ppermute | solution.py:196
  47.0 31.9 %collective-permute-start.10 = (bf16[256,640]{1,0:T(8,128)(2,1)S(1)}, bf16[256,640]{1,0:T(8,128)(2,1)S(1)}, u32[]{:S(2)}, u32[]{:S(2)}) collective-permute-start(bf16[256,640]{1,0:T(8,128)(2,1)S(1)} %bitcast.21), channel_id=1, source_target_pairs={{0,2},{2,4},{4,6},{6,0},{1,3},{3,5},{5,7},{7,1},{8,10},{10,12},{12... | collective-permute-start | bytes 983048 | tf_op jit(solution)/shard_map/ppermute | solution.py:196
  63.9 3.5 %collective-permute-start.3 = (bf16[224,640]{1,0:T(8,128)(2,1)S(1)}, bf16[224,640]{1,0:T(8,128)(2,1)S(1)}, u32[]{:S(2)}, u32[]{:S(2)}) collective-permute-start(bf16[224,640]{1,0:T(8,128)(2,1)S(1)} %add_select_fusion.own_ref), channel_id=1, source_target_pairs={{0,1},{1,0},{2,3},{3,2},{4,5},{5,4},{6,7},{7,6},{8,9},{9,8},{10,11... | collective-permute-start | bytes 860168 | tf_op jit(solution)/shard_map/ppermute | solution.py:227
  72.3 86.3 %all-to-all-start.2 = ((bf16[16,80,640]{2,1,0:T(8,128)(2,1)}), bf16[16,80,640]{2,1,0:T(8,128)(2,1)S(1)}, u32[]{:S(2)}, u32[]{:S(2)}) async-start(bf16[16,80,640]{2,1,0:T(8,128)(2,1)} %bitcast.16), calls=%async_computation.2 | async-start | bytes 3276800 | tf_op jit(solution)/shard_map/all_to_all | solution.py:231
  82.3 61.1 %collective-permute-start.13 = (bf16[4,256,640]{2,1,0:T(8,128)(2,1)}, bf16[4,256,640]{2,1,0:T(8,128)(2,1)}, u32[]{:S(2)}, u32[]{:S(2)}) collective-permute-start(bf16[4,256,640]{2,1,0:T(8,128)(2,1)} %pad_maximum_fusion), channel_id=1, source_target_pairs={{0,1},{1,0},{2,3},{3,2},{4,5},{5,4},{6,7},{7,6},{8,9},{9,8},{10,11... | collective-permute-start | bytes 3932168 | tf_op jit(solution)/shard_map/ppermute | solution.py:198
  84.6 31.9 %collective-permute-start.4 = (bf16[80,2048]{1,0:T(8,128)(2,1)S(1)}, bf16[80,2048]{1,0:T(8,128)(2,1)S(1)}, u32[]{:S(2)}, u32[]{:S(2)}) collective-permute-start(bf16[80,2048]{1,0:T(8,128)(2,1)S(1)} %multiply_reduce_fusion), channel_id=1, source_target_pairs={{0,8},{8,16},{16,24},{136,144},{144,152},{272,280},{1,9},{9,17},{1... | collective-permute-start | bytes 983048 | tf_op jit(solution)/shard_map/ppermute | solution.py:218
  85.9 30.6 %collective-permute-start.5 = (bf16[80,2048]{1,0:T(8,128)(2,1)S(1)}, bf16[80,2048]{1,0:T(8,128)(2,1)S(1)}, u32[]{:S(2)}, u32[]{:S(2)}) collective-permute-start(bf16[80,2048]{1,0:T(8,128)(2,1)S(1)} %multiply_reduce_fusion), channel_id=1, source_target_pairs={{0,16},{8,24},{136,152},{1,17},{9,25},{137,153},{2,18},{10,26},{13... | collective-permute-start | bytes 983048 | tf_op jit(solution)/shard_map/ppermute | solution.py:219
  86.6 30.0 %collective-permute-start.6 = (bf16[80,2048]{1,0:T(8,128)(2,1)S(1)}, bf16[80,2048]{1,0:T(8,128)(2,1)S(1)}, u32[]{:S(2)}, u32[]{:S(2)}) collective-permute-start(bf16[80,2048]{1,0:T(8,128)(2,1)S(1)} %multiply_reduce_fusion), channel_id=1, source_target_pairs={{0,24},{1,25},{2,26},{3,27},{4,28},{5,29},{6,30},{7,31},{32,56},{3... | collective-permute-start | bytes 983048 | tf_op jit(solution)/shard_map/ppermute | solution.py:219
  120.8 13.0 %collective-permute-start.7 = (bf16[80,2048]{1,0:T(8,128)(2,1)}, bf16[80,2048]{1,0:T(8,128)(2,1)S(1)}, u32[]{:S(2)}, u32[]{:S(2)}) collective-permute-start(bf16[80,2048]{1,0:T(8,128)(2,1)} %get-tuple-element.18), channel_id=1, source_target_pairs={{0,32},{32,64},{64,96},{96,0},{1,33},{33,65},{65,97},{97,1},{2,34}... | collective-permute-start | bytes 983048 | tf_op jit(solution)/shard_map/ppermute | solution.py:234
  124.2 17.5 %collective-permute-start.8 = (bf16[80,2048]{1,0:T(8,128)(2,1)}, bf16[80,2048]{1,0:T(8,128)(2,1)S(1)}, u32[]{:S(2)}, u32[]{:S(2)}) collective-permute-start(bf16[80,2048]{1,0:T(8,128)(2,1)} %get-tuple-element.19), channel_id=1, source_target_pairs={{0,64},{32,96},{64,0},{96,32},{1,65},{33,97},{65,1},{97,33},{2,66}... | collective-permute-start | bytes 983048 | tf_op jit(solution)/shard_map/ppermute | solution.py:234
  128.8 14.6 %collective-permute-start.9 = (bf16[80,2048]{1,0:T(8,128)(2,1)}, bf16[80,2048]{1,0:T(8,128)(2,1)S(1)}, u32[]{:S(2)}, u32[]{:S(2)}) collective-permute-start(bf16[80,2048]{1,0:T(8,128)(2,1)} %get-tuple-element.20), channel_id=1, source_target_pairs={{0,96},{32,0},{64,32},{96,64},{1,97},{33,1},{65,33},{97,65},{2,98}... | collective-permute-start | bytes 983048 | tf_op jit(solution)/shard_map/ppermute | solution.py:234
  133.8 9.6 %copy-start.12 = (bf16[80,2048]{1,0:T(8,128)(2,1)}, bf16[80,2048]{1,0:T(8,128)(2,1)S(1)}, u32[]{:S(2)}) copy-start(bf16[80,2048]{1,0:T(8,128)(2,1)S(1)} %collective-permute-done.7.refs_1_) | copy-start | bytes 983044
  148.5 13.8 %collective-permute-start.14 = (f32[80,640]{1,0:T(8,128)}, f32[80,640]{1,0:T(8,128)S(1)}, u32[]{:S(2)}, u32[]{:S(2)}) collective-permute-start(f32[80,640]{1,0:T(8,128)} %get-tuple-element.22), channel_id=1, source_target_pairs={{0,96},{32,0},{64,32},{96,64},{1,97},{33,1},{65,33},{97,65},{2,98}... | collective-permute-start | bytes 614408 | tf_op jit(solution)/shard_map/ppermute | solution.py:236
  153.0 11.6 %collective-permute-start.15 = (f32[80,640]{1,0:T(8,128)}, f32[80,640]{1,0:T(8,128)S(1)}, u32[]{:S(2)}, u32[]{:S(2)}) collective-permute-start(f32[80,640]{1,0:T(8,128)} %get-tuple-element.23), channel_id=1, source_target_pairs={{0,64},{32,96},{64,0},{96,32},{1,65},{33,97},{65,1},{97,33},{2,66}... | collective-permute-start | bytes 614408 | tf_op jit(solution)/shard_map/ppermute | solution.py:236
  156.7 11.0 %collective-permute-start.16 = (f32[80,640]{1,0:T(8,128)}, f32[80,640]{1,0:T(8,128)S(1)}, u32[]{:S(2)}, u32[]{:S(2)}) collective-permute-start(f32[80,640]{1,0:T(8,128)} %get-tuple-element.24), channel_id=1, source_target_pairs={{0,32},{32,64},{64,96},{96,0},{1,33},{33,65},{65,97},{97,1},{2,34}... | collective-permute-start | bytes 614408 | tf_op jit(solution)/shard_map/ppermute | solution.py:236
  158.6 9.1 %copy-start = (bf16[16,80,640]{2,1,0:T(8,128)(2,1)}, bf16[16,80,640]{2,1,0:T(8,128)(2,1)S(1)}, u32[]{:S(2)}) copy-start(bf16[16,80,640]{2,1,0:T(8,128)(2,1)S(1)} %all-to-all-done.2) | copy-start | bytes 4915204
  (18 other events, 38.1 us)

commit v6 on v5

--- a/solution.py
+++ b/solution.py
@@ -45,11 +45,6 @@
                 pieces_ref[x * CORE + c, y * height : (y + 1) * height] = rows[f * height : (f + 1) * height]
 
 
-def spread_kernel(rows_ref, out_ref):
-    for z in range(ZLO):
-        out_ref[z * X : (z + 1) * X] = rows_ref[...]
-
-
 def prefix_kernel(*refs):
     total_refs, decoders_ref, out_refs = refs[: TGT - 1], refs[TGT - 1], refs[TGT:]
     step = 16
@@ -77,18 +72,23 @@
 
 def virtual_kernel(*refs):
     prefix_refs, own_refs, other_ref, out_refs, rows_ref = refs[:X], refs[X : X + Y], refs[X + Y], refs[X + Y + 1 : -1], refs[-1]
-    groups, slices, depth, width = rows_ref.shape
-    y, core = lax.axis_index("y"), lax.axis_index("core")
+    planes, columns, slices, depth, width = rows_ref.shape
+    z, y, core = lax.axis_index("zlo"), lax.axis_index("y"), lax.axis_index("core")
     for r in range(Y):
         row = (y + Y - r) % Y
-        rows_ref[:, row * CORE + core] = own_refs[r][...].reshape(groups, depth, width)
-        rows_ref[:, row * CORE + 1 - core] = other_ref[r].reshape(groups, depth, width)
+        own = own_refs[r][...].reshape(columns, planes, depth, width)
+        other = other_ref[r].reshape(columns, planes, depth, width)
+        for k in range(planes):
+            plane = (z + planes - k) % planes
+            rows_ref[plane, :, row * CORE + core] = own[:, k]
+            rows_ref[plane, :, row * CORE + 1 - core] = other[:, k]
     height = prefix_refs[0].shape[0]
-    chunk = slices * depth
+    chunk = columns * slices * depth // 2
     total = jnp.zeros((X * height, width), jnp.float32)
-    for g in range(0, groups, 2):
-        left = jnp.concatenate([ref[:, g * chunk : (g + 2) * chunk] for ref in prefix_refs], 0)
-        right = rows_ref[g : g + 2].reshape(2 * chunk, width)
+    for g in range(2 * planes):
+        left = jnp.concatenate([ref[:, g * chunk : (g + 1) * chunk] for ref in prefix_refs], 0)
+        half = columns // 2
+        right = rows_ref[g // 2, (g % 2) * half : (g % 2 + 1) * half].reshape(chunk, width)
         total += jnp.dot(left, right, preferred_element_type=jnp.float32)
     for r in range(X):
         out_refs[r][...] = total[r * height : (r + 1) * height]
@@ -138,15 +138,6 @@
     )(window_ids, sliced)
 
 
-def spread_of(rows):
-    return pl.pallas_call(
-        spread_kernel,
-        out_shape=jax.ShapeDtypeStruct((ZLO * rows.shape[0],) + rows.shape[1:], rows.dtype),
-        in_specs=[VMEM],
-        out_specs=VMEM,
-    )(rows)
-
-
 def prefix_of(totals, decoders):
     piece = jax.ShapeDtypeStruct(decoders.shape[1:], jnp.bfloat16)
     return pl.pallas_call(
@@ -160,13 +151,13 @@
 def virtual_of(prefix, own, other):
     height, depth = prefix[0].shape
     width = other.shape[2]
-    groups = ZLO * X
+    slices = Y * CORE
     return pl.pallas_call(
         virtual_kernel,
         out_shape=[jax.ShapeDtypeStruct((height, width), jnp.float32)] * X,
         in_specs=[VMEM] * (len(prefix) + len(own) + 1),
         out_specs=[VMEM] * X,
-        scratch_shapes=[pltpu.VMEM((groups, Y * CORE, depth // (groups * Y * CORE), width), jnp.bfloat16)],
+        scratch_shapes=[pltpu.VMEM((ZLO, X, slices, depth // (ZLO * X * slices), width), jnp.bfloat16)],
     )(*prefix, *own, other)
 
 
@@ -209,14 +200,13 @@
     slices = Y * CORE
     tokens = token_count // slices
 
-    spread = spread_of(encoders)
-    encoder_rows = lax.all_to_all(spread, ("zlo", "x"), 0, 0, tiled=True).reshape(-1, fw)
+    planes = [encoders] + [lax.ppermute(encoders, "zlo", ring(ZLO, k)) for k in range(1, ZLO)]
+    encoder_rows = lax.all_to_all(jnp.stack(planes, 1), "x", 0, 0, tiled=True).reshape(-1, fw)
     encoder_own, encoder_other = over_feat(encoder_rows)
 
     live = (block * targets + jnp.arange(targets) >= source).astype(jnp.float32)
     total = jnp.sum(decoders[0].astype(jnp.float32) * live[:, None, None], 0).astype(jnp.bfloat16)
-    earlier = [lax.ppermute(total, ("zlo", "tgt"), total_pairs(1))]
-    earlier += [lax.ppermute(total, ("zlo", "tgt"), total_pairs(k)) for k in (2, 3)]
+    earlier = [lax.ppermute(total, ("zlo", "tgt"), total_pairs(k)) for k in (3, 2, 1)]
 
     by_tokens = split(activations[0].T, slices)
     sliced = lax.all_to_all(by_tokens, FEAT, 0, 0, tiled=True).reshape(slices * local_feats, tokens)

time: 172 us -> 175 us (1.017)
  the two profiles are of different devices: /device:TPU:456 before, /device:TPU:296 now
where the time goes in v6:
time: 175 us; the launch traced here: 174 us
  starting transfers between devices  77.6 us (44%)
  waiting for transfers between devices  65.9 us (38%)
  Pallas kernels  19.9 us (11%)
  local copies, waits for them, and re-layouts  5.5 us (3%)
  other arithmetic  4.78 us (3%)
    ppermute x3, waiting for transfers between devices, per_device(): lax.ppermute(total, ('zlo', 'tgt'), total_pairs(k))  31 us
    ppermute x3, starting transfers between devices, per_device(): moved = [lax.ppermute(pieces[k], 'x', ring(X, k)) for k in range(1, X)]  11.3 us
    ppermute x3, waiting for transfers between devices, per_device(): moved = [lax.ppermute(pieces[k], 'x', ring(X, k)) for k in range(1, X)]  11.2 us
    ppermute x3, starting transfers between devices, per_device(): lax.ppermute(encoders, 'zlo', ring(ZLO, k))  11 us
    ppermute x3, starting transfers between devices, over_feat(): others = [lax.ppermute(piece, 'y', ring(Y, k)) for k in range(1, Y)]  10.4 us
    ppermute x3, starting transfers between devices, per_device(): lax.ppermute(virtual[k], 'x', ring(X, X - k))  10.1 us
    ppermute x3, waiting for transfers between devices, per_device(): lax.ppermute(virtual[k], 'x', ring(X, X - k))  9.11 us
    ppermute x3, starting transfers between devices, per_device(): lax.ppermute(total, ('zlo', 'tgt'), total_pairs(k))  7.93 us
  transfers between devices with their start and end apart: 24, of which 11 were waited for; matrix products, arithmetic and copies ran while one was open for 3% of the time, Pallas kernels for 9%

profile of v6, /device:TPU:296, one launch (start us, length us, event | category | flops | bytes accessed | tf_op | source)
XLA Modules:
  0.0 174.1 jit_solution(10616379578730594029)
XLA Ops:
  2.2 4.9 %all-to-all-start = ((bf16[8,160,224]{2,1,0:T(8,128)(2,1)}), bf16[8,160,224]{2,1,0:T(8,128)(2,1)S(1)}, u32[]{:S(2)}, u32[]{:S(2)}) async-start(bf16[8,160,224]{2,1,0:T(8,128)(2,1)} %shard_map.46), calls=%async_computation | async-start | bytes 1310720 | tf_op jit(solution)/shard_map/all_to_all | solution.py:212
  10.0 2.9 %collective-permute-start.10 = (bf16[4,16,640]{2,1,0:T(8,128)(2,1)S(1)}, bf16[4,16,640]{2,1,0:T(8,128)(2,1)S(1)}, u32[]{:S(2)}, u32[]{:S(2)}) collective-permute-start(bf16[4,16,640]{2,1,0:T(8,128)(2,1)S(1)} %copy-done.21), channel_id=1, source_target_pairs={{0,128},{128,256},{256,384},{384,0},{1,129},{129,257},{257,385},{3... | collective-permute-start | bytes 245768 | tf_op jit(solution)/shard_map/ppermute | solution.py:203
  13.0 5.2 %collective-permute-start.11 = (bf16[4,16,640]{2,1,0:T(8,128)(2,1)S(1)}, bf16[4,16,640]{2,1,0:T(8,128)(2,1)S(1)}, u32[]{:S(2)}, u32[]{:S(2)}) collective-permute-start(bf16[4,16,640]{2,1,0:T(8,128)(2,1)S(1)} %copy-done.21), channel_id=1, source_target_pairs={{0,256},{128,384},{256,0},{384,128},{1,257},{129,385},{257,1},{385... | collective-permute-start | bytes 245768 | tf_op jit(solution)/shard_map/ppermute | solution.py:203
  21.4 4.3 %all-to-all-start.3 = ((bf16[4,4,16,640]{3,2,1,0:T(8,128)(2,1)}), bf16[4,4,16,640]{3,2,1,0:T(8,128)(2,1)S(1)}, u32[]{:S(2)}, u32[]{:S(2)}) async-start(bf16[4,4,16,640]{3,2,1,0:T(8,128)(2,1)} %pad_maximum_fusion.1), calls=%async_computation.3 | async-start | bytes 655360 | tf_op jit(solution)/shard_map/all_to_all | solution.py:204
  25.7 3.3 %shard_map.47 = (bf16[224,640]{1,0:T(8,128)(2,1)}, bf16[8,320,224]{2,1,0:T(8,128)(2,1)}) custom-call(s32[16,640]{1,0:T(8,128)} %ids_ref.1, bf16[1280,224]{1,0:T(8,128)(2,1)} %bitcast.28), custom_call_target="tpu_custom_call" | custom-call | tf_op jit(solution)/shard_map/pallas_call | solution.py:130
  28.9 3.7 %all-to-all-done.3 = bf16[4,4,16,640]{3,2,1,0:T(8,128)(2,1)S(1)} async-done(((bf16[4,4,16,640]{3,2,1,0:T(8,128)(2,1)}), bf16[4,4,16,640]{3,2,1,0:T(8,128)(2,1)S(1)}, u32[]{:S(2)}, u32[]{:S(2)}) %all-to-all-start.3) | async-done | bytes 327712 | tf_op jit(solution)/shard_map/all_to_all | solution.py:204
  32.7 3.7 %all-to-all-start.1 = ((bf16[8,320,224]{2,1,0:T(8,128)(2,1)}), bf16[8,320,224]{2,1,0:T(8,128)(2,1)S(1)}, u32[]{:S(2)}, u32[]{:S(2)}) async-start(bf16[8,320,224]{2,1,0:T(8,128)(2,1)} %get-tuple-element.15), calls=%async_computation.1 | async-start | bytes 2621440 | tf_op jit(solution)/shard_map/all_to_all | solution.py:219
  39.1 3.4 %collective-permute-start.13 = (bf16[256,640]{1,0:T(8,128)(2,1)S(1)}, bf16[256,640]{1,0:T(8,128)(2,1)S(1)}, u32[]{:S(2)}, u32[]{:S(2)}) collective-permute-start(bf16[256,640]{1,0:T(8,128)(2,1)S(1)} %bitcast.23), channel_id=1, source_target_pairs={{0,2},{2,4},{4,6},{6,0},{1,3},{3,5},{5,7},{7,1},{8,10},{10,12},{12... | collective-permute-start | bytes 983048 | tf_op jit(solution)/shard_map/ppermute | solution.py:187
  45.1 4.4 %collective-permute-start.15 = (bf16[256,640]{1,0:T(8,128)(2,1)S(1)}, bf16[256,640]{1,0:T(8,128)(2,1)S(1)}, u32[]{:S(2)}, u32[]{:S(2)}) collective-permute-start(bf16[256,640]{1,0:T(8,128)(2,1)S(1)} %bitcast.25), channel_id=1, source_target_pairs={{0,6},{2,0},{4,2},{6,4},{1,7},{3,1},{5,3},{7,5},{8,14},{10,8},{12,... | collective-permute-start | bytes 983048 | tf_op jit(solution)/shard_map/ppermute | solution.py:187
  50.3 6.9 %collective-permute-done.2 = bf16[224,640]{1,0:T(8,128)(2,1)} collective-permute-done((bf16[224,640]{1,0:T(8,128)(2,1)S(1)}, bf16[224,640]{1,0:T(8,128)(2,1)}, u32[]{:S(2)}, u32[]{:S(2)}) %collective-permute-start.2) | collective-permute-done | bytes 286752 | tf_op jit(solution)/shard_map/ppermute | solution.py:215
  62.9 3.8 %shard_map.48 = bf16[4,320,640]{2,1,0:T(8,128)(2,1)} custom-call(bf16[4,2,320,224]{3,2,1,0:T(8,128)(2,1)} %bitcast.21, bf16[224,640]{1,0:T(8,128)(2,1)} %copy-done.8, bf16[224,640]{1,0:T(8,128)(2,1)} %copy-done.15), custom_call_target="tpu_custom_call" | custom-call | tf_op jit(solution)/shard_map/pallas_call | solution.py:165
  66.7 7.4 %all-to-all-start.2 = ((bf16[16,80,640]{2,1,0:T(8,128)(2,1)}), bf16[16,80,640]{2,1,0:T(8,128)(2,1)S(1)}, u32[]{:S(2)}, u32[]{:S(2)}) async-start(bf16[16,80,640]{2,1,0:T(8,128)(2,1)} %bitcast.20), calls=%async_computation.2 | async-start | bytes 3276800 | tf_op jit(solution)/shard_map/all_to_all | solution.py:221
  81.3 6.6 %collective-permute-start.6 = (bf16[80,2048]{1,0:T(8,128)(2,1)S(1)}, bf16[80,2048]{1,0:T(8,128)(2,1)S(1)}, u32[]{:S(2)}, u32[]{:S(2)}) collective-permute-start(bf16[80,2048]{1,0:T(8,128)(2,1)S(1)} %multiply_reduce_fusion), channel_id=1, source_target_pairs={{0,8},{8,16},{16,24},{136,144},{144,152},{272,280},{1,9},{9,17},{1... | collective-permute-start | bytes 983048 | tf_op jit(solution)/shard_map/ppermute | solution.py:209
  87.9 31.0 %collective-permute-done.6.refs_2_ = bf16[80,2048]{1,0:T(8,128)(2,1)S(1)} collective-permute-done((bf16[80,2048]{1,0:T(8,128)(2,1)S(1)}, bf16[80,2048]{1,0:T(8,128)(2,1)S(1)}, u32[]{:S(2)}, u32[]{:S(2)}) %collective-permute-start.6) | collective-permute-done | bytes 327712 | tf_op jit(solution)/shard_map/ppermute | solution.py:209
  119.7 3.4 %shard_map.49 = (bf16[80,2048]{1,0:T(8,128)(2,1)}, bf16[80,2048]{1,0:T(8,128)(2,1)}, bf16[80,2048]{1,0:T(8,128)(2,1)}, bf16[80,2048]{1,0:T(8,128)(2,1)}) custom-call(bf16[80,2048]{1,0:T(8,128)(2,1)} %copy-done.9, bf16[80,2048]{1,0:T(8,128)(2,1)} %copy-done.10, bf16[80,2048]{1,0:T(8,128)(2,1)} %copy-done.11, bf16[4,80,2048]{2,1,0:T(8,128)(2,1)} %bitcast.22), custom_call_target="tpu_custom_call" | custom-call | tf_op jit(solution)/shard_map/pallas_call | solution.py:143
  123.1 3.4 %collective-permute-start.7 = (bf16[80,2048]{1,0:T(8,128)(2,1)}, bf16[80,2048]{1,0:T(8,128)(2,1)S(1)}, u32[]{:S(2)}, u32[]{:S(2)}) collective-permute-start(bf16[80,2048]{1,0:T(8,128)(2,1)} %get-tuple-element.18), channel_id=1, source_target_pairs={{0,32},{32,64},{64,96},{96,0},{1,33},{33,65},{65,97},{97,1},{2,34}... | collective-permute-start | bytes 983048 | tf_op jit(solution)/shard_map/ppermute | solution.py:224
  126.4 4.6 %collective-permute-start.8 = (bf16[80,2048]{1,0:T(8,128)(2,1)}, bf16[80,2048]{1,0:T(8,128)(2,1)S(1)}, u32[]{:S(2)}, u32[]{:S(2)}) collective-permute-start(bf16[80,2048]{1,0:T(8,128)(2,1)} %get-tuple-element.19), channel_id=1, source_target_pairs={{0,64},{32,96},{64,0},{96,32},{1,65},{33,97},{65,1},{97,33},{2,66}... | collective-permute-start | bytes 983048 | tf_op jit(solution)/shard_map/ppermute | solution.py:224
  131.0 3.4 %collective-permute-start.9 = (bf16[80,2048]{1,0:T(8,128)(2,1)}, bf16[80,2048]{1,0:T(8,128)(2,1)S(1)}, u32[]{:S(2)}, u32[]{:S(2)}) collective-permute-start(bf16[80,2048]{1,0:T(8,128)(2,1)} %get-tuple-element.20), channel_id=1, source_target_pairs={{0,96},{32,0},{64,32},{96,64},{1,97},{33,1},{65,33},{97,65},{2,98}... | collective-permute-start | bytes 983048 | tf_op jit(solution)/shard_map/ppermute | solution.py:224
  136.1 7.9 %collective-permute-done.8.refs_2_ = bf16[80,2048]{1,0:T(8,128)(2,1)S(1)} collective-permute-done((bf16[80,2048]{1,0:T(8,128)(2,1)}, bf16[80,2048]{1,0:T(8,128)(2,1)S(1)}, u32[]{:S(2)}, u32[]{:S(2)}) %collective-permute-start.8) | collective-permute-done | bytes 327712 | tf_op jit(solution)/shard_map/ppermute | solution.py:224
  146.4 4.4 %shard_map.50 = (f32[80,640]{1,0:T(8,128)}, f32[80,640]{1,0:T(8,128)}, f32[80,640]{1,0:T(8,128)}, f32[80,640]{1,0:T(8,128)}) custom-call(bf16[80,2048]{1,0:T(8,128)(2,1)} %get-tuple-element.17.refs_0_, bf16[80,2048]{1,0:T(8,128)(2,1)} %copy-done.12, bf16[80,2048]{1,0:T(8,128)(2,1)} %copy-done.13, bf16[80,2048]{1,0:T(8,128)(2,1)} %copy-done.14, ...), custom_call_target="tpu_custom_call" | custom-call | tf_op jit(solution)/shard_map/pallas_call | solution.py:155
  150.8 4.5 %collective-permute-start.17 = (f32[80,640]{1,0:T(8,128)}, f32[80,640]{1,0:T(8,128)S(1)}, u32[]{:S(2)}, u32[]{:S(2)}) collective-permute-start(f32[80,640]{1,0:T(8,128)} %get-tuple-element.22), channel_id=1, source_target_pairs={{0,96},{32,0},{64,32},{96,64},{1,97},{33,1},{65,33},{97,65},{2,98}... | collective-permute-start | bytes 614408 | tf_op jit(solution)/shard_map/ppermute | solution.py:226
  155.3 3.7 %collective-permute-start.18 = (f32[80,640]{1,0:T(8,128)}, f32[80,640]{1,0:T(8,128)S(1)}, u32[]{:S(2)}, u32[]{:S(2)}) collective-permute-start(f32[80,640]{1,0:T(8,128)} %get-tuple-element.23), channel_id=1, source_target_pairs={{0,64},{32,96},{64,0},{96,32},{1,65},{33,97},{65,1},{97,33},{2,66}... | collective-permute-start | bytes 614408 | tf_op jit(solution)/shard_map/ppermute | solution.py:226
  160.9 3.6 %collective-permute-done.17.refs_1_ = f32[80,640]{1,0:T(8,128)S(1)} collective-permute-done((f32[80,640]{1,0:T(8,128)}, f32[80,640]{1,0:T(8,128)S(1)}, u32[]{:S(2)}, u32[]{:S(2)}) %collective-permute-start.17) | collective-permute-done | bytes 204832 | tf_op jit(solution)/shard_map/ppermute | solution.py:226
  166.9 3.2 %collective-permute-done.19.refs_3_ = f32[80,640]{1,0:T(8,128)S(1)} collective-permute-done((f32[80,640]{1,0:T(8,128)}, f32[80,640]{1,0:T(8,128)S(1)}, u32[]{:S(2)}, u32[]{:S(2)}) %collective-permute-start.19) | collective-permute-done | bytes 204832 | tf_op jit(solution)/shard_map/ppermute | solution.py:226
  (79 shorter events, 40.2 us)
Async XLA Ops:
  2.2 19.2 %all-to-all-start = ((bf16[8,160,224]{2,1,0:T(8,128)(2,1)}), bf16[8,160,224]{2,1,0:T(8,128)(2,1)S(1)}, u32[]{:S(2)}, u32[]{:S(2)}) async-start(bf16[8,160,224]{2,1,0:T(8,128)(2,1)} %shard_map.46), calls=%async_computation | async-start | bytes 1310720 | tf_op jit(solution)/shard_map/all_to_all | solution.py:212
  7.1 11.0 %collective-permute-start.12 = (bf16[4,16,640]{2,1,0:T(8,128)(2,1)S(1)}, bf16[4,16,640]{2,1,0:T(8,128)(2,1)S(1)}, u32[]{:S(2)}, u32[]{:S(2)}) collective-permute-start(bf16[4,16,640]{2,1,0:T(8,128)(2,1)S(1)} %copy-done.21), channel_id=1, source_target_pairs={{0,384},{128,0},{256,128},{384,256},{1,385},{129,1},{257,129},{385... | collective-permute-start | bytes 245768 | tf_op jit(solution)/shard_map/ppermute | solution.py:203
  10.0 8.1 %collective-permute-start.10 = (bf16[4,16,640]{2,1,0:T(8,128)(2,1)S(1)}, bf16[4,16,640]{2,1,0:T(8,128)(2,1)S(1)}, u32[]{:S(2)}, u32[]{:S(2)}) collective-permute-start(bf16[4,16,640]{2,1,0:T(8,128)(2,1)S(1)} %copy-done.21), channel_id=1, source_target_pairs={{0,128},{128,256},{256,384},{384,0},{1,129},{129,257},{257,385},{3... | collective-permute-start | bytes 245768 | tf_op jit(solution)/shard_map/ppermute | solution.py:203
  13.0 7.6 %collective-permute-start.11 = (bf16[4,16,640]{2,1,0:T(8,128)(2,1)S(1)}, bf16[4,16,640]{2,1,0:T(8,128)(2,1)S(1)}, u32[]{:S(2)}, u32[]{:S(2)}) collective-permute-start(bf16[4,16,640]{2,1,0:T(8,128)(2,1)S(1)} %copy-done.21), channel_id=1, source_target_pairs={{0,256},{128,384},{256,0},{384,128},{1,257},{129,385},{257,1},{385... | collective-permute-start | bytes 245768 | tf_op jit(solution)/shard_map/ppermute | solution.py:203
  21.4 11.3 %all-to-all-start.3 = ((bf16[4,4,16,640]{3,2,1,0:T(8,128)(2,1)}), bf16[4,4,16,640]{3,2,1,0:T(8,128)(2,1)S(1)}, u32[]{:S(2)}, u32[]{:S(2)}) async-start(bf16[4,4,16,640]{3,2,1,0:T(8,128)(2,1)} %pad_maximum_fusion.1), calls=%async_computation.3 | async-start | bytes 655360 | tf_op jit(solution)/shard_map/all_to_all | solution.py:204
  32.7 29.1 %all-to-all-start.1 = ((bf16[8,320,224]{2,1,0:T(8,128)(2,1)}), bf16[8,320,224]{2,1,0:T(8,128)(2,1)S(1)}, u32[]{:S(2)}, u32[]{:S(2)}) async-start(bf16[8,320,224]{2,1,0:T(8,128)(2,1)} %get-tuple-element.15), calls=%async_computation.1 | async-start | bytes 2621440 | tf_op jit(solution)/shard_map/all_to_all | solution.py:219
  36.4 8.7 %collective-permute-start = (bf16[224,640]{1,0:T(8,128)(2,1)S(1)}, bf16[224,640]{1,0:T(8,128)(2,1)S(1)}, u32[]{:S(2)}, u32[]{:S(2)}) collective-permute-start(bf16[224,640]{1,0:T(8,128)(2,1)S(1)} %copy-done.16), channel_id=1, source_target_pairs={{408,24},{409,25},{410,26},{411,27},{412,28},{413,29},{414,30},{41... | collective-permute-start | bytes 860168 | tf_op jit(solution)/shard_map/ppermute | solution.py:215
  37.1 12.5 %collective-permute-start.1 = (bf16[224,640]{1,0:T(8,128)(2,1)S(1)}, bf16[224,640]{1,0:T(8,128)(2,1)S(1)}, u32[]{:S(2)}, u32[]{:S(2)}) collective-permute-start(bf16[224,640]{1,0:T(8,128)(2,1)S(1)} %copy-done.16), channel_id=1, source_target_pairs={{272,16},{408,152},{273,17},{409,153},{274,18},{410,154},{275,19},... | collective-permute-start | bytes 860168 | tf_op jit(solution)/shard_map/ppermute | solution.py:215
  37.8 19.4 %collective-permute-start.2 = (bf16[224,640]{1,0:T(8,128)(2,1)S(1)}, bf16[224,640]{1,0:T(8,128)(2,1)}, u32[]{:S(2)}, u32[]{:S(2)}) collective-permute-start(bf16[224,640]{1,0:T(8,128)(2,1)S(1)} %copy-done.16), channel_id=1, source_target_pairs={{136,8},{272,144},{408,280},{137,9},{273,145},{409,281},{138,10},{... | collective-permute-start | bytes 860168 | tf_op jit(solution)/shard_map/ppermute | solution.py:215
  39.1 35.0 %collective-permute-start.13 = (bf16[256,640]{1,0:T(8,128)(2,1)S(1)}, bf16[256,640]{1,0:T(8,128)(2,1)S(1)}, u32[]{:S(2)}, u32[]{:S(2)}) collective-permute-start(bf16[256,640]{1,0:T(8,128)(2,1)S(1)} %bitcast.23), channel_id=1, source_target_pairs={{0,2},{2,4},{4,6},{6,0},{1,3},{3,5},{5,7},{7,1},{8,10},{10,12},{12... | collective-permute-start | bytes 983048 | tf_op jit(solution)/shard_map/ppermute | solution.py:187
  42.5 31.7 %collective-permute-start.14 = (bf16[256,640]{1,0:T(8,128)(2,1)S(1)}, bf16[256,640]{1,0:T(8,128)(2,1)S(1)}, u32[]{:S(2)}, u32[]{:S(2)}) collective-permute-start(bf16[256,640]{1,0:T(8,128)(2,1)S(1)} %bitcast.24), channel_id=1, source_target_pairs={{0,4},{2,6},{4,0},{6,2},{1,5},{3,7},{5,1},{7,3},{8,12},{10,14},{12... | collective-permute-start | bytes 983048 | tf_op jit(solution)/shard_map/ppermute | solution.py:187
  45.1 29.0 %collective-permute-start.15 = (bf16[256,640]{1,0:T(8,128)(2,1)S(1)}, bf16[256,640]{1,0:T(8,128)(2,1)S(1)}, u32[]{:S(2)}, u32[]{:S(2)}) collective-permute-start(bf16[256,640]{1,0:T(8,128)(2,1)S(1)} %bitcast.25), channel_id=1, source_target_pairs={{0,6},{2,0},{4,2},{6,4},{1,7},{3,1},{5,3},{7,5},{8,14},{10,8},{12,... | collective-permute-start | bytes 983048 | tf_op jit(solution)/shard_map/ppermute | solution.py:187
  58.3 3.5 %collective-permute-start.3 = (bf16[224,640]{1,0:T(8,128)(2,1)S(1)}, bf16[224,640]{1,0:T(8,128)(2,1)S(1)}, u32[]{:S(2)}, u32[]{:S(2)}) collective-permute-start(bf16[224,640]{1,0:T(8,128)(2,1)S(1)} %add_select_fusion.own_ref), channel_id=1, source_target_pairs={{0,1},{1,0},{2,3},{3,2},{4,5},{5,4},{6,7},{7,6},{8,9},{9,8},{10,11... | collective-permute-start | bytes 860168 | tf_op jit(solution)/shard_map/ppermute | solution.py:217
  66.7 103.3 %all-to-all-start.2 = ((bf16[16,80,640]{2,1,0:T(8,128)(2,1)}), bf16[16,80,640]{2,1,0:T(8,128)(2,1)S(1)}, u32[]{:S(2)}, u32[]{:S(2)}) async-start(bf16[16,80,640]{2,1,0:T(8,128)(2,1)} %bitcast.20), calls=%async_computation.2 | async-start | bytes 3276800 | tf_op jit(solution)/shard_map/all_to_all | solution.py:221
  77.7 68.0 %collective-permute-start.16 = (bf16[4,256,640]{2,1,0:T(8,128)(2,1)}, bf16[4,256,640]{2,1,0:T(8,128)(2,1)}, u32[]{:S(2)}, u32[]{:S(2)}) collective-permute-start(bf16[4,256,640]{2,1,0:T(8,128)(2,1)} %pad_maximum_fusion), channel_id=1, source_target_pairs={{0,1},{1,0},{2,3},{3,2},{4,5},{5,4},{6,7},{7,6},{8,9},{9,8},{10,11... | collective-permute-start | bytes 3932168 | tf_op jit(solution)/shard_map/ppermute | solution.py:189
  79.9 8.0 %collective-permute-start.4 = (bf16[80,2048]{1,0:T(8,128)(2,1)S(1)}, bf16[80,2048]{1,0:T(8,128)(2,1)S(1)}, u32[]{:S(2)}, u32[]{:S(2)}) collective-permute-start(bf16[80,2048]{1,0:T(8,128)(2,1)S(1)} %multiply_reduce_fusion), channel_id=1, source_target_pairs={{0,24},{1,25},{2,26},{3,27},{4,28},{5,29},{6,30},{7,31},{32,56},{3... | collective-permute-start | bytes 983048 | tf_op jit(solution)/shard_map/ppermute | solution.py:209
  80.6 7.3 %collective-permute-start.5 = (bf16[80,2048]{1,0:T(8,128)(2,1)S(1)}, bf16[80,2048]{1,0:T(8,128)(2,1)S(1)}, u32[]{:S(2)}, u32[]{:S(2)}) collective-permute-start(bf16[80,2048]{1,0:T(8,128)(2,1)S(1)} %multiply_reduce_fusion), channel_id=1, source_target_pairs={{0,16},{8,24},{136,152},{1,17},{9,25},{137,153},{2,18},{10,26},{13... | collective-permute-start | bytes 983048 | tf_op jit(solution)/shard_map/ppermute | solution.py:209
  81.3 37.6 %collective-permute-start.6 = (bf16[80,2048]{1,0:T(8,128)(2,1)S(1)}, bf16[80,2048]{1,0:T(8,128)(2,1)S(1)}, u32[]{:S(2)}, u32[]{:S(2)}) collective-permute-start(bf16[80,2048]{1,0:T(8,128)(2,1)S(1)} %multiply_reduce_fusion), channel_id=1, source_target_pairs={{0,8},{8,16},{16,24},{136,144},{144,152},{272,280},{1,9},{9,17},{1... | collective-permute-start | bytes 983048 | tf_op jit(solution)/shard_map/ppermute | solution.py:209
  123.1 13.0 %collective-permute-start.7 = (bf16[80,2048]{1,0:T(8,128)(2,1)}, bf16[80,2048]{1,0:T(8,128)(2,1)S(1)}, u32[]{:S(2)}, u32[]{:S(2)}) collective-permute-start(bf16[80,2048]{1,0:T(8,128)(2,1)} %get-tuple-element.18), channel_id=1, source_target_pairs={{0,32},{32,64},{64,96},{96,0},{1,33},{33,65},{65,97},{97,1},{2,34}... | collective-permute-start | bytes 983048 | tf_op jit(solution)/shard_map/ppermute | solution.py:224
  126.4 17.5 %collective-permute-start.8 = (bf16[80,2048]{1,0:T(8,128)(2,1)}, bf16[80,2048]{1,0:T(8,128)(2,1)S(1)}, u32[]{:S(2)}, u32[]{:S(2)}) collective-permute-start(bf16[80,2048]{1,0:T(8,128)(2,1)} %get-tuple-element.19), channel_id=1, source_target_pairs={{0,64},{32,96},{64,0},{96,32},{1,65},{33,97},{65,1},{97,33},{2,66}... | collective-permute-start | bytes 983048 | tf_op jit(solution)/shard_map/ppermute | solution.py:224
  131.0 14.6 %collective-permute-start.9 = (bf16[80,2048]{1,0:T(8,128)(2,1)}, bf16[80,2048]{1,0:T(8,128)(2,1)S(1)}, u32[]{:S(2)}, u32[]{:S(2)}) collective-permute-start(bf16[80,2048]{1,0:T(8,128)(2,1)} %get-tuple-element.20), channel_id=1, source_target_pairs={{0,96},{32,0},{64,32},{96,64},{1,97},{33,1},{65,33},{97,65},{2,98}... | collective-permute-start | bytes 983048 | tf_op jit(solution)/shard_map/ppermute | solution.py:224
  150.8 13.8 %collective-permute-start.17 = (f32[80,640]{1,0:T(8,128)}, f32[80,640]{1,0:T(8,128)S(1)}, u32[]{:S(2)}, u32[]{:S(2)}) collective-permute-start(f32[80,640]{1,0:T(8,128)} %get-tuple-element.22), channel_id=1, source_target_pairs={{0,96},{32,0},{64,32},{96,64},{1,97},{33,1},{65,33},{97,65},{2,98}... | collective-permute-start | bytes 614408 | tf_op jit(solution)/shard_map/ppermute | solution.py:226
  155.3 11.6 %collective-permute-start.18 = (f32[80,640]{1,0:T(8,128)}, f32[80,640]{1,0:T(8,128)S(1)}, u32[]{:S(2)}, u32[]{:S(2)}) collective-permute-start(f32[80,640]{1,0:T(8,128)} %get-tuple-element.23), channel_id=1, source_target_pairs={{0,64},{32,96},{64,0},{96,32},{1,65},{33,97},{65,1},{97,33},{2,66}... | collective-permute-start | bytes 614408 | tf_op jit(solution)/shard_map/ppermute | solution.py:226
  159.0 11.0 %collective-permute-start.19 = (f32[80,640]{1,0:T(8,128)}, f32[80,640]{1,0:T(8,128)S(1)}, u32[]{:S(2)}, u32[]{:S(2)}) collective-permute-start(f32[80,640]{1,0:T(8,128)} %get-tuple-element.24), channel_id=1, source_target_pairs={{0,32},{32,64},{64,96},{96,0},{1,33},{33,65},{65,97},{97,1},{2,34}... | collective-permute-start | bytes 614408 | tf_op jit(solution)/shard_map/ppermute | solution.py:226
  (22 other events, 156.0 us)

commit v7 on v5

--- a/solution.py
+++ b/solution.py
@@ -102,14 +102,19 @@
         out_ref[q] = part.astype(out_ref.dtype)
 
 
-def weigh_kernel(scale, gram_ref, *refs):
+def add_kernel(scale, gram_ref, out_ref):
+    for layer in range(gram_ref.shape[0]):
+        gram = gram_ref[layer, 0].astype(jnp.float32)
+        for row in range(1, gram_ref.shape[1]):
+            gram += gram_ref[layer, row].astype(jnp.float32)
+        out_ref[layer] = gram * scale
+
+
+def weigh_kernel(gram_ref, *refs):
     virtual_refs, out_ref = refs[:-1], refs[-1]
     for r in range(X):
         layer = (lax.axis_index("x") + r) % X
-        gram = gram_ref[layer, 0].astype(jnp.float32)
-        for row in range(1, Y):
-            gram += gram_ref[layer, row].astype(jnp.float32)
-        out_ref[layer] = virtual_refs[r][...] * (gram * scale)
+        out_ref[layer] = virtual_refs[r][...] * gram_ref[layer]
 
 
 VMEM = pl.BlockSpec(memory_space=pltpu.VMEM)
@@ -179,11 +184,21 @@
     )(window, own, other)
 
 
-def weigh(gram, virtual, token_count):
-    return pl.pallas_call(
-        functools.partial(weigh_kernel, 1.0 / token_count),
-        out_shape=jax.ShapeDtypeStruct((X,) + virtual[0].shape, jnp.float32),
-        in_specs=[VMEM] + [VMEM] * len(virtual),
+def added(gram, token_count):
+    layers, _, height, width = gram.shape
+    return pl.pallas_call(
+        functools.partial(add_kernel, 1.0 / token_count),
+        out_shape=jax.ShapeDtypeStruct((layers, height, width), jnp.float32),
+        in_specs=[VMEM],
+        out_specs=VMEM,
+    )(gram)
+
+
+def weigh(gram, virtual):
+    return pl.pallas_call(
+        weigh_kernel,
+        out_shape=jax.ShapeDtypeStruct(gram.shape, jnp.float32),
+        in_specs=[VMEM] * (len(virtual) + 1),
         out_specs=VMEM,
     )(gram, *virtual)
 
@@ -231,10 +246,12 @@
     partial = lax.all_to_all(partial, ("x", "y"), 0, 0, tiled=True).reshape(X, Y, height, fw)
 
     pieces = prefix_of(earlier, decoders[0])
-    moved = [lax.ppermute(pieces[k], "x", ring(X, k)) for k in range(1, X)]
+    moved = [lax.ppermute(pieces[k], "x", ring(X, k)) for k in range(1, X - 1)]
+    moved.append(lax.ppermute(pieces[X - 1], "x", ring(X, X - 1)))
     virtual = virtual_of([pieces[0]] + moved, encoder_own, encoder_other)
     virtual = [virtual[0]] + [lax.ppermute(virtual[k], "x", ring(X, X - k)) for k in range(1, X)]
-    return weigh(partial, virtual, token_count)[None]
+    gram = added(partial, token_count)
+    return weigh(gram, virtual)[None]
 
 
 def solution(mesh):

time: 172 us -> 172 us (level)
  waiting for transfers between devices: 78.2 us -> 74.5 us
  Pallas kernels: 21.5 us -> 23.7 us
    ppermute x3, waiting for transfers between devices: 9.09 us -> 5.35 us  [per_device(): lax.ppermute(virtual[k], 'x', ring(X, X - k))]
    pallas_call x1 -> x2, Pallas kernels: 2.82 us -> 4.98 us  [the longest x1 2.54 us: added(): pl.pallas_call(functools.partial(add_kernel, 1.0 / token_count), out_shap...]
  transfers between devices with their start and end apart: 21 -> 21, of which waited for: 11 -> 10; matrix products, arithmetic and copies ran while one was open for 2% -> 2% of each run, Pallas kernels for 10% -> 11%
where the time goes in v7:
time: 172 us; the launch traced here: 171 us
  waiting for transfers between devices  74.5 us (43%)
  starting transfers between devices  62 us (36%)
  Pallas kernels  23.7 us (14%)
  local copies, waits for them, and re-layouts  6.32 us (4%)
  other arithmetic  4 us (2%)
    ppermute x1, waiting for transfers between devices, per_device(): earlier = [lax.ppermute(total, ('zlo', 'tgt'), total_pairs(1))]  29.3 us
    ppermute x3, waiting for transfers between devices, per_device(): lax.ppermute(columns, ('zlo', 'tgt'), window_pairs(k))  11.8 us
    ppermute x3, starting transfers between devices, per_device(): lax.ppermute(virtual[k], 'x', ring(X, X - k))  10.1 us
    ppermute x2, waiting for transfers between devices, per_device(): moved = [lax.ppermute(pieces[k], 'x', ring(X, k)) for k in range(1, X - 1)]  9.58 us
    ppermute x3, starting transfers between devices, over_feat(): others = [lax.ppermute(piece, 'y', ring(Y, k)) for k in range(1, Y)]  9.21 us
    all_to_all x1, waiting for transfers between devices, per_device(): lax.all_to_all(by_tokens, FEAT, 0, 0, tiled=True)  8.59 us
    ppermute x2, starting transfers between devices, per_device(): moved = [lax.ppermute(pieces[k], 'x', ring(X, k)) for k in range(1, X - 1)]  7.95 us
    all_to_all x1, starting transfers between devices, per_device(): lax.all_to_all(spread, ('zlo', 'x'), 0, 0, tiled=True).reshape(-1, fw)  7.13 us
  transfers between devices with their start and end apart: 21, of which 10 were waited for; matrix products, arithmetic and copies ran while one was open for 2% of the time, Pallas kernels for 11%

profile of v7, /device:TPU:456, one launch (start us, length us, event | category | flops | bytes accessed | tf_op | source)
XLA Modules:
  0.0 170.9 jit_solution(14448915394983958435)
XLA Ops:
  2.2 4.9 %all-to-all-start = ((bf16[8,160,224]{2,1,0:T(8,128)(2,1)}), bf16[8,160,224]{2,1,0:T(8,128)(2,1)S(1)}, u32[]{:S(2)}, u32[]{:S(2)}) async-start(bf16[8,160,224]{2,1,0:T(8,128)(2,1)} %shard_map.46), calls=%async_computation | async-start | bytes 1310720 | tf_op jit(solution)/shard_map/all_to_all | solution.py:237
  8.8 8.6 %all-to-all-done = bf16[8,160,224]{2,1,0:T(8,128)(2,1)S(1)} async-done(((bf16[8,160,224]{2,1,0:T(8,128)(2,1)}), bf16[8,160,224]{2,1,0:T(8,128)(2,1)S(1)}, u32[]{:S(2)}, u32[]{:S(2)}) %all-to-all-start) | async-done | bytes 573472 | tf_op jit(solution)/shard_map/all_to_all | solution.py:237
  17.4 7.1 %all-to-all-start.3 = ((bf16[16,16,640]{2,1,0:T(8,128)(2,1)}), bf16[16,16,640]{2,1,0:T(8,128)(2,1)S(1)}, u32[]{:S(2)}, u32[]{:S(2)}) async-start(bf16[16,16,640]{2,1,0:T(8,128)(2,1)} %shard_map.51), calls=%async_computation.3 | async-start | bytes 655360 | tf_op jit(solution)/shard_map/all_to_all | solution.py:228
  24.5 3.3 %shard_map.47 = (bf16[224,640]{1,0:T(8,128)(2,1)}, bf16[8,320,224]{2,1,0:T(8,128)(2,1)}) custom-call(s32[16,640]{1,0:T(8,128)} %ids_ref.1, bf16[1280,224]{1,0:T(8,128)(2,1)} %bitcast.24), custom_call_target="tpu_custom_call" | custom-call | tf_op jit(solution)/shard_map/pallas_call | solution.py:135
  27.8 6.7 %all-to-all-done.3 = bf16[16,16,640]{2,1,0:T(8,128)(2,1)S(1)} async-done(((bf16[16,16,640]{2,1,0:T(8,128)(2,1)}), bf16[16,16,640]{2,1,0:T(8,128)(2,1)S(1)}, u32[]{:S(2)}, u32[]{:S(2)}) %all-to-all-start.3) | async-done | bytes 327712 | tf_op jit(solution)/shard_map/all_to_all | solution.py:228
  34.5 3.7 %all-to-all-start.1 = ((bf16[8,320,224]{2,1,0:T(8,128)(2,1)}), bf16[8,320,224]{2,1,0:T(8,128)(2,1)S(1)}, u32[]{:S(2)}, u32[]{:S(2)}) async-start(bf16[8,320,224]{2,1,0:T(8,128)(2,1)} %get-tuple-element.15), calls=%async_computation.1 | async-start | bytes 2621440 | tf_op jit(solution)/shard_map/all_to_all | solution.py:244
  40.9 3.4 %collective-permute-start.11 = (bf16[256,640]{1,0:T(8,128)(2,1)S(1)}, bf16[256,640]{1,0:T(8,128)(2,1)S(1)}, u32[]{:S(2)}, u32[]{:S(2)}) collective-permute-start(bf16[256,640]{1,0:T(8,128)(2,1)S(1)} %bitcast.19), channel_id=1, source_target_pairs={{0,4},{2,6},{4,0},{6,2},{1,5},{3,7},{5,1},{7,3},{8,12},{10,14},{12... | collective-permute-start | bytes 983048 | tf_op jit(solution)/shard_map/ppermute | solution.py:211
  44.3 2.7 %collective-permute-start.12 = (bf16[256,640]{1,0:T(8,128)(2,1)S(1)}, bf16[256,640]{1,0:T(8,128)(2,1)S(1)}, u32[]{:S(2)}, u32[]{:S(2)}) collective-permute-start(bf16[256,640]{1,0:T(8,128)(2,1)S(1)} %bitcast.20), channel_id=1, source_target_pairs={{0,6},{2,0},{4,2},{6,4},{1,7},{3,1},{5,3},{7,5},{8,14},{10,8},{12,... | collective-permute-start | bytes 983048 | tf_op jit(solution)/shard_map/ppermute | solution.py:211
  47.0 3.2 %collective-permute-start.10 = (bf16[256,640]{1,0:T(8,128)(2,1)S(1)}, bf16[256,640]{1,0:T(8,128)(2,1)S(1)}, u32[]{:S(2)}, u32[]{:S(2)}) collective-permute-start(bf16[256,640]{1,0:T(8,128)(2,1)S(1)} %bitcast.21), channel_id=1, source_target_pairs={{0,2},{2,4},{4,6},{6,0},{1,3},{3,5},{5,7},{7,1},{8,10},{10,12},{12... | collective-permute-start | bytes 983048 | tf_op jit(solution)/shard_map/ppermute | solution.py:211
  50.9 11.8 %collective-permute-done.2 = bf16[224,640]{1,0:T(8,128)(2,1)} collective-permute-done((bf16[224,640]{1,0:T(8,128)(2,1)S(1)}, bf16[224,640]{1,0:T(8,128)(2,1)}, u32[]{:S(2)}, u32[]{:S(2)}) %collective-permute-start.2) | collective-permute-done | bytes 286752 | tf_op jit(solution)/shard_map/ppermute | solution.py:240
  68.5 3.8 %shard_map.48 = bf16[4,320,640]{2,1,0:T(8,128)(2,1)} custom-call(bf16[4,2,320,224]{3,2,1,0:T(8,128)(2,1)} %bitcast.17, bf16[224,640]{1,0:T(8,128)(2,1)} %copy-done.8, bf16[224,640]{1,0:T(8,128)(2,1)} %copy-done.15), custom_call_target="tpu_custom_call" | custom-call | tf_op jit(solution)/shard_map/pallas_call | solution.py:179
  72.3 6.5 %all-to-all-start.2 = ((bf16[16,80,640]{2,1,0:T(8,128)(2,1)}), bf16[16,80,640]{2,1,0:T(8,128)(2,1)S(1)}, u32[]{:S(2)}, u32[]{:S(2)}) async-start(bf16[16,80,640]{2,1,0:T(8,128)(2,1)} %bitcast.16), calls=%async_computation.2 | async-start | bytes 3276800 | tf_op jit(solution)/shard_map/all_to_all | solution.py:246
  79.8 2.5 %pad_maximum_fusion = bf16[4,256,640]{2,1,0:T(8,128)(2,1)} fusion(bf16[1,256,640]{2,1,0:T(8,128)(2,1)} %bitcast.26, bf16[1,256,640]{2,1,0:T(8,128)(2,1)} %bitcast.25, bf16[1,256,640]{2,1,0:T(8,128)(2,1)} %bitcast.27, bf16[1,256,640]{2,1,0:T(8,128)(2,1)S(1)} %bitcast.22), kind=kLoop, calls=%fused_computation.1 | loop fusion | flops 1966080 | bytes 2621440 | tf_op jit(solution)/shard_map/stack | solution.py:213
  87.3 29.3 %collective-permute-done.4.refs_0_ = bf16[80,2048]{1,0:T(8,128)(2,1)S(1)} collective-permute-done((bf16[80,2048]{1,0:T(8,128)(2,1)S(1)}, bf16[80,2048]{1,0:T(8,128)(2,1)S(1)}, u32[]{:S(2)}, u32[]{:S(2)}) %collective-permute-start.4) | collective-permute-done | bytes 327712 | tf_op jit(solution)/shard_map/ppermute | solution.py:233
  117.5 3.4 %shard_map.50 = (bf16[80,2048]{1,0:T(8,128)(2,1)}, bf16[80,2048]{1,0:T(8,128)(2,1)}, bf16[80,2048]{1,0:T(8,128)(2,1)}, bf16[80,2048]{1,0:T(8,128)(2,1)}) custom-call(bf16[80,2048]{1,0:T(8,128)(2,1)} %copy-done.9, bf16[80,2048]{1,0:T(8,128)(2,1)} %copy-done.10, bf16[80,2048]{1,0:T(8,128)(2,1)} %copy-done.11, bf16[4,80,2048]{2,1,0:T(8,128)(2,1)} %bitcast.18), custom_call_target="tpu_custom_call" | custom-call | tf_op jit(solution)/shard_map/pallas_call | solution.py:157
  120.8 3.4 %collective-permute-start.7 = (bf16[80,2048]{1,0:T(8,128)(2,1)}, bf16[80,2048]{1,0:T(8,128)(2,1)S(1)}, u32[]{:S(2)}, u32[]{:S(2)}) collective-permute-start(bf16[80,2048]{1,0:T(8,128)(2,1)} %get-tuple-element.18), channel_id=1, source_target_pairs={{0,32},{32,64},{64,96},{96,0},{1,33},{33,65},{65,97},{97,1},{2,34}... | collective-permute-start | bytes 983048 | tf_op jit(solution)/shard_map/ppermute | solution.py:249
  124.2 4.6 %collective-permute-start.8 = (bf16[80,2048]{1,0:T(8,128)(2,1)}, bf16[80,2048]{1,0:T(8,128)(2,1)S(1)}, u32[]{:S(2)}, u32[]{:S(2)}) collective-permute-start(bf16[80,2048]{1,0:T(8,128)(2,1)} %get-tuple-element.19), channel_id=1, source_target_pairs={{0,64},{32,96},{64,0},{96,32},{1,65},{33,97},{65,1},{97,33},{2,66}... | collective-permute-start | bytes 983048 | tf_op jit(solution)/shard_map/ppermute | solution.py:249
  128.8 3.4 %collective-permute-start.9 = (bf16[80,2048]{1,0:T(8,128)(2,1)}, bf16[80,2048]{1,0:T(8,128)(2,1)S(1)}, u32[]{:S(2)}, u32[]{:S(2)}) collective-permute-start(bf16[80,2048]{1,0:T(8,128)(2,1)} %get-tuple-element.20), channel_id=1, source_target_pairs={{0,96},{32,0},{64,32},{96,64},{1,97},{33,1},{65,33},{97,65},{2,98}... | collective-permute-start | bytes 983048 | tf_op jit(solution)/shard_map/ppermute | solution.py:250
  133.8 7.9 %collective-permute-done.8.refs_2_ = bf16[80,2048]{1,0:T(8,128)(2,1)S(1)} collective-permute-done((bf16[80,2048]{1,0:T(8,128)(2,1)}, bf16[80,2048]{1,0:T(8,128)(2,1)S(1)}, u32[]{:S(2)}, u32[]{:S(2)}) %collective-permute-start.8) | collective-permute-done | bytes 327712 | tf_op jit(solution)/shard_map/ppermute | solution.py:249
  144.1 4.4 %shard_map.52 = (f32[80,640]{1,0:T(8,128)}, f32[80,640]{1,0:T(8,128)}, f32[80,640]{1,0:T(8,128)}, f32[80,640]{1,0:T(8,128)}) custom-call(bf16[80,2048]{1,0:T(8,128)(2,1)} %get-tuple-element.17.refs_0_, bf16[80,2048]{1,0:T(8,128)(2,1)} %copy-done.12, bf16[80,2048]{1,0:T(8,128)(2,1)} %copy-done.13, bf16[80,2048]{1,0:T(8,128)(2,1)} %copy-done.14, ...), custom_call_target="tpu_custom_call" | custom-call | tf_op jit(solution)/shard_map/pallas_call | solution.py:169
  148.5 4.5 %collective-permute-start.14 = (f32[80,640]{1,0:T(8,128)}, f32[80,640]{1,0:T(8,128)S(1)}, u32[]{:S(2)}, u32[]{:S(2)}) collective-permute-start(f32[80,640]{1,0:T(8,128)} %get-tuple-element.22), channel_id=1, source_target_pairs={{0,96},{32,0},{64,32},{96,64},{1,97},{33,1},{65,33},{97,65},{2,98}... | collective-permute-start | bytes 614408 | tf_op jit(solution)/shard_map/ppermute | solution.py:252
  153.0 3.7 %collective-permute-start.15 = (f32[80,640]{1,0:T(8,128)}, f32[80,640]{1,0:T(8,128)S(1)}, u32[]{:S(2)}, u32[]{:S(2)}) collective-permute-start(f32[80,640]{1,0:T(8,128)} %get-tuple-element.23), channel_id=1, source_target_pairs={{0,64},{32,96},{64,0},{96,32},{1,65},{33,97},{65,1},{97,33},{2,66}... | collective-permute-start | bytes 614408 | tf_op jit(solution)/shard_map/ppermute | solution.py:252
  159.8 2.5 %shard_map.49.gram_ref = f32[4,80,640]{2,1,0:T(8,128)} custom-call(bf16[4,4,80,640]{3,2,1,0:T(8,128)(2,1)} %bitcast.15), custom_call_target="tpu_custom_call" | custom-call | tf_op jit(solution)/shard_map/pallas_call | solution.py:189
  164.6 3.2 %collective-permute-done.16.refs_3_ = f32[80,640]{1,0:T(8,128)S(1)} collective-permute-done((f32[80,640]{1,0:T(8,128)}, f32[80,640]{1,0:T(8,128)S(1)}, u32[]{:S(2)}, u32[]{:S(2)}) %collective-permute-start.16) | collective-permute-done | bytes 204832 | tf_op jit(solution)/shard_map/ppermute | solution.py:252
  (72 shorter events, 32.2 us)
Async XLA Ops:
  2.2 15.2 %all-to-all-start = ((bf16[8,160,224]{2,1,0:T(8,128)(2,1)}), bf16[8,160,224]{2,1,0:T(8,128)(2,1)S(1)}, u32[]{:S(2)}, u32[]{:S(2)}) async-start(bf16[8,160,224]{2,1,0:T(8,128)(2,1)} %shard_map.46), calls=%async_computation | async-start | bytes 1310720 | tf_op jit(solution)/shard_map/all_to_all | solution.py:237
  17.4 7.1 %copy-start.4 = (bf16[8,160,224]{2,1,0:T(8,128)(2,1)}, bf16[8,160,224]{2,1,0:T(8,128)(2,1)S(1)}, u32[]{:S(2)}) copy-start(bf16[8,160,224]{2,1,0:T(8,128)(2,1)S(1)} %all-to-all-done) | copy-start | bytes 1720324
  17.4 17.1 %all-to-all-start.3 = ((bf16[16,16,640]{2,1,0:T(8,128)(2,1)}), bf16[16,16,640]{2,1,0:T(8,128)(2,1)S(1)}, u32[]{:S(2)}, u32[]{:S(2)}) async-start(bf16[16,16,640]{2,1,0:T(8,128)(2,1)} %shard_map.51), calls=%async_computation.3 | async-start | bytes 655360 | tf_op jit(solution)/shard_map/all_to_all | solution.py:228
  34.5 45.3 %copy-start.3 = (bf16[16,16,640]{2,1,0:T(8,128)(2,1)}, bf16[16,16,640]{2,1,0:T(8,128)(2,1)S(1)}, u32[]{:S(2)}) copy-start(bf16[16,16,640]{2,1,0:T(8,128)(2,1)S(1)} %all-to-all-done.3) | copy-start | bytes 983044
  34.5 32.8 %all-to-all-start.1 = ((bf16[8,320,224]{2,1,0:T(8,128)(2,1)}), bf16[8,320,224]{2,1,0:T(8,128)(2,1)S(1)}, u32[]{:S(2)}, u32[]{:S(2)}) async-start(bf16[8,320,224]{2,1,0:T(8,128)(2,1)} %get-tuple-element.15), calls=%async_computation.1 | async-start | bytes 2621440 | tf_op jit(solution)/shard_map/all_to_all | solution.py:244
  38.2 8.8 %collective-permute-start = (bf16[224,640]{1,0:T(8,128)(2,1)S(1)}, bf16[224,640]{1,0:T(8,128)(2,1)S(1)}, u32[]{:S(2)}, u32[]{:S(2)}) collective-permute-start(bf16[224,640]{1,0:T(8,128)(2,1)S(1)} %copy-done.16), channel_id=1, source_target_pairs={{408,24},{409,25},{410,26},{411,27},{412,28},{413,29},{414,30},{41... | collective-permute-start | bytes 860168 | tf_op jit(solution)/shard_map/ppermute | solution.py:240
  38.9 11.2 %collective-permute-start.1 = (bf16[224,640]{1,0:T(8,128)(2,1)S(1)}, bf16[224,640]{1,0:T(8,128)(2,1)S(1)}, u32[]{:S(2)}, u32[]{:S(2)}) collective-permute-start(bf16[224,640]{1,0:T(8,128)(2,1)S(1)} %copy-done.16), channel_id=1, source_target_pairs={{272,16},{408,152},{273,17},{409,153},{274,18},{410,154},{275,19},... | collective-permute-start | bytes 860168 | tf_op jit(solution)/shard_map/ppermute | solution.py:240
  39.6 23.1 %collective-permute-start.2 = (bf16[224,640]{1,0:T(8,128)(2,1)S(1)}, bf16[224,640]{1,0:T(8,128)(2,1)}, u32[]{:S(2)}, u32[]{:S(2)}) collective-permute-start(bf16[224,640]{1,0:T(8,128)(2,1)S(1)} %copy-done.16), channel_id=1, source_target_pairs={{136,8},{272,144},{408,280},{137,9},{273,145},{409,281},{138,10},{... | collective-permute-start | bytes 860168 | tf_op jit(solution)/shard_map/ppermute | solution.py:240
  40.9 37.9 %collective-permute-start.11 = (bf16[256,640]{1,0:T(8,128)(2,1)S(1)}, bf16[256,640]{1,0:T(8,128)(2,1)S(1)}, u32[]{:S(2)}, u32[]{:S(2)}) collective-permute-start(bf16[256,640]{1,0:T(8,128)(2,1)S(1)} %bitcast.19), channel_id=1, source_target_pairs={{0,4},{2,6},{4,0},{6,2},{1,5},{3,7},{5,1},{7,3},{8,12},{10,14},{12... | collective-permute-start | bytes 983048 | tf_op jit(solution)/shard_map/ppermute | solution.py:211
  44.3 34.5 %collective-permute-start.12 = (bf16[256,640]{1,0:T(8,128)(2,1)S(1)}, bf16[256,640]{1,0:T(8,128)(2,1)S(1)}, u32[]{:S(2)}, u32[]{:S(2)}) collective-permute-start(bf16[256,640]{1,0:T(8,128)(2,1)S(1)} %bitcast.20), channel_id=1, source_target_pairs={{0,6},{2,0},{4,2},{6,4},{1,7},{3,1},{5,3},{7,5},{8,14},{10,8},{12,... | collective-permute-start | bytes 983048 | tf_op jit(solution)/shard_map/ppermute | solution.py:211
  47.0 31.9 %collective-permute-start.10 = (bf16[256,640]{1,0:T(8,128)(2,1)S(1)}, bf16[256,640]{1,0:T(8,128)(2,1)S(1)}, u32[]{:S(2)}, u32[]{:S(2)}) collective-permute-start(bf16[256,640]{1,0:T(8,128)(2,1)S(1)} %bitcast.21), channel_id=1, source_target_pairs={{0,2},{2,4},{4,6},{6,0},{1,3},{3,5},{5,7},{7,1},{8,10},{10,12},{12... | collective-permute-start | bytes 983048 | tf_op jit(solution)/shard_map/ppermute | solution.py:211
  63.9 3.5 %collective-permute-start.3 = (bf16[224,640]{1,0:T(8,128)(2,1)S(1)}, bf16[224,640]{1,0:T(8,128)(2,1)S(1)}, u32[]{:S(2)}, u32[]{:S(2)}) collective-permute-start(bf16[224,640]{1,0:T(8,128)(2,1)S(1)} %add_select_fusion.own_ref), channel_id=1, source_target_pairs={{0,1},{1,0},{2,3},{3,2},{4,5},{5,4},{6,7},{7,6},{8,9},{9,8},{10,11... | collective-permute-start | bytes 860168 | tf_op jit(solution)/shard_map/ppermute | solution.py:242
  72.3 86.3 %all-to-all-start.2 = ((bf16[16,80,640]{2,1,0:T(8,128)(2,1)}), bf16[16,80,640]{2,1,0:T(8,128)(2,1)S(1)}, u32[]{:S(2)}, u32[]{:S(2)}) async-start(bf16[16,80,640]{2,1,0:T(8,128)(2,1)} %bitcast.16), calls=%async_computation.2 | async-start | bytes 3276800 | tf_op jit(solution)/shard_map/all_to_all | solution.py:246
  82.3 61.1 %collective-permute-start.13 = (bf16[4,256,640]{2,1,0:T(8,128)(2,1)}, bf16[4,256,640]{2,1,0:T(8,128)(2,1)}, u32[]{:S(2)}, u32[]{:S(2)}) collective-permute-start(bf16[4,256,640]{2,1,0:T(8,128)(2,1)} %pad_maximum_fusion), channel_id=1, source_target_pairs={{0,1},{1,0},{2,3},{3,2},{4,5},{5,4},{6,7},{7,6},{8,9},{9,8},{10,11... | collective-permute-start | bytes 3932168 | tf_op jit(solution)/shard_map/ppermute | solution.py:213
  84.6 31.9 %collective-permute-start.4 = (bf16[80,2048]{1,0:T(8,128)(2,1)S(1)}, bf16[80,2048]{1,0:T(8,128)(2,1)S(1)}, u32[]{:S(2)}, u32[]{:S(2)}) collective-permute-start(bf16[80,2048]{1,0:T(8,128)(2,1)S(1)} %multiply_reduce_fusion), channel_id=1, source_target_pairs={{0,8},{8,16},{16,24},{136,144},{144,152},{272,280},{1,9},{9,17},{1... | collective-permute-start | bytes 983048 | tf_op jit(solution)/shard_map/ppermute | solution.py:233
  85.9 30.6 %collective-permute-start.5 = (bf16[80,2048]{1,0:T(8,128)(2,1)S(1)}, bf16[80,2048]{1,0:T(8,128)(2,1)S(1)}, u32[]{:S(2)}, u32[]{:S(2)}) collective-permute-start(bf16[80,2048]{1,0:T(8,128)(2,1)S(1)} %multiply_reduce_fusion), channel_id=1, source_target_pairs={{0,16},{8,24},{136,152},{1,17},{9,25},{137,153},{2,18},{10,26},{13... | collective-permute-start | bytes 983048 | tf_op jit(solution)/shard_map/ppermute | solution.py:234
  86.6 30.0 %collective-permute-start.6 = (bf16[80,2048]{1,0:T(8,128)(2,1)S(1)}, bf16[80,2048]{1,0:T(8,128)(2,1)S(1)}, u32[]{:S(2)}, u32[]{:S(2)}) collective-permute-start(bf16[80,2048]{1,0:T(8,128)(2,1)S(1)} %multiply_reduce_fusion), channel_id=1, source_target_pairs={{0,24},{1,25},{2,26},{3,27},{4,28},{5,29},{6,30},{7,31},{32,56},{3... | collective-permute-start | bytes 983048 | tf_op jit(solution)/shard_map/ppermute | solution.py:234
  120.8 13.0 %collective-permute-start.7 = (bf16[80,2048]{1,0:T(8,128)(2,1)}, bf16[80,2048]{1,0:T(8,128)(2,1)S(1)}, u32[]{:S(2)}, u32[]{:S(2)}) collective-permute-start(bf16[80,2048]{1,0:T(8,128)(2,1)} %get-tuple-element.18), channel_id=1, source_target_pairs={{0,32},{32,64},{64,96},{96,0},{1,33},{33,65},{65,97},{97,1},{2,34}... | collective-permute-start | bytes 983048 | tf_op jit(solution)/shard_map/ppermute | solution.py:249
  124.2 17.5 %collective-permute-start.8 = (bf16[80,2048]{1,0:T(8,128)(2,1)}, bf16[80,2048]{1,0:T(8,128)(2,1)S(1)}, u32[]{:S(2)}, u32[]{:S(2)}) collective-permute-start(bf16[80,2048]{1,0:T(8,128)(2,1)} %get-tuple-element.19), channel_id=1, source_target_pairs={{0,64},{32,96},{64,0},{96,32},{1,65},{33,97},{65,1},{97,33},{2,66}... | collective-permute-start | bytes 983048 | tf_op jit(solution)/shard_map/ppermute | solution.py:249
  128.8 14.6 %collective-permute-start.9 = (bf16[80,2048]{1,0:T(8,128)(2,1)}, bf16[80,2048]{1,0:T(8,128)(2,1)S(1)}, u32[]{:S(2)}, u32[]{:S(2)}) collective-permute-start(bf16[80,2048]{1,0:T(8,128)(2,1)} %get-tuple-element.20), channel_id=1, source_target_pairs={{0,96},{32,0},{64,32},{96,64},{1,97},{33,1},{65,33},{97,65},{2,98}... | collective-permute-start | bytes 983048 | tf_op jit(solution)/shard_map/ppermute | solution.py:250
  133.8 9.6 %copy-start.12 = (bf16[80,2048]{1,0:T(8,128)(2,1)}, bf16[80,2048]{1,0:T(8,128)(2,1)S(1)}, u32[]{:S(2)}) copy-start(bf16[80,2048]{1,0:T(8,128)(2,1)S(1)} %collective-permute-done.7.refs_1_) | copy-start | bytes 983044
  148.5 13.9 %collective-permute-start.14 = (f32[80,640]{1,0:T(8,128)}, f32[80,640]{1,0:T(8,128)S(1)}, u32[]{:S(2)}, u32[]{:S(2)}) collective-permute-start(f32[80,640]{1,0:T(8,128)} %get-tuple-element.22), channel_id=1, source_target_pairs={{0,96},{32,0},{64,32},{96,64},{1,97},{33,1},{65,33},{97,65},{2,98}... | collective-permute-start | bytes 614408 | tf_op jit(solution)/shard_map/ppermute | solution.py:252
  153.0 11.6 %collective-permute-start.15 = (f32[80,640]{1,0:T(8,128)}, f32[80,640]{1,0:T(8,128)S(1)}, u32[]{:S(2)}, u32[]{:S(2)}) collective-permute-start(f32[80,640]{1,0:T(8,128)} %get-tuple-element.23), channel_id=1, source_target_pairs={{0,64},{32,96},{64,0},{96,32},{1,65},{33,97},{65,1},{97,33},{2,66}... | collective-permute-start | bytes 614408 | tf_op jit(solution)/shard_map/ppermute | solution.py:252
  156.7 11.0 %collective-permute-start.16 = (f32[80,640]{1,0:T(8,128)}, f32[80,640]{1,0:T(8,128)S(1)}, u32[]{:S(2)}, u32[]{:S(2)}) collective-permute-start(f32[80,640]{1,0:T(8,128)} %get-tuple-element.24), channel_id=1, source_target_pairs={{0,32},{32,64},{64,96},{96,0},{1,33},{33,65},{65,97},{97,1},{2,34}... | collective-permute-start | bytes 614408 | tf_op jit(solution)/shard_map/ppermute | solution.py:252
  (18 other events, 32.0 us)

commit v8 on v7

--- a/solution.py
+++ b/solution.py
@@ -246,10 +246,11 @@
     partial = lax.all_to_all(partial, ("x", "y"), 0, 0, tiled=True).reshape(X, Y, height, fw)
 
     pieces = prefix_of(earlier, decoders[0])
-    moved = [lax.ppermute(pieces[k], "x", ring(X, k)) for k in range(1, X - 1)]
-    moved.append(lax.ppermute(pieces[X - 1], "x", ring(X, X - 1)))
+    moved = [lax.ppermute(pieces[k], "x", ring(X, k)) for k in range(1, X)]
     virtual = virtual_of([pieces[0]] + moved, encoder_own, encoder_other)
-    virtual = [virtual[0]] + [lax.ppermute(virtual[k], "x", ring(X, X - k)) for k in range(1, X)]
+    far = lax.ppermute(virtual[2], "x", ring(X, X - 2))
+    near = [lax.ppermute(virtual[k], "x", ring(X, X - k)) for k in (1, 3)]
+    virtual = [virtual[0], near[0], far, near[1]]
     gram = added(partial, token_count)
     return weigh(gram, virtual)[None]
 

time: 172 us -> 172 us (level)
  no operation moved by 1% of the time
where the time goes in v8:
time: 172 us; the launch traced here: 171 us
  waiting for transfers between devices  74.5 us (43%)
  starting transfers between devices  62 us (36%)
  Pallas kernels  23.7 us (14%)
  local copies, waits for them, and re-layouts  6.32 us (4%)
  other arithmetic  4 us (2%)
    ppermute x1, waiting for transfers between devices, per_device(): earlier = [lax.ppermute(total, ('zlo', 'tgt'), total_pairs(1))]  29.3 us
    ppermute x3, waiting for transfers between devices, per_device(): lax.ppermute(columns, ('zlo', 'tgt'), window_pairs(k))  11.8 us
    ppermute x3, starting transfers between devices, per_device(): moved = [lax.ppermute(pieces[k], 'x', ring(X, k)) for k in range(1, X)]  11.3 us
    ppermute x3, waiting for transfers between devices, per_device(): moved = [lax.ppermute(pieces[k], 'x', ring(X, k)) for k in range(1, X)]  11.2 us
    ppermute x3, starting transfers between devices, over_feat(): others = [lax.ppermute(piece, 'y', ring(Y, k)) for k in range(1, Y)]  9.21 us
    all_to_all x1, waiting for transfers between devices, per_device(): lax.all_to_all(by_tokens, FEAT, 0, 0, tiled=True)  8.59 us
    all_to_all x1, starting transfers between devices, per_device(): lax.all_to_all(spread, ('zlo', 'x'), 0, 0, tiled=True).reshape(-1, fw)  7.13 us
    all_to_all x1, waiting for transfers between devices, per_device(): lax.all_to_all(spread, ('zlo', 'x'), 0, 0, tiled=True).reshape(-1, fw)  6.7 us
  transfers between devices with their start and end apart: 21, of which 10 were waited for; matrix products, arithmetic and copies ran while one was open for 2% of the time, Pallas kernels for 11%

profile of v8, /device:TPU:456, one launch (start us, length us, event | category | flops | bytes accessed | tf_op | source)
XLA Modules:
  0.0 170.9 jit_solution(14448915394983958435)
XLA Ops:
  2.2 4.9 %all-to-all-start = ((bf16[8,160,224]{2,1,0:T(8,128)(2,1)}), bf16[8,160,224]{2,1,0:T(8,128)(2,1)S(1)}, u32[]{:S(2)}, u32[]{:S(2)}) async-start(bf16[8,160,224]{2,1,0:T(8,128)(2,1)} %shard_map.46), calls=%async_computation | async-start | bytes 1310720 | tf_op jit(solution)/shard_map/all_to_all | solution.py:237
  8.8 8.6 %all-to-all-done = bf16[8,160,224]{2,1,0:T(8,128)(2,1)S(1)} async-done(((bf16[8,160,224]{2,1,0:T(8,128)(2,1)}), bf16[8,160,224]{2,1,0:T(8,128)(2,1)S(1)}, u32[]{:S(2)}, u32[]{:S(2)}) %all-to-all-start) | async-done | bytes 573472 | tf_op jit(solution)/shard_map/all_to_all | solution.py:237
  17.4 7.1 %all-to-all-start.3 = ((bf16[16,16,640]{2,1,0:T(8,128)(2,1)}), bf16[16,16,640]{2,1,0:T(8,128)(2,1)S(1)}, u32[]{:S(2)}, u32[]{:S(2)}) async-start(bf16[16,16,640]{2,1,0:T(8,128)(2,1)} %shard_map.51), calls=%async_computation.3 | async-start | bytes 655360 | tf_op jit(solution)/shard_map/all_to_all | solution.py:228
  24.5 3.3 %shard_map.47 = (bf16[224,640]{1,0:T(8,128)(2,1)}, bf16[8,320,224]{2,1,0:T(8,128)(2,1)}) custom-call(s32[16,640]{1,0:T(8,128)} %ids_ref.1, bf16[1280,224]{1,0:T(8,128)(2,1)} %bitcast.24), custom_call_target="tpu_custom_call" | custom-call | tf_op jit(solution)/shard_map/pallas_call | solution.py:135
  27.8 6.7 %all-to-all-done.3 = bf16[16,16,640]{2,1,0:T(8,128)(2,1)S(1)} async-done(((bf16[16,16,640]{2,1,0:T(8,128)(2,1)}), bf16[16,16,640]{2,1,0:T(8,128)(2,1)S(1)}, u32[]{:S(2)}, u32[]{:S(2)}) %all-to-all-start.3) | async-done | bytes 327712 | tf_op jit(solution)/shard_map/all_to_all | solution.py:228
  34.5 3.7 %all-to-all-start.1 = ((bf16[8,320,224]{2,1,0:T(8,128)(2,1)}), bf16[8,320,224]{2,1,0:T(8,128)(2,1)S(1)}, u32[]{:S(2)}, u32[]{:S(2)}) async-start(bf16[8,320,224]{2,1,0:T(8,128)(2,1)} %get-tuple-element.15), calls=%async_computation.1 | async-start | bytes 2621440 | tf_op jit(solution)/shard_map/all_to_all | solution.py:244
  40.9 3.4 %collective-permute-start.11 = (bf16[256,640]{1,0:T(8,128)(2,1)S(1)}, bf16[256,640]{1,0:T(8,128)(2,1)S(1)}, u32[]{:S(2)}, u32[]{:S(2)}) collective-permute-start(bf16[256,640]{1,0:T(8,128)(2,1)S(1)} %bitcast.19), channel_id=1, source_target_pairs={{0,4},{2,6},{4,0},{6,2},{1,5},{3,7},{5,1},{7,3},{8,12},{10,14},{12... | collective-permute-start | bytes 983048 | tf_op jit(solution)/shard_map/ppermute | solution.py:211
  44.3 2.7 %collective-permute-start.12 = (bf16[256,640]{1,0:T(8,128)(2,1)S(1)}, bf16[256,640]{1,0:T(8,128)(2,1)S(1)}, u32[]{:S(2)}, u32[]{:S(2)}) collective-permute-start(bf16[256,640]{1,0:T(8,128)(2,1)S(1)} %bitcast.20), channel_id=1, source_target_pairs={{0,6},{2,0},{4,2},{6,4},{1,7},{3,1},{5,3},{7,5},{8,14},{10,8},{12,... | collective-permute-start | bytes 983048 | tf_op jit(solution)/shard_map/ppermute | solution.py:211
  47.0 3.2 %collective-permute-start.10 = (bf16[256,640]{1,0:T(8,128)(2,1)S(1)}, bf16[256,640]{1,0:T(8,128)(2,1)S(1)}, u32[]{:S(2)}, u32[]{:S(2)}) collective-permute-start(bf16[256,640]{1,0:T(8,128)(2,1)S(1)} %bitcast.21), channel_id=1, source_target_pairs={{0,2},{2,4},{4,6},{6,0},{1,3},{3,5},{5,7},{7,1},{8,10},{10,12},{12... | collective-permute-start | bytes 983048 | tf_op jit(solution)/shard_map/ppermute | solution.py:211
  50.9 11.8 %collective-permute-done.2 = bf16[224,640]{1,0:T(8,128)(2,1)} collective-permute-done((bf16[224,640]{1,0:T(8,128)(2,1)S(1)}, bf16[224,640]{1,0:T(8,128)(2,1)}, u32[]{:S(2)}, u32[]{:S(2)}) %collective-permute-start.2) | collective-permute-done | bytes 286752 | tf_op jit(solution)/shard_map/ppermute | solution.py:240
  68.5 3.8 %shard_map.48 = bf16[4,320,640]{2,1,0:T(8,128)(2,1)} custom-call(bf16[4,2,320,224]{3,2,1,0:T(8,128)(2,1)} %bitcast.17, bf16[224,640]{1,0:T(8,128)(2,1)} %copy-done.8, bf16[224,640]{1,0:T(8,128)(2,1)} %copy-done.15), custom_call_target="tpu_custom_call" | custom-call | tf_op jit(solution)/shard_map/pallas_call | solution.py:179
  72.3 6.5 %all-to-all-start.2 = ((bf16[16,80,640]{2,1,0:T(8,128)(2,1)}), bf16[16,80,640]{2,1,0:T(8,128)(2,1)S(1)}, u32[]{:S(2)}, u32[]{:S(2)}) async-start(bf16[16,80,640]{2,1,0:T(8,128)(2,1)} %bitcast.16), calls=%async_computation.2 | async-start | bytes 3276800 | tf_op jit(solution)/shard_map/all_to_all | solution.py:246
  79.8 2.5 %pad_maximum_fusion = bf16[4,256,640]{2,1,0:T(8,128)(2,1)} fusion(bf16[1,256,640]{2,1,0:T(8,128)(2,1)} %bitcast.26, bf16[1,256,640]{2,1,0:T(8,128)(2,1)} %bitcast.25, bf16[1,256,640]{2,1,0:T(8,128)(2,1)} %bitcast.27, bf16[1,256,640]{2,1,0:T(8,128)(2,1)S(1)} %bitcast.22), kind=kLoop, calls=%fused_computation.1 | loop fusion | flops 1966080 | bytes 2621440 | tf_op jit(solution)/shard_map/stack | solution.py:213
  87.3 29.3 %collective-permute-done.4.refs_0_ = bf16[80,2048]{1,0:T(8,128)(2,1)S(1)} collective-permute-done((bf16[80,2048]{1,0:T(8,128)(2,1)S(1)}, bf16[80,2048]{1,0:T(8,128)(2,1)S(1)}, u32[]{:S(2)}, u32[]{:S(2)}) %collective-permute-start.4) | collective-permute-done | bytes 327712 | tf_op jit(solution)/shard_map/ppermute | solution.py:233
  117.5 3.4 %shard_map.50 = (bf16[80,2048]{1,0:T(8,128)(2,1)}, bf16[80,2048]{1,0:T(8,128)(2,1)}, bf16[80,2048]{1,0:T(8,128)(2,1)}, bf16[80,2048]{1,0:T(8,128)(2,1)}) custom-call(bf16[80,2048]{1,0:T(8,128)(2,1)} %copy-done.9, bf16[80,2048]{1,0:T(8,128)(2,1)} %copy-done.10, bf16[80,2048]{1,0:T(8,128)(2,1)} %copy-done.11, bf16[4,80,2048]{2,1,0:T(8,128)(2,1)} %bitcast.18), custom_call_target="tpu_custom_call" | custom-call | tf_op jit(solution)/shard_map/pallas_call | solution.py:157
  120.8 3.4 %collective-permute-start.7 = (bf16[80,2048]{1,0:T(8,128)(2,1)}, bf16[80,2048]{1,0:T(8,128)(2,1)S(1)}, u32[]{:S(2)}, u32[]{:S(2)}) collective-permute-start(bf16[80,2048]{1,0:T(8,128)(2,1)} %get-tuple-element.18), channel_id=1, source_target_pairs={{0,32},{32,64},{64,96},{96,0},{1,33},{33,65},{65,97},{97,1},{2,34}... | collective-permute-start | bytes 983048 | tf_op jit(solution)/shard_map/ppermute | solution.py:249
  124.2 4.6 %collective-permute-start.8 = (bf16[80,2048]{1,0:T(8,128)(2,1)}, bf16[80,2048]{1,0:T(8,128)(2,1)S(1)}, u32[]{:S(2)}, u32[]{:S(2)}) collective-permute-start(bf16[80,2048]{1,0:T(8,128)(2,1)} %get-tuple-element.19), channel_id=1, source_target_pairs={{0,64},{32,96},{64,0},{96,32},{1,65},{33,97},{65,1},{97,33},{2,66}... | collective-permute-start | bytes 983048 | tf_op jit(solution)/shard_map/ppermute | solution.py:249
  128.8 3.4 %collective-permute-start.9 = (bf16[80,2048]{1,0:T(8,128)(2,1)}, bf16[80,2048]{1,0:T(8,128)(2,1)S(1)}, u32[]{:S(2)}, u32[]{:S(2)}) collective-permute-start(bf16[80,2048]{1,0:T(8,128)(2,1)} %get-tuple-element.20), channel_id=1, source_target_pairs={{0,96},{32,0},{64,32},{96,64},{1,97},{33,1},{65,33},{97,65},{2,98}... | collective-permute-start | bytes 983048 | tf_op jit(solution)/shard_map/ppermute | solution.py:249
  133.8 7.9 %collective-permute-done.8.refs_2_ = bf16[80,2048]{1,0:T(8,128)(2,1)S(1)} collective-permute-done((bf16[80,2048]{1,0:T(8,128)(2,1)}, bf16[80,2048]{1,0:T(8,128)(2,1)S(1)}, u32[]{:S(2)}, u32[]{:S(2)}) %collective-permute-start.8) | collective-permute-done | bytes 327712 | tf_op jit(solution)/shard_map/ppermute | solution.py:249
  144.1 4.4 %shard_map.52 = (f32[80,640]{1,0:T(8,128)}, f32[80,640]{1,0:T(8,128)}, f32[80,640]{1,0:T(8,128)}, f32[80,640]{1,0:T(8,128)}) custom-call(bf16[80,2048]{1,0:T(8,128)(2,1)} %get-tuple-element.17.refs_0_, bf16[80,2048]{1,0:T(8,128)(2,1)} %copy-done.12, bf16[80,2048]{1,0:T(8,128)(2,1)} %copy-done.13, bf16[80,2048]{1,0:T(8,128)(2,1)} %copy-done.14, ...), custom_call_target="tpu_custom_call" | custom-call | tf_op jit(solution)/shard_map/pallas_call | solution.py:169
  148.5 4.5 %collective-permute-start.14 = (f32[80,640]{1,0:T(8,128)}, f32[80,640]{1,0:T(8,128)S(1)}, u32[]{:S(2)}, u32[]{:S(2)}) collective-permute-start(f32[80,640]{1,0:T(8,128)} %get-tuple-element.22), channel_id=1, source_target_pairs={{0,96},{32,0},{64,32},{96,64},{1,97},{33,1},{65,33},{97,65},{2,98}... | collective-permute-start | bytes 614408 | tf_op jit(solution)/shard_map/ppermute | solution.py:252
  153.0 3.7 %collective-permute-start.15 = (f32[80,640]{1,0:T(8,128)}, f32[80,640]{1,0:T(8,128)S(1)}, u32[]{:S(2)}, u32[]{:S(2)}) collective-permute-start(f32[80,640]{1,0:T(8,128)} %get-tuple-element.23), channel_id=1, source_target_pairs={{0,64},{32,96},{64,0},{96,32},{1,65},{33,97},{65,1},{97,33},{2,66}... | collective-permute-start | bytes 614408 | tf_op jit(solution)/shard_map/ppermute | solution.py:251
  159.8 2.5 %shard_map.49.gram_ref = f32[4,80,640]{2,1,0:T(8,128)} custom-call(bf16[4,4,80,640]{3,2,1,0:T(8,128)(2,1)} %bitcast.15), custom_call_target="tpu_custom_call" | custom-call | tf_op jit(solution)/shard_map/pallas_call | solution.py:189
  164.6 3.2 %collective-permute-done.16.refs_3_ = f32[80,640]{1,0:T(8,128)S(1)} collective-permute-done((f32[80,640]{1,0:T(8,128)}, f32[80,640]{1,0:T(8,128)S(1)}, u32[]{:S(2)}, u32[]{:S(2)}) %collective-permute-start.16) | collective-permute-done | bytes 204832 | tf_op jit(solution)/shard_map/ppermute | solution.py:252
  (72 shorter events, 32.2 us)
Async XLA Ops:
  2.2 15.2 %all-to-all-start = ((bf16[8,160,224]{2,1,0:T(8,128)(2,1)}), bf16[8,160,224]{2,1,0:T(8,128)(2,1)S(1)}, u32[]{:S(2)}, u32[]{:S(2)}) async-start(bf16[8,160,224]{2,1,0:T(8,128)(2,1)} %shard_map.46), calls=%async_computation | async-start | bytes 1310720 | tf_op jit(solution)/shard_map/all_to_all | solution.py:237
  17.4 7.1 %copy-start.4 = (bf16[8,160,224]{2,1,0:T(8,128)(2,1)}, bf16[8,160,224]{2,1,0:T(8,128)(2,1)S(1)}, u32[]{:S(2)}) copy-start(bf16[8,160,224]{2,1,0:T(8,128)(2,1)S(1)} %all-to-all-done) | copy-start | bytes 1720324
  17.4 17.1 %all-to-all-start.3 = ((bf16[16,16,640]{2,1,0:T(8,128)(2,1)}), bf16[16,16,640]{2,1,0:T(8,128)(2,1)S(1)}, u32[]{:S(2)}, u32[]{:S(2)}) async-start(bf16[16,16,640]{2,1,0:T(8,128)(2,1)} %shard_map.51), calls=%async_computation.3 | async-start | bytes 655360 | tf_op jit(solution)/shard_map/all_to_all | solution.py:228
  34.5 45.3 %copy-start.3 = (bf16[16,16,640]{2,1,0:T(8,128)(2,1)}, bf16[16,16,640]{2,1,0:T(8,128)(2,1)S(1)}, u32[]{:S(2)}) copy-start(bf16[16,16,640]{2,1,0:T(8,128)(2,1)S(1)} %all-to-all-done.3) | copy-start | bytes 983044
  34.5 32.8 %all-to-all-start.1 = ((bf16[8,320,224]{2,1,0:T(8,128)(2,1)}), bf16[8,320,224]{2,1,0:T(8,128)(2,1)S(1)}, u32[]{:S(2)}, u32[]{:S(2)}) async-start(bf16[8,320,224]{2,1,0:T(8,128)(2,1)} %get-tuple-element.15), calls=%async_computation.1 | async-start | bytes 2621440 | tf_op jit(solution)/shard_map/all_to_all | solution.py:244
  38.2 8.8 %collective-permute-start = (bf16[224,640]{1,0:T(8,128)(2,1)S(1)}, bf16[224,640]{1,0:T(8,128)(2,1)S(1)}, u32[]{:S(2)}, u32[]{:S(2)}) collective-permute-start(bf16[224,640]{1,0:T(8,128)(2,1)S(1)} %copy-done.16), channel_id=1, source_target_pairs={{408,24},{409,25},{410,26},{411,27},{412,28},{413,29},{414,30},{41... | collective-permute-start | bytes 860168 | tf_op jit(solution)/shard_map/ppermute | solution.py:240
  38.9 11.2 %collective-permute-start.1 = (bf16[224,640]{1,0:T(8,128)(2,1)S(1)}, bf16[224,640]{1,0:T(8,128)(2,1)S(1)}, u32[]{:S(2)}, u32[]{:S(2)}) collective-permute-start(bf16[224,640]{1,0:T(8,128)(2,1)S(1)} %copy-done.16), channel_id=1, source_target_pairs={{272,16},{408,152},{273,17},{409,153},{274,18},{410,154},{275,19},... | collective-permute-start | bytes 860168 | tf_op jit(solution)/shard_map/ppermute | solution.py:240
  39.6 23.1 %collective-permute-start.2 = (bf16[224,640]{1,0:T(8,128)(2,1)S(1)}, bf16[224,640]{1,0:T(8,128)(2,1)}, u32[]{:S(2)}, u32[]{:S(2)}) collective-permute-start(bf16[224,640]{1,0:T(8,128)(2,1)S(1)} %copy-done.16), channel_id=1, source_target_pairs={{136,8},{272,144},{408,280},{137,9},{273,145},{409,281},{138,10},{... | collective-permute-start | bytes 860168 | tf_op jit(solution)/shard_map/ppermute | solution.py:240
  40.9 37.9 %collective-permute-start.11 = (bf16[256,640]{1,0:T(8,128)(2,1)S(1)}, bf16[256,640]{1,0:T(8,128)(2,1)S(1)}, u32[]{:S(2)}, u32[]{:S(2)}) collective-permute-start(bf16[256,640]{1,0:T(8,128)(2,1)S(1)} %bitcast.19), channel_id=1, source_target_pairs={{0,4},{2,6},{4,0},{6,2},{1,5},{3,7},{5,1},{7,3},{8,12},{10,14},{12... | collective-permute-start | bytes 983048 | tf_op jit(solution)/shard_map/ppermute | solution.py:211
  44.3 34.5 %collective-permute-start.12 = (bf16[256,640]{1,0:T(8,128)(2,1)S(1)}, bf16[256,640]{1,0:T(8,128)(2,1)S(1)}, u32[]{:S(2)}, u32[]{:S(2)}) collective-permute-start(bf16[256,640]{1,0:T(8,128)(2,1)S(1)} %bitcast.20), channel_id=1, source_target_pairs={{0,6},{2,0},{4,2},{6,4},{1,7},{3,1},{5,3},{7,5},{8,14},{10,8},{12,... | collective-permute-start | bytes 983048 | tf_op jit(solution)/shard_map/ppermute | solution.py:211
  47.0 31.9 %collective-permute-start.10 = (bf16[256,640]{1,0:T(8,128)(2,1)S(1)}, bf16[256,640]{1,0:T(8,128)(2,1)S(1)}, u32[]{:S(2)}, u32[]{:S(2)}) collective-permute-start(bf16[256,640]{1,0:T(8,128)(2,1)S(1)} %bitcast.21), channel_id=1, source_target_pairs={{0,2},{2,4},{4,6},{6,0},{1,3},{3,5},{5,7},{7,1},{8,10},{10,12},{12... | collective-permute-start | bytes 983048 | tf_op jit(solution)/shard_map/ppermute | solution.py:211
  63.9 3.5 %collective-permute-start.3 = (bf16[224,640]{1,0:T(8,128)(2,1)S(1)}, bf16[224,640]{1,0:T(8,128)(2,1)S(1)}, u32[]{:S(2)}, u32[]{:S(2)}) collective-permute-start(bf16[224,640]{1,0:T(8,128)(2,1)S(1)} %add_select_fusion.own_ref), channel_id=1, source_target_pairs={{0,1},{1,0},{2,3},{3,2},{4,5},{5,4},{6,7},{7,6},{8,9},{9,8},{10,11... | collective-permute-start | bytes 860168 | tf_op jit(solution)/shard_map/ppermute | solution.py:242
  72.3 86.3 %all-to-all-start.2 = ((bf16[16,80,640]{2,1,0:T(8,128)(2,1)}), bf16[16,80,640]{2,1,0:T(8,128)(2,1)S(1)}, u32[]{:S(2)}, u32[]{:S(2)}) async-start(bf16[16,80,640]{2,1,0:T(8,128)(2,1)} %bitcast.16), calls=%async_computation.2 | async-start | bytes 3276800 | tf_op jit(solution)/shard_map/all_to_all | solution.py:246
  82.3 61.1 %collective-permute-start.13 = (bf16[4,256,640]{2,1,0:T(8,128)(2,1)}, bf16[4,256,640]{2,1,0:T(8,128)(2,1)}, u32[]{:S(2)}, u32[]{:S(2)}) collective-permute-start(bf16[4,256,640]{2,1,0:T(8,128)(2,1)} %pad_maximum_fusion), channel_id=1, source_target_pairs={{0,1},{1,0},{2,3},{3,2},{4,5},{5,4},{6,7},{7,6},{8,9},{9,8},{10,11... | collective-permute-start | bytes 3932168 | tf_op jit(solution)/shard_map/ppermute | solution.py:213
  84.6 31.9 %collective-permute-start.4 = (bf16[80,2048]{1,0:T(8,128)(2,1)S(1)}, bf16[80,2048]{1,0:T(8,128)(2,1)S(1)}, u32[]{:S(2)}, u32[]{:S(2)}) collective-permute-start(bf16[80,2048]{1,0:T(8,128)(2,1)S(1)} %multiply_reduce_fusion), channel_id=1, source_target_pairs={{0,8},{8,16},{16,24},{136,144},{144,152},{272,280},{1,9},{9,17},{1... | collective-permute-start | bytes 983048 | tf_op jit(solution)/shard_map/ppermute | solution.py:233
  85.9 30.6 %collective-permute-start.5 = (bf16[80,2048]{1,0:T(8,128)(2,1)S(1)}, bf16[80,2048]{1,0:T(8,128)(2,1)S(1)}, u32[]{:S(2)}, u32[]{:S(2)}) collective-permute-start(bf16[80,2048]{1,0:T(8,128)(2,1)S(1)} %multiply_reduce_fusion), channel_id=1, source_target_pairs={{0,16},{8,24},{136,152},{1,17},{9,25},{137,153},{2,18},{10,26},{13... | collective-permute-start | bytes 983048 | tf_op jit(solution)/shard_map/ppermute | solution.py:234
  86.6 30.0 %collective-permute-start.6 = (bf16[80,2048]{1,0:T(8,128)(2,1)S(1)}, bf16[80,2048]{1,0:T(8,128)(2,1)S(1)}, u32[]{:S(2)}, u32[]{:S(2)}) collective-permute-start(bf16[80,2048]{1,0:T(8,128)(2,1)S(1)} %multiply_reduce_fusion), channel_id=1, source_target_pairs={{0,24},{1,25},{2,26},{3,27},{4,28},{5,29},{6,30},{7,31},{32,56},{3... | collective-permute-start | bytes 983048 | tf_op jit(solution)/shard_map/ppermute | solution.py:234
  120.8 13.0 %collective-permute-start.7 = (bf16[80,2048]{1,0:T(8,128)(2,1)}, bf16[80,2048]{1,0:T(8,128)(2,1)S(1)}, u32[]{:S(2)}, u32[]{:S(2)}) collective-permute-start(bf16[80,2048]{1,0:T(8,128)(2,1)} %get-tuple-element.18), channel_id=1, source_target_pairs={{0,32},{32,64},{64,96},{96,0},{1,33},{33,65},{65,97},{97,1},{2,34}... | collective-permute-start | bytes 983048 | tf_op jit(solution)/shard_map/ppermute | solution.py:249
  124.2 17.5 %collective-permute-start.8 = (bf16[80,2048]{1,0:T(8,128)(2,1)}, bf16[80,2048]{1,0:T(8,128)(2,1)S(1)}, u32[]{:S(2)}, u32[]{:S(2)}) collective-permute-start(bf16[80,2048]{1,0:T(8,128)(2,1)} %get-tuple-element.19), channel_id=1, source_target_pairs={{0,64},{32,96},{64,0},{96,32},{1,65},{33,97},{65,1},{97,33},{2,66}... | collective-permute-start | bytes 983048 | tf_op jit(solution)/shard_map/ppermute | solution.py:249
  128.8 14.6 %collective-permute-start.9 = (bf16[80,2048]{1,0:T(8,128)(2,1)}, bf16[80,2048]{1,0:T(8,128)(2,1)S(1)}, u32[]{:S(2)}, u32[]{:S(2)}) collective-permute-start(bf16[80,2048]{1,0:T(8,128)(2,1)} %get-tuple-element.20), channel_id=1, source_target_pairs={{0,96},{32,0},{64,32},{96,64},{1,97},{33,1},{65,33},{97,65},{2,98}... | collective-permute-start | bytes 983048 | tf_op jit(solution)/shard_map/ppermute | solution.py:249
  133.8 9.6 %copy-start.12 = (bf16[80,2048]{1,0:T(8,128)(2,1)}, bf16[80,2048]{1,0:T(8,128)(2,1)S(1)}, u32[]{:S(2)}) copy-start(bf16[80,2048]{1,0:T(8,128)(2,1)S(1)} %collective-permute-done.7.refs_1_) | copy-start | bytes 983044
  148.5 13.9 %collective-permute-start.14 = (f32[80,640]{1,0:T(8,128)}, f32[80,640]{1,0:T(8,128)S(1)}, u32[]{:S(2)}, u32[]{:S(2)}) collective-permute-start(f32[80,640]{1,0:T(8,128)} %get-tuple-element.22), channel_id=1, source_target_pairs={{0,96},{32,0},{64,32},{96,64},{1,97},{33,1},{65,33},{97,65},{2,98}... | collective-permute-start | bytes 614408 | tf_op jit(solution)/shard_map/ppermute | solution.py:252
  153.0 11.6 %collective-permute-start.15 = (f32[80,640]{1,0:T(8,128)}, f32[80,640]{1,0:T(8,128)S(1)}, u32[]{:S(2)}, u32[]{:S(2)}) collective-permute-start(f32[80,640]{1,0:T(8,128)} %get-tuple-element.23), channel_id=1, source_target_pairs={{0,64},{32,96},{64,0},{96,32},{1,65},{33,97},{65,1},{97,33},{2,66}... | collective-permute-start | bytes 614408 | tf_op jit(solution)/shard_map/ppermute | solution.py:251
  156.7 11.0 %collective-permute-start.16 = (f32[80,640]{1,0:T(8,128)}, f32[80,640]{1,0:T(8,128)S(1)}, u32[]{:S(2)}, u32[]{:S(2)}) collective-permute-start(f32[80,640]{1,0:T(8,128)} %get-tuple-element.24), channel_id=1, source_target_pairs={{0,32},{32,64},{64,96},{96,0},{1,33},{33,65},{65,97},{97,1},{2,34}... | collective-permute-start | bytes 614408 | tf_op jit(solution)/shard_map/ppermute | solution.py:252
  (18 other events, 32.0 us)
